TPU v7x, 128 devices: a whole 4x4x4 slice. The times are simulated.
128 devices in a mesh: slab: 8 (over x_lo, z), piece: 16 (over y, x_hi, core).
Axes of the slice: x: 4 (x_hi: 2, x_lo: 2; x = x_hi * 2 + x_lo), y: 4, z: 4, core: 2. Of those that a mesh axis runs over, the one named last changes fastest.
Arguments:
- fine_tiles: bfloat16 [1024, 64, 512], P(('slab', 'piece')), may hold values from -0.25 to 0.25
- fine_cols: int32 [1024, 8], P(('slab', 'piece')), may hold values from 0 to 23
- bond_mask: int32 [1024, 8], P(('slab', 'piece')), may hold values 0 or 1
- diag_inv: bfloat16 [1024, 64, 64], P(('slab', 'piece')), may hold values from -0.75 to 0.75
- tentative: bfloat16 [1024, 64, 64], P(('slab', 'piece')), may hold values from -0.75 to 0.75
- aggregate: int32 [1024], P(('slab', 'piece')), may hold values from 0 to 7
- tentative_two: bfloat16 [1024, 64, 64], P(('slab', 'piece')), may hold values from -0.75 to 0.75
- aggregate_two: int32 [1024], P(('slab', 'piece')), may hold values from 0 to 15
Outputs:
- coarse_one: float32 [1024, 64, 3584], P(('slab', 'piece'))
- coarse_two: float32 [128, 64, 7168], P(('slab', 'piece'))
All inputs are finite; a program needn't handle non-finite values. No bound on the sum of `bond_mask` on one device may be relied on, other than what follows from the above.
Results may differ from a plain program's by a relative error of at most 0.008.
Values may be sent and summed in bfloat16 or wider, within the bound.
No kernel may reach another device: no remote copies, remote signals or barrier semaphores. Data moves between devices by JAX's collectives and lax.ppermute only.
A program may use at most 128 MiB of HBM per device.

v0:
```python
import jax
import jax.numpy as jnp
from jax import lax
from jax.sharding import PartitionSpec as P

DAMPING = 2.0 / 3.0
EXACT_MODE = lax.Precision.HIGHEST


def passed_along(block, axis, distance):
    devices = range(lax.axis_size(axis))
    route = [(i - distance, i) for i in devices if i - distance in devices]
    return lax.ppermute(block, axis, route)


def padded(cells, sides, width):
    for axis, dim in sides:
        count = lax.axis_size(axis)
        ends = count - 1
        head = lax.slice_in_dim(cells, 0, width, axis=dim)
        tail = lax.slice_in_dim(cells, cells.shape[dim] - width, cells.shape[dim], axis=dim)
        cells = jnp.concatenate(
            [
                lax.ppermute(tail, axis, [(i, (i + 1) % count) for i in range(ends)]),
                cells,
                lax.ppermute(head, axis, [((i + 1) % count, i) for i in range(ends)]),
            ],
            axis=dim,
        )
    return cells


def slot_tiles(tiles, agg_ids, count):
    onehot = (agg_ids[:, None] == jnp.arange(count, dtype=jnp.int32)[None, :]).astype(jnp.float32)
    placed = tiles.astype(jnp.float32)[:, :, None, :] * onehot[:, None, :, None]
    return placed.astype(jnp.bfloat16).reshape(
        tiles.shape[0], tiles.shape[1], count * tiles.shape[2]
    )


def prolong_rows(quad, fine_cols, bond_mask, diag_inv, own_slot, basis_rim):
    blocks, tile_size = (diag_inv.shape[0], diag_inv.shape[1])
    slot_count = fine_cols.shape[1]
    agg_width = own_slot.shape[2]
    smooth = jnp.einsum("irs,iskt->ikrt", diag_inv, quad, preferred_element_type=jnp.float32)
    smooth = (DAMPING * bond_mask.astype(jnp.float32)[:, :, None, None] * smooth).astype(
        jnp.bfloat16
    )
    summed = jnp.zeros((blocks, tile_size, 3, agg_width), jnp.float32)
    for k in range(slot_count):
        column = fine_cols[:, k]
        rows_in = jnp.take(basis_rim, column, axis=0)
        product = jnp.einsum(
            "irs,isq->irq", smooth[:, k], rows_in, preferred_element_type=jnp.float32
        )
        side_mask = (column[:, None] // blocks == jnp.arange(3, dtype=jnp.int32)[None, :]).astype(
            jnp.float32
        )
        summed = summed - product[:, :, None, :] * side_mask[:, None, :, None]
    summed = summed.at[:, :, 1, :].add(own_slot.astype(jnp.float32))
    return summed.reshape(blocks, tile_size, 3 * agg_width).astype(jnp.bfloat16)


def apply_rows(quad, fine_cols, bond_mask, prolong_rim, agg_width):
    blocks, tile_size = (quad.shape[0], quad.shape[1])
    slot_count = fine_cols.shape[1]
    masked = quad * bond_mask.astype(jnp.bfloat16)[:, None, :, None]
    sides = jnp.zeros((blocks, tile_size, 3, 3 * agg_width), jnp.float32)
    for k in range(slot_count):
        column = fine_cols[:, k]
        rows_in = jnp.take(prolong_rim, column, axis=0)
        product = jnp.einsum(
            "irs,isq->irq", masked[:, :, k, :], rows_in, preferred_element_type=jnp.float32
        )
        side_mask = (column[:, None] // blocks == jnp.arange(3, dtype=jnp.int32)[None, :]).astype(
            jnp.float32
        )
        sides = sides + product[:, :, None, :] * side_mask[:, None, :, None]
    summed = jnp.pad(sides[:, :, 0], ((0, 0), (0, 0), (0, 2 * agg_width)))
    summed = summed + jnp.pad(sides[:, :, 1], ((0, 0), (0, 0), (agg_width, agg_width)))
    summed = summed + jnp.pad(sides[:, :, 2], ((0, 0), (0, 0), (2 * agg_width, 0)))
    return summed.astype(jnp.bfloat16)


def level_partial(coarse_rows, two_tiles, two_ids, basis, groups):
    agg_count, tile_size = (two_tiles.shape[0], two_tiles.shape[1])
    left = jnp.einsum(
        "ars,arc->asc", two_tiles.astype(jnp.float32), coarse_rows, precision=EXACT_MODE
    )
    left = left.reshape(agg_count, tile_size, 7, agg_count, tile_size)
    right = basis.astype(jnp.float32).reshape(7, agg_count, tile_size, groups * tile_size)
    both = jnp.einsum("asobt,obtq->asoq", left, right, precision=EXACT_MODE)
    onehot = (two_ids[:, None] == jnp.arange(groups, dtype=jnp.int32)[None, :]).astype(jnp.float32)
    placed = jnp.einsum("ag,asoq->gsoq", onehot, both, precision=EXACT_MODE)
    return placed.reshape(groups, tile_size, 7 * groups * tile_size)


def neighbour_basis(q2slot, offset):
    return passed_along(q2slot, "slab", -offset)


def per_device(
    fine_tiles, fine_cols, bond_mask, diag_inv, tentative, aggregate, tentative_two, aggregate_two
):
    blocks, tile_size = (diag_inv.shape[0], diag_inv.shape[1])
    slot_count = fine_cols.shape[1]
    agg_count = tentative_two.shape[0]
    groups = lax.axis_size("piece")
    agg_width = agg_count * tile_size
    quad = fine_tiles.reshape(blocks, tile_size, slot_count, tile_size)
    qslot = slot_tiles(tentative, aggregate, agg_count)
    basis_rim = padded(qslot, (("slab", 0),), blocks)
    prolong = prolong_rows(quad, fine_cols, bond_mask, diag_inv, qslot, basis_rim)
    prolong_rim = padded(prolong, (("slab", 0),), blocks)
    applied = apply_rows(quad, fine_cols, bond_mask, prolong_rim, agg_width)
    product = lax.dot_general(
        prolong.reshape(blocks * tile_size, 3 * agg_width),
        applied.reshape(blocks * tile_size, 5 * agg_width),
        (((0,), (0,)), ((), ())),
        preferred_element_type=jnp.float32,
    )
    row_parts = product.reshape(3, agg_count, tile_size, 5 * agg_width)
    from_next = passed_along(row_parts[0].astype(jnp.bfloat16), "slab", -1).astype(jnp.float32)
    from_prev = passed_along(row_parts[2].astype(jnp.bfloat16), "slab", 1).astype(jnp.float32)
    coarse = jnp.pad(row_parts[1], ((0, 0), (0, 0), (agg_width, agg_width)))
    coarse = coarse + jnp.pad(from_next, ((0, 0), (0, 0), (2 * agg_width, 0)))
    coarse = coarse + jnp.pad(from_prev, ((0, 0), (0, 0), (0, 2 * agg_width)))
    q2slot = slot_tiles(tentative_two, aggregate_two, groups)
    layers = []
    for offset in range(-3, 4):
        if offset == 0:
            layers.append(q2slot)
        else:
            layers.append(neighbour_basis(q2slot, offset))
    basis = jnp.concatenate(layers, 0)
    partial_value = level_partial(coarse, tentative_two, aggregate_two, basis, groups)
    summed = lax.psum(partial_value.astype(jnp.bfloat16), "piece").astype(jnp.float32)
    level_two = lax.dynamic_slice_in_dim(summed, lax.axis_index("piece"), 1, 0)
    return (coarse, level_two)


def solution(mesh):
    placed = (
        P(("slab", "piece"), None, None),
        P(("slab", "piece"), None),
        P(("slab", "piece"), None),
        P(("slab", "piece"), None, None),
        P(("slab", "piece"), None, None),
        P(("slab", "piece")),
        P(("slab", "piece"), None, None),
        P(("slab", "piece")),
    )
    return jax.shard_map(
        per_device,
        mesh=mesh,
        in_specs=placed,
        out_specs=(P(("slab", "piece"), None, None), P(("slab", "piece"), None, None)),
        check_vma=False,
    )
```

profile of v0, /device:TPU:2, one launch (start us, length us, event | category | flops | bytes accessed | tf_op | source)
XLA Modules:
  0.0 831.9 jit_solution(17065797882051411604)
XLA Ops:
  23.4 4.7 collective-permute-done
  46.8 5.0 multiply_subtract_fusion
  55.5 21.0 %scatter-add.4 = f32[8,64,3,512]{3,2,1,0:T(4,128)} dynamic-update-slice(f32[8,64,3,512]{3,2,1,0:T(4,128)} %copy-done.3, f32[8,64,1,512]{3,2,1,0:T(1,128)S(1)} %slice_add_fusion, s32[]{:T(128)} %constant.135.clone.1, s32[]{:T(128)} %constant.135.clone.1, s32[]{:T(128)} %constant.134.clone.1, s32[]{:T(128)} %constant.135.clone.1) | dynamic-update-slice | bytes 2097156 | tf_op jit(solution)/shard_map/scatter-add | solution.py:60
  86.2 15.2 %collective-permute-start.3 = (bf16[8,64,1536]{2,1,0:T(8,128)(2,1)}, bf16[8,64,1536]{2,1,0:T(8,128)(2,1)}, u32[]{:S(2)}, u32[]{:S(2)}) collective-permute-start(bf16[8,64,1536]{2,1,0:T(8,128)(2,1)} %convert_element_type.179), channel_id=1, source_target_pairs={{16,0},{32,16},{48,32},{64,48},{80,64},{96,80},{112,96},{17,1},{33... | collective-permute-start | bytes 4718600 | tf_op jit(solution)/shard_map/ppermute | solution.py:26
  109.7 12.8 %collective-permute-done.2 = bf16[8,64,1536]{2,1,0:T(8,128)(2,1)} collective-permute-done((bf16[8,64,1536]{2,1,0:T(8,128)(2,1)}, bf16[8,64,1536]{2,1,0:T(8,128)(2,1)}, u32[]{:S(2)}, u32[]{:S(2)}) %collective-permute-start.2) | collective-permute-done | bytes 1572896 | tf_op jit(solution)/shard_map/ppermute | solution.py:24
  129.0 4.1 gather_fusion.13
  133.2 4.2 gather_fusion.12
  141.5 4.2 gather_fusion.10
  145.7 4.1 gather_fusion.9
  149.8 4.1 gather_fusion.8
  176.0 6.6 multiply_add_fusion
  186.2 13.0 %fusion.129 = (bf16[1536,2560]{1,0:T(8,128)(2,1)}, f32[1536,2560]{1,0:T(8,128)}) fusion(bf16[8,64,1536]{2,1,0:T(8,128)(2,1)S(1)} %copy-done.5, f32[8,64,1536]{2,1,0:T(8,128)} %get-tuple-element.33, f32[8,64,1536]{2,1,0:T(8,128)} %get-tuple-element.34, f32[8,64,1536]{2,1,0:T(8,128)S(1)} %get-tuple-element.32), kind=kOutput, calls=%fused_computation.267 | convolution fusion | flops 4034396160 | bytes 34603008 | tf_op jit(solution)/shard_map/dot_general | solution.py:116
  214.1 19.7 %collective-permute-done.6 = bf16[8,64,1024]{2,1,0:T(8,128)(2,1)S(1)} collective-permute-done((bf16[8,64,1024]{2,1,0:T(8,128)(2,1)S(1)}, bf16[8,64,1024]{2,1,0:T(8,128)(2,1)S(1)}, u32[]{:S(2)}, u32[]{:S(2)}) %collective-permute-start.6) | collective-permute-done | bytes 1048608 | tf_op jit(solution)/shard_map/ppermute | solution.py:13
  233.9 82.1 %collective-permute-start.9 = (bf16[8,64,1024]{2,1,0:T(8,128)(2,1)S(1)}, bf16[8,64,1024]{2,1,0:T(8,128)(2,1)S(1)}, u32[]{:S(2)}, u32[]{:S(2)}) collective-permute-start(bf16[8,64,1024]{2,1,0:T(8,128)(2,1)S(1)} %multiply_convert_fusion), channel_id=1, source_target_pairs={{16,0},{32,16},{48,32},{64,48},{80,64},{96,80},{112,96},{17,1},{33... | collective-permute-start | bytes 3145736 | tf_op jit(solution)/shard_map/ppermute | solution.py:13
  317.9 44.3 %collective-permute-done.8 = bf16[8,64,1024]{2,1,0:T(8,128)(2,1)S(1)} collective-permute-done((bf16[8,64,1024]{2,1,0:T(8,128)(2,1)S(1)}, bf16[8,64,1024]{2,1,0:T(8,128)(2,1)S(1)}, u32[]{:S(2)}, u32[]{:S(2)}) %collective-permute-start.8) | collective-permute-done | bytes 1048608 | tf_op jit(solution)/shard_map/ppermute | solution.py:13
  364.8 22.4 %collective-permute-done.11 = bf16[8,64,1024]{2,1,0:T(8,128)(2,1)S(1)} collective-permute-done((bf16[8,64,1024]{2,1,0:T(8,128)(2,1)S(1)}, bf16[8,64,1024]{2,1,0:T(8,128)(2,1)S(1)}, u32[]{:S(2)}, u32[]{:S(2)}) %collective-permute-start.11) | collective-permute-done | bytes 1048608 | tf_op jit(solution)/shard_map/ppermute | solution.py:13
  387.3 5.5 slice.213
  397.2 5.9 convolution_bitcast_fusion.1
  403.1 11.3 %reshape.330 = f32[8,64,7,8,64]{4,3,2,1,0:T(8,128)} reshape(f32[8,64,3584]{2,1,0:T(8,128)} %convolution_bitcast_fusion.1) | data formatting | bytes 14680064 | tf_op jit(solution)/shard_map/reshape | solution.py:90
  414.4 24.0 %fusion.2 = f32[7,1024,8,64,1]{1,2,4,0,3:T(8,128)S(1)} fusion(bf16[7,8,64,1024,1]{3,2,1,0,4:T(8,128)(2,1)} %bitcast.100, f32[8,64,7,8,64]{4,3,2,1,0:T(8,128)} %reshape.330), kind=kOutput, calls=%fused_computation.18 | convolution fusion | flops 22548578304 | bytes 29360128 | tf_op jit(solution)/shard_map/asobt,obtq->asoq/dot_general | solution.py:92
  438.4 12.6 %fusion.4 = bf16[16,64,7,1024]{3,0,2,1:T(8,128)(2,1)S(1)} fusion(f32[7,1024,8,64,1]{1,2,4,0,3:T(8,128)S(1)} %fusion.2, s32[8]{0:T(128)S(1)} %copy-done.25), kind=kOutput, calls=%fused_computation.21 | convolution fusion | flops 711983232 | bytes 29360160 | tf_op jit(solution)/shard_map/ag,asoq->gsoq/dot_general | solution.py:94
  451.0 20.6 %copy.49 = bf16[16,64,7,1024]{3,2,1,0:T(8,128)(2,1)} copy(bf16[16,64,7,1024]{3,0,2,1:T(8,128)(2,1)S(1)} %fusion.4) | data formatting | bytes 29360128 | tf_op jit(solution)/shard_map/convert_element_type | solution.py:137
  471.7 29.0 %convert_element_type.188 = bf16[16,64,7168]{2,1,0:T(8,128)(2,1)} reshape(bf16[16,64,7,1024]{3,2,1,0:T(8,128)(2,1)} %copy.49) | data formatting | bytes 29360128 | tf_op jit(solution)/shard_map/convert_element_type | solution.py:137
  500.7 321.5 %all-reduce.8.cloned.1.call-done = bf16[16,64,7168]{2,1,0:T(8,128)(2,1)} async-done(((bf16[16,64,7168]{2,1,0:T(8,128)(2,1)}), bf16[16,64,7168]{2,1,0:T(8,128)(2,1)}) %all-reduce.8.cloned.1.call-update) | async-done | bytes 14680080 | tf_op jit(solution)/shard_map/psum | solution.py:137
  (166 shorter events, 118.8 us)
Async XLA Ops:
  7.2 14.7 %copy-start = (bf16[8,64,64]{2,1,0:T(8,128)(2,1)S(1)}, bf16[8,64,64]{2,1,0:T(8,128)(2,1)}, u32[]{:S(2)}) copy-start(bf16[8,64,64]{2,1,0:T(8,128)(2,1)} %param.17) | copy-start | bytes 196612
  7.2 10.8 %copy-start.21 = (s32[8,8]{1,0:T(8,128)S(1)}, s32[8,8]{1,0:T(8,128)}, u32[]{:S(2)}) copy-start(s32[8,8]{1,0:T(8,128)} %param.15) | copy-start | bytes 772
  7.2 11.3 %copy-start.23 = (s32[8,8]{1,0:T(8,128)S(1)}, s32[8,8]{1,0:T(8,128)}, u32[]{:S(2)}) copy-start(s32[8,8]{1,0:T(8,128)} %param.16) | copy-start | bytes 772
  7.2 815.0 %all-reduce.8.cloned.1.call-start = ((), (), s32[]{:S(2)}) async-start(), calls=%async_computation | async-start | bytes 29360128 | tf_op jit(solution)/shard_map/psum | solution.py:137
  10.0 18.1 %collective-permute-start = (bf16[8,64,512]{2,1,0:T(8,128)(2,1)}, bf16[8,64,512]{2,1,0:T(8,128)(2,1)}, u32[]{:S(2)}, u32[]{:S(2)}) collective-permute-start(bf16[8,64,512]{2,1,0:T(8,128)(2,1)} %multiply_convert_fusion.2), channel_id=1, source_target_pairs={{0,16},{16,32},{32,48},{48,64},{64,80},{80,96},{96,112},{1,17},{17... | collective-permute-start | bytes 1572872 | tf_op jit(solution)/shard_map/ppermute | solution.py:24
  13.8 15.8 %collective-permute-start.1 = (bf16[8,64,512]{2,1,0:T(8,128)(2,1)}, bf16[8,64,512]{2,1,0:T(8,128)(2,1)}, u32[]{:S(2)}, u32[]{:S(2)}) collective-permute-start(bf16[8,64,512]{2,1,0:T(8,128)(2,1)} %multiply_convert_fusion.2), channel_id=1, source_target_pairs={{16,0},{32,16},{48,32},{64,48},{80,64},{96,80},{112,96},{17,1},{33... | collective-permute-start | bytes 1572872 | tf_op jit(solution)/shard_map/ppermute | solution.py:26
  21.8 6.3 copy-start.13
  41.4 3.9 copy-start.16
  79.4 22.7 %copy-start.20 = (bf16[8,64,64]{2,1,0:T(8,128)(2,1)S(1)}, bf16[8,64,64]{2,1,0:T(8,128)(2,1)}, u32[]{:S(2)}) copy-start(bf16[8,64,64]{2,1,0:T(8,128)(2,1)} %param.20) | copy-start | bytes 196612
  82.5 39.9 %collective-permute-start.2 = (bf16[8,64,1536]{2,1,0:T(8,128)(2,1)}, bf16[8,64,1536]{2,1,0:T(8,128)(2,1)}, u32[]{:S(2)}, u32[]{:S(2)}) collective-permute-start(bf16[8,64,1536]{2,1,0:T(8,128)(2,1)} %convert_element_type.179), channel_id=1, source_target_pairs={{0,16},{16,32},{32,48},{48,64},{64,80},{80,96},{96,112},{1,17},{17... | collective-permute-start | bytes 4718600 | tf_op jit(solution)/shard_map/ppermute | solution.py:24
  86.2 40.2 %collective-permute-start.3 = (bf16[8,64,1536]{2,1,0:T(8,128)(2,1)}, bf16[8,64,1536]{2,1,0:T(8,128)(2,1)}, u32[]{:S(2)}, u32[]{:S(2)}) collective-permute-start(bf16[8,64,1536]{2,1,0:T(8,128)(2,1)} %convert_element_type.179), channel_id=1, source_target_pairs={{16,0},{32,16},{48,32},{64,48},{80,64},{96,80},{112,96},{17,1},{33... | collective-permute-start | bytes 4718600 | tf_op jit(solution)/shard_map/ppermute | solution.py:26
  108.1 17.0 %copy-start.4 = (bf16[8,64,1536]{2,1,0:T(8,128)(2,1)S(1)}, bf16[8,64,1536]{2,1,0:T(8,128)(2,1)}, u32[]{:S(2)}) copy-start(bf16[8,64,1536]{2,1,0:T(8,128)(2,1)} %convert_element_type.179) | copy-start | bytes 4718596
  182.6 3.6 copy-start.5
  202.0 190.7 %collective-permute-start.4 = (bf16[8,64,2560]{2,1,0:T(8,128)(2,1)S(1)}, bf16[8,64,2560]{2,1,0:T(8,128)(2,1)S(1)}, u32[]{:S(2)}, u32[]{:S(2)}) collective-permute-start(bf16[8,64,2560]{2,1,0:T(8,128)(2,1)S(1)} %bitcast.99), channel_id=1, source_target_pairs={{16,0},{32,16},{48,32},{64,48},{80,64},{96,80},{112,96},{17,1},{33... | collective-permute-start | bytes 7864328 | tf_op jit(solution)/shard_map/ppermute | solution.py:13
  205.8 187.0 %collective-permute-start.5 = (bf16[8,64,2560]{2,1,0:T(8,128)(2,1)S(1)}, bf16[8,64,2560]{2,1,0:T(8,128)(2,1)S(1)}, u32[]{:S(2)}, u32[]{:S(2)}) collective-permute-start(bf16[8,64,2560]{2,1,0:T(8,128)(2,1)S(1)} %bitcast.98), channel_id=1, source_target_pairs={{0,16},{16,32},{32,48},{48,64},{64,80},{80,96},{96,112},{1,17},{17... | collective-permute-start | bytes 7864328 | tf_op jit(solution)/shard_map/ppermute | solution.py:13
  208.2 25.7 %collective-permute-start.6 = (bf16[8,64,1024]{2,1,0:T(8,128)(2,1)S(1)}, bf16[8,64,1024]{2,1,0:T(8,128)(2,1)S(1)}, u32[]{:S(2)}, u32[]{:S(2)}) collective-permute-start(bf16[8,64,1024]{2,1,0:T(8,128)(2,1)S(1)} %multiply_convert_fusion), channel_id=1, source_target_pairs={{0,48},{16,64},{32,80},{48,96},{64,112},{1,49},{17,65},{33,81},{49... | collective-permute-start | bytes 3145736 | tf_op jit(solution)/shard_map/ppermute | solution.py:13
  210.1 105.8 %collective-permute-start.7 = (bf16[8,64,1024]{2,1,0:T(8,128)(2,1)S(1)}, bf16[8,64,1024]{2,1,0:T(8,128)(2,1)S(1)}, u32[]{:S(2)}, u32[]{:S(2)}) collective-permute-start(bf16[8,64,1024]{2,1,0:T(8,128)(2,1)S(1)} %multiply_convert_fusion), channel_id=1, source_target_pairs={{0,32},{16,48},{32,64},{48,80},{64,96},{80,112},{1,33},{17,49},{33... | collective-permute-start | bytes 3145736 | tf_op jit(solution)/shard_map/ppermute | solution.py:13
  212.2 150.0 %collective-permute-start.8 = (bf16[8,64,1024]{2,1,0:T(8,128)(2,1)S(1)}, bf16[8,64,1024]{2,1,0:T(8,128)(2,1)S(1)}, u32[]{:S(2)}, u32[]{:S(2)}) collective-permute-start(bf16[8,64,1024]{2,1,0:T(8,128)(2,1)S(1)} %multiply_convert_fusion), channel_id=1, source_target_pairs={{0,16},{16,32},{32,48},{48,64},{64,80},{80,96},{96,112},{1,17},{17... | collective-permute-start | bytes 3145736 | tf_op jit(solution)/shard_map/ppermute | solution.py:13
  233.9 130.8 %collective-permute-start.9 = (bf16[8,64,1024]{2,1,0:T(8,128)(2,1)S(1)}, bf16[8,64,1024]{2,1,0:T(8,128)(2,1)S(1)}, u32[]{:S(2)}, u32[]{:S(2)}) collective-permute-start(bf16[8,64,1024]{2,1,0:T(8,128)(2,1)S(1)} %multiply_convert_fusion), channel_id=1, source_target_pairs={{16,0},{32,16},{48,32},{64,48},{80,64},{96,80},{112,96},{17,1},{33... | collective-permute-start | bytes 3145736 | tf_op jit(solution)/shard_map/ppermute | solution.py:13
  316.0 48.8 %collective-permute-start.10 = (bf16[8,64,1024]{2,1,0:T(8,128)(2,1)S(1)}, bf16[8,64,1024]{2,1,0:T(8,128)(2,1)S(1)}, u32[]{:S(2)}, u32[]{:S(2)}) collective-permute-start(bf16[8,64,1024]{2,1,0:T(8,128)(2,1)S(1)} %multiply_convert_fusion), channel_id=1, source_target_pairs={{32,0},{48,16},{64,32},{80,48},{96,64},{112,80},{33,1},{49,17},{65... | collective-permute-start | bytes 3145736 | tf_op jit(solution)/shard_map/ppermute | solution.py:13
  362.2 25.0 %collective-permute-start.11 = (bf16[8,64,1024]{2,1,0:T(8,128)(2,1)S(1)}, bf16[8,64,1024]{2,1,0:T(8,128)(2,1)S(1)}, u32[]{:S(2)}, u32[]{:S(2)}) collective-permute-start(bf16[8,64,1024]{2,1,0:T(8,128)(2,1)S(1)} %multiply_convert_fusion), channel_id=1, source_target_pairs={{48,0},{64,16},{80,32},{96,48},{112,64},{49,1},{65,17},{81,33},{97... | collective-permute-start | bytes 3145736 | tf_op jit(solution)/shard_map/ppermute | solution.py:13
  387.3 5.5 copy-start.22
  414.4 24.1 %copy-start.25 = (s32[8]{0:T(128)S(1)}, s32[8]{0:T(128)}, u32[]{:S(2)}) copy-start(s32[8]{0:T(128)} %param.21) | copy-start | bytes 100
  500.6 324.1 %copy-start.1 = (bf16[8,64,64]{2,1,0:T(8,128)(2,1)S(1)}, bf16[8,64,64]{2,1,0:T(8,128)(2,1)}, u32[]{:S(2)}) copy-start(bf16[8,64,64]{2,1,0:T(8,128)(2,1)} %param.17) | copy-start | bytes 196612
  (16 other events, 35.9 us)
Sparse Core Ops, SparseCore 0:
  500.8 321.3 all-reduce.7
where the time goes:
time: 844 us; the launch traced here: 832 us
  waiting for transfers between devices  427 us (51%)
  local copies, waits for them, and re-layouts  168 us (20%)
  starting transfers between devices  124 us (15%)
  matrix products  72 us (9%)
  other arithmetic  25.5 us (3%)
  between operations  15.2 us (2%)
    psum x1, waiting for transfers between devices, per_device(): lax.psum(partial_value.astype(jnp.bfloat16), 'piece').astype(jnp.float32)  322 us
    ppermute x8, starting transfers between devices, passed_along(): return lax.ppermute(block, axis, route)  97.7 us
    ppermute x8, waiting for transfers between devices, passed_along(): return lax.ppermute(block, axis, route)  86.4 us
    convert_element_type x2, local copies, waits for them, and re-layouts, per_device(): partial_value.astype(jnp.bfloat16)  49.6 us
    gather x8, local copies, waits for them, and re-layouts, apply_rows(): rows_in = jnp.take(prolong_rim, column, axis=0)  33.2 us
    dot_general x1, matrix products, level_partial(): both = jnp.einsum('asobt,obtq->asoq', left, right, precision=EXACT_MODE)  24 us
    scatter-add x1, local copies, waits for them, and re-layouts, prolong_rows(): summed = summed.at[:, :, 1, :].add(own_slot.astype(jnp.float32))  21 us
    ppermute x2, starting transfers between devices, padded(): lax.ppermute(head, axis, [((i + 1) % count, i) for i in range(ends)])  19.3 us
  transfers between devices with their start and end apart: 13, of which 7 were waited for; matrix products, arithmetic and copies ran while one was open for 3% of the time, Pallas kernels for 0%

commit v1 on v0

v1 whole, which is shorter than its diff:
```python
import functools

import jax
import jax.numpy as jnp
from jax import lax
from jax.experimental import pallas as pl
from jax.experimental.pallas import tpu as pltpu
from jax.sharding import PartitionSpec as P

DAMPING = 2.0 / 3.0
TILE = 64
N = 8
W = N * TILE
LANES = 128
TRASH = 3 * N
WIDE = 3 * W + LANES
ROW_D, ROW_Q, ROW_T, ROW_META, ROWS = W, W + 64, W + 128, W + 192, W + 208
VMEM = pl.BlockSpec(memory_space=pltpu.VMEM)
BF16, F32, I32 = jnp.bfloat16, jnp.float32, jnp.int32
GROUPS = 16
PART = 4
CHUNK = N * PART
TERM_W = 7 * W + LANES
DENSE = 7 * GROUPS * TILE
QUARTER = DENSE // 4


def params():
    return pltpu.CompilerParams(vmem_limit_bytes=62 << 20)


def dot(a, b):
    return jnp.dot(a, b, preferred_element_type=F32)


def iota(shape, dim):
    return lax.broadcasted_iota(I32, shape, dim)


def pack_kernel(a_ref, d_ref, q_ref, t_ref, cols_ref, mask_ref, agg_ref, agg2_ref, out_ref, meta):
    for i in range(N):
        out_ref[i * TILE:(i + 1) * TILE, :] = a_ref[i]
    for row, ref in ((ROW_D, d_ref), (ROW_Q, q_ref), (ROW_T, t_ref)):
        for w in range(N // 2):
            pair = jnp.concatenate([ref[2 * w], ref[2 * w + 1]], axis=1)
            out_ref[row:row + TILE, w * LANES:(w + 1) * LANES] = pair
    meta[...] = jnp.zeros_like(meta)
    meta[0:8, 0:8] = jnp.where(mask_ref[...] > 0, cols_ref[...], TRASH).astype(F32)
    meta[8:9, 0:8] = agg_ref[...].astype(F32)
    meta[9:10, 0:8] = agg2_ref[...].astype(F32)
    out_ref[ROW_META:ROWS, :] = meta[...].astype(BF16)


def pack(a, d, q, t, cols, mask, agg, agg2):
    return pl.pallas_call(
        pack_kernel,
        out_shape=jax.ShapeDtypeStruct((ROWS, W), BF16),
        in_specs=[VMEM] * 8,
        out_specs=VMEM,
        scratch_shapes=[pltpu.VMEM((16, W), F32)],
        compiler_params=params(),
    )(a, d, q, t, cols, mask, agg.reshape(1, N), agg2.reshape(1, N))


def halves(x):
    high = iota(x.shape, 1) >= TILE
    swapped = jnp.concatenate([x[:, TILE:], x[:, :TILE]], axis=1)
    zero = jnp.zeros_like(x)
    return (
        (jnp.where(high, zero, x), jnp.where(high, swapped, zero)),
        (jnp.where(high, zero, swapped), jnp.where(high, x, zero)),
    )


def window(index):
    return pl.ds(pl.multiple_of((index // 2) * LANES, LANES), LANES)


def pick(variants, index):
    return jnp.where(index % 2 == 1, variants[1], variants[0])


def block_diagonal(row):
    block = iota(row.shape, 1) // TILE
    zero = jnp.zeros_like(row)
    return jnp.concatenate([jnp.where(block == i, row, zero) for i in range(N)], axis=0)


def to_scalars(pairs, sem):
    copies = [pltpu.make_async_copy(v, s, sem.at[n]) for n, (v, s) in enumerate(pairs)]
    for c in copies:
        c.start()
    for c in copies:
        c.wait()


def level_kernel(m3, m2, m1, own, p1, p2, p3, c_ref, term_ref,
                 ad, sm, qs, pr, ra, tpt, meta_v, meta_s, ids_v, sem):
    near = (m2, m1, own, p1, p2)
    wide = (m3, m2, m1, own, p1, p2, p3)
    base = tuple(0 if r.shape[0] == ROWS else ROW_Q for r in wide)
    for n, ref in enumerate(wide):
        top = ROW_META - base[n]
        meta_v[n] = ref[top:top + 16, 0:LANES].astype(F32).astype(I32)
    to_scalars([(meta_v.at[n], meta_s.at[n]) for n in range(7)], sem)

    for n, ref in enumerate(wide):
        qs[n] = jnp.zeros((W, W), BF16)
        top = ROW_Q - base[n]
        for w in range(N // 2):
            sides = halves(ref[top:top + TILE, w * LANES:(w + 1) * LANES])
            for h in range(2):
                c = 2 * w + h
                g = meta_s[n, 8, c]
                qs[n, c * TILE:(c + 1) * TILE, window(g)] = pick(sides[h], g)

    for t, ref in enumerate(near):
        def place_row(i, carry, t=t, ref=ref):
            rows = pl.ds(pl.multiple_of(i * TILE, TILE), TILE)
            ad[t, rows, :] = jnp.zeros((TILE, WIDE), BF16)
            for w in range(N // 2):
                sides = halves(ref[rows, w * LANES:(w + 1) * LANES])
                for h in range(2):
                    c = meta_s[t + 1, i, 2 * w + h]
                    ad[t, rows, window(c)] = ad[t, rows, window(c)] + pick(sides[h], c)
            return carry

        lax.fori_loop(0, N, place_row, 0)
        for w in range(N // 2):
            pair = ref[ROW_D:ROW_D + TILE, w * LANES:(w + 1) * LANES]
            high = iota(pair.shape, 1) >= TILE
            zero = jnp.zeros_like(pair)
            diag = jnp.concatenate([jnp.where(high, zero, pair), jnp.where(high, pair, zero)], axis=0)
            rows = slice(w * LANES, (w + 1) * LANES)
            sm[t, rows, :] = (DAMPING * dot(diag, ad[t, rows, 0:3 * W])).astype(BF16)

    def prolong(t, carry):
        for j in range(3):
            block = -dot(sm[t, :, j * W:(j + 1) * W], qs[t + j])
            if j == 1:
                block = qs[t + 1].astype(F32) + block
            pr[t, :, j * W:(j + 1) * W] = block.astype(BF16)
        return carry

    lax.fori_loop(0, 5, prolong, 0)

    turned = [pr[t, :, (3 - t) * W:(4 - t) * W].T for t in (1, 2, 3)]
    for f in range(5):
        total = None
        for t in (1, 2, 3):
            j = f - t + 1
            if 0 <= j < 3:
                part = dot(turned[t - 1], ad[t, :, j * W:(j + 1) * W])
                total = part if total is None else total + part
        ra[:, f * W:(f + 1) * W] = total.astype(BF16)

    def coarse(o, fs):
        total = None
        for f in fs:
            part = dot(ra[:, pl.ds(pl.multiple_of(f * W, W), W)],
                       pr[f, :, pl.ds(pl.multiple_of((o - f) * W, W), W)])
            total = part if total is None else total + part
        c_ref[:, pl.ds(pl.multiple_of(o * W, W), W)] = total

    coarse(0, (0,))
    coarse(1, (0, 1))

    def middle(o, carry):
        coarse(o, (o - 2, o - 1, o))
        return carry

    lax.fori_loop(2, 5, middle, 0)
    coarse(5, (3, 4))
    coarse(6, (4,))

    here = ROW_T
    left = block_diagonal(own[here:here + TILE, :])
    lead = iota((W, W), 0)
    target = ((lead >> 2) & 7) * TILE + (lead >> 5) * PART + (lead & 3)
    turn = (target == iota((W, W), 1)).astype(F32).astype(BF16)
    tpt[...] = lax.dot_general(turn, left, (((1,), (1,)), ((), ())), preferred_element_type=F32).astype(BF16)
    ids_v[...] = jnp.zeros_like(ids_v)
    for n, ref in enumerate(wide):
        lhs = dot(tpt[...], c_ref[:, n * W:(n + 1) * W].astype(BF16)).astype(BF16)
        top = ROW_T - base[n]
        for w in range(N // 2):
            pair = ref[top:top + TILE, w * LANES:(w + 1) * LANES]
            high = iota(pair.shape, 1) >= TILE
            zero = jnp.zeros_like(pair)
            diag = jnp.concatenate([jnp.where(high, zero, pair), jnp.where(high, pair, zero)], axis=0)
            at = n * W + w * LANES
            term_ref[:, at:at + LANES] = dot(lhs[:, w * LANES:(w + 1) * LANES], diag).astype(BF16)
        ids_v[n:n + 1, :] = meta_v[n, 9:10, :].astype(F32)
    for q in range(GROUPS):
        term_ref[q * CHUNK:(q + 1) * CHUNK, 7 * W:TERM_W] = ids_v[...].astype(BF16)


def levels(*bufs):
    return pl.pallas_call(
        level_kernel,
        out_shape=(jax.ShapeDtypeStruct((W, 7 * W), F32), jax.ShapeDtypeStruct((W, TERM_W), BF16)),
        in_specs=[VMEM] * 7,
        out_specs=(VMEM, VMEM),
        scratch_shapes=[
            pltpu.VMEM((5, W, WIDE), BF16),
            pltpu.VMEM((5, W, 3 * W), BF16),
            pltpu.VMEM((7, W, W), BF16),
            pltpu.VMEM((5, W, 3 * W), BF16),
            pltpu.VMEM((W, 5 * W), BF16),
            pltpu.VMEM((W, W), BF16),
            pltpu.VMEM((7, 16, LANES), I32),
            pltpu.SMEM((7, 16, LANES), I32),
            pltpu.VMEM((CHUNK, LANES), F32),
            pltpu.SemaphoreType.DMA((7,)),
        ],
        compiler_params=params(),
    )(*bufs)


def merge_kernel(x_ref, out_ref, y, ids_v, ids_s, sem):
    for p in range(GROUPS):
        ids_v[p] = x_ref[p, 0:16, 7 * W:TERM_W].astype(F32).astype(I32)
    to_scalars([(ids_v, ids_s)], sem)
    y[...] = jnp.zeros_like(y)

    def one(n, carry):
        p, o = n // 7, n % 7
        rows = pl.ds(pl.multiple_of(p * CHUNK, CHUNK), CHUNK)
        for w in range(N // 2):
            at = pl.ds(pl.multiple_of(o * W + w * LANES, LANES), LANES)
            sides = halves(x_ref[p, :, at])
            for h in range(2):
                g = ids_s[p, o, 2 * w + h]
                cols = pl.ds(pl.multiple_of(o * GROUPS * TILE + (g // 2) * LANES, LANES), LANES)
                y[rows, cols] = y[rows, cols] + pick(sides[h], g)
        return carry

    lax.fori_loop(0, GROUPS * 7, one, 0)

    groups = jnp.concatenate([ids_v[p, 3:4, :] for p in range(GROUPS)], axis=0).astype(F32).astype(BF16)
    spread = (((iota((LANES, W), 1) >> 2) & 7) == iota((LANES, W), 0)).astype(F32).astype(BF16)
    each = dot(groups, spread)
    mine = (iota((GROUPS, W), 1) >> 5) == iota((GROUPS, W), 0)
    group = jnp.sum(jnp.where(mine, each, 0.0), axis=0, keepdims=True).astype(I32)
    row, col = iota((256, W), 0), iota((256, W), 1)
    hit = ((row >> 4) == group) & ((row & 3) == (col & 3))
    total = None
    for cq in range(4):
        take = (hit & (((row >> 2) & 3) == cq)).astype(F32).astype(BF16)
        part = dot(take, y[:, cq * QUARTER:(cq + 1) * QUARTER])
        total = part if total is None else total + part
    out_ref[...] = total.astype(BF16)


def merge(x):
    return pl.pallas_call(
        merge_kernel,
        out_shape=jax.ShapeDtypeStruct((256, QUARTER), BF16),
        in_specs=[VMEM],
        out_specs=VMEM,
        scratch_shapes=[
            pltpu.VMEM((GROUPS * CHUNK, DENSE), BF16),
            pltpu.VMEM((GROUPS, 16, LANES), I32),
            pltpu.SMEM((GROUPS, 16, LANES), I32),
            pltpu.SemaphoreType.DMA((1,)),
        ],
        compiler_params=params(),
    )(x)


def finish_kernel(x_ref, out_ref):
    row, col = iota((TILE, 256), 0), iota((TILE, 256), 1)
    same = ((row >> 2) == (col >> 4)) & ((row & 3) == (col & 3))
    for cq in range(4):
        take = (same & (((col >> 2) & 3) == cq)).astype(F32).astype(BF16)
        out_ref[0, :, cq * QUARTER:(cq + 1) * QUARTER] = dot(take, x_ref[...])


def finish(x):
    return pl.pallas_call(
        finish_kernel,
        out_shape=jax.ShapeDtypeStruct((1, TILE, DENSE), F32),
        in_specs=[VMEM],
        out_specs=VMEM,
        compiler_params=params(),
    )(x)


def along(block, step):
    count = lax.axis_size("slab")
    route = [(i, i + step) for i in range(count) if 0 <= i + step < count]
    return lax.ppermute(block, "slab", route)


def per_device(fine_tiles, fine_cols, bond_mask, diag_inv, tentative, aggregate, tentative_two, aggregate_two):
    own = pack(fine_tiles, diag_inv, tentative, tentative_two, fine_cols, bond_mask, aggregate, aggregate_two)
    m1, p1 = along(own, 1), along(own, -1)
    m2, p2 = along(m1, 1), along(p1, -1)
    m3, p3 = along(m2[ROW_Q:], 1), along(p2[ROW_Q:], -1)
    coarse, term = levels(m3, m2, m1, own, p1, p2, p3)
    got = lax.all_to_all(term.reshape(GROUPS, CHUNK, TERM_W), "piece", 0, 0)
    dense = merge(got)
    back = lax.all_to_all(dense.reshape(GROUPS, 16, QUARTER), "piece", 0, 0)
    level_two = finish(back.reshape(256, QUARTER))
    return coarse.reshape(N, TILE, 7 * W), level_two


def solution(mesh):
    both = ("slab", "piece")
    placed = (
        P(both, None, None), P(both, None), P(both, None), P(both, None, None),
        P(both, None, None), P(both), P(both, None, None), P(both),
    )
    return jax.shard_map(
        per_device,
        mesh=mesh,
        in_specs=placed,
        out_specs=(P(both, None, None), P(both, None, None)),
        check_vma=False,
    )
```

time: 844 us -> 192 us (0.23); the launches traced: 832 us -> 191 us
  waiting for transfers between devices: 427 us -> 34.2 us
  local copies, waits for them, and re-layouts: 168 us -> 0.69 us
  starting transfers between devices: 124 us -> 24.5 us
  blocking collectives: 0 us -> 74.9 us
  matrix products: 72 us -> 0 us
  Pallas kernels: 0 us -> 56.3 us
  other arithmetic: 25.5 us -> 0 us
  between operations: 15.2 us -> 0.77 us
    psum x1 -> x0, waiting for transfers between devices: 322 us -> none  [per_device(): lax.psum(partial_value.astype(jnp.bfloat16), 'piece').astype(jnp.float32)]
    ppermute x12 -> x6, starting transfers between devices: 124 us -> 24.5 us  [along(): return lax.ppermute(block, 'slab', route)]
    all_to_all x0 -> x2, blocking collectives: none -> 74.9 us  [the longest x1 54 us: per_device(): got = lax.all_to_all(term.reshape(GROUPS, CHUNK, TERM_W), 'piece', 0, 0)]
    dot_general x21 -> x0, matrix products: 72 us -> none  [the longest x1 24 us: level_partial(): both = jnp.einsum('asobt,obtq->asoq', left, right, precision=EXACT_MODE)]
    ppermute x12 -> x6, waiting for transfers between devices: 105 us -> 34.2 us  [along(): return lax.ppermute(block, 'slab', route)]
    pallas_call x0 -> x4, Pallas kernels: none -> 56.3 us  [the longest x1 29.2 us: levels(): pl.pallas_call(level_kernel, out_shape=(jax.ShapeDtypeStruct((W, 7 * W),...]
    convert_element_type x12 -> x0, local copies, waits for them, and re-layouts: 53.4 us -> none  [the longest x2 49.6 us: per_device(): partial_value.astype(jnp.bfloat16)]
    gather x16 -> x0, local copies, waits for them, and re-layouts: 43.4 us -> none  [the longest x8 33.2 us: apply_rows(): rows_in = jnp.take(prolong_rim, column, axis=0)]
  transfers between devices with their start and end apart: 13 -> 6, of which waited for: 7 -> 4; matrix products, arithmetic and copies ran while one was open for 3% -> 0% of each run, Pallas kernels for 0% -> 0%
where the time goes in v1:
time: 192 us; the launch traced here: 191 us
  blocking collectives  74.9 us (39%)
  Pallas kernels  56.3 us (29%)
  waiting for transfers between devices  34.2 us (18%)
  starting transfers between devices  24.5 us (13%)
    all_to_all x1, blocking collectives, per_device(): got = lax.all_to_all(term.reshape(GROUPS, CHUNK, TERM_W), 'piece', 0, 0)  54 us
    ppermute x6, waiting for transfers between devices, along(): return lax.ppermute(block, 'slab', route)  34.2 us
    pallas_call x1, Pallas kernels, levels(): pl.pallas_call(level_kernel, out_shape=(jax.ShapeDtypeStruct((W, 7 * W),...  29.2 us
    ppermute x6, starting transfers between devices, along(): return lax.ppermute(block, 'slab', route)  24.5 us
    pallas_call x1, Pallas kernels, merge(): pl.pallas_call(merge_kernel, out_shape=jax.ShapeDtypeStruct((256, QUARTER...  21.7 us
    all_to_all x1, blocking collectives, per_device(): back = lax.all_to_all(dense.reshape(GROUPS, 16, QUARTER), 'piece', 0, 0)  20.9 us
  transfers between devices with their start and end apart: 6, of which 4 were waited for; matrix products, arithmetic and copies ran while one was open for 0% of the time, Pallas kernels for 0%

profile of v1, /device:TPU:2, one launch (start us, length us, event | category | flops | bytes accessed | tf_op | source)
XLA Modules:
  0.0 191.5 jit_solution(501078921335240218)
XLA Ops:
  0.6 2.2 %shard_map.95.own = bf16[720,512]{1,0:T(8,128)(2,1)} custom-call(bf16[8,64,512]{2,1,0:T(8,128)(2,1)} %a_ref.1, bf16[8,64,64]{2,1,0:T(8,128)(2,1)} %d_ref.1, bf16[8,64,64]{2,1,0:T(8,128)(2,1)} %q_ref.1, bf16[8,64,64]{2,1,0:T(8,128)(2,1)} %t_ref.1, s32[8,8]{1,0:T(8,128)} %cols_ref.1, s32[8,8]{1,0:T(8,128)} %mask_ref.1, s32[1,8]{1,0:T(1,128)} %bitcast.9, ...), custom_call_target="tpu_custom_call" | custom-call | tf_op jit(solution)/shard_map/pallas_call | solution.py:55
  2.8 5.9 %collective-permute-start.3 = (bf16[720,512]{1,0:T(8,128)(2,1)}, bf16[720,512]{1,0:T(8,128)(2,1)S(1)}, u32[]{:S(2)}, u32[]{:S(2)}) collective-permute-start(bf16[720,512]{1,0:T(8,128)(2,1)} %shard_map.95.own), channel_id=1, source_target_pairs={{16,0},{32,16},{48,32},{64,48},{80,64},{96,80},{112,96},{17,1},{33... | collective-permute-start | bytes 2211848 | tf_op jit(solution)/shard_map/ppermute | solution.py:292
  8.7 1.9 %collective-permute-start = (bf16[720,512]{1,0:T(8,128)(2,1)}, bf16[720,512]{1,0:T(8,128)(2,1)S(1)}, u32[]{:S(2)}, u32[]{:S(2)}) collective-permute-start(bf16[720,512]{1,0:T(8,128)(2,1)} %shard_map.95.own), channel_id=1, source_target_pairs={{0,16},{16,32},{32,48},{48,64},{64,80},{80,96},{96,112},{1,17},{17... | collective-permute-start | bytes 2211848 | tf_op jit(solution)/shard_map/ppermute | solution.py:292
  10.7 14.1 %collective-permute-done.3.p1 = bf16[720,512]{1,0:T(8,128)(2,1)S(1)} collective-permute-done((bf16[720,512]{1,0:T(8,128)(2,1)}, bf16[720,512]{1,0:T(8,128)(2,1)S(1)}, u32[]{:S(2)}, u32[]{:S(2)}) %collective-permute-start.3) | collective-permute-done | bytes 737312 | tf_op jit(solution)/shard_map/ppermute | solution.py:292
  24.8 6.4 %collective-permute-start.4 = (bf16[720,512]{1,0:T(8,128)(2,1)S(1)}, bf16[720,512]{1,0:T(8,128)(2,1)S(1)}, u32[]{:S(2)}, u32[]{:S(2)}) collective-permute-start(bf16[720,512]{1,0:T(8,128)(2,1)S(1)} %collective-permute-done.3.p1), channel_id=1, source_target_pairs={{16,0},{32,16},{48,32},{64,48},{80,64},{96,80},{112,96},{17,1},{33... | collective-permute-start | bytes 2211848 | tf_op jit(solution)/shard_map/ppermute | solution.py:292
  31.2 0.0 collective-permute-done.m1
  31.2 0.0 copy-done.2
  31.2 0.0 copy-start.3
  31.2 1.9 %collective-permute-start.1 = (bf16[720,512]{1,0:T(8,128)(2,1)S(1)}, bf16[720,512]{1,0:T(8,128)(2,1)S(1)}, u32[]{:S(2)}, u32[]{:S(2)}) collective-permute-start(bf16[720,512]{1,0:T(8,128)(2,1)S(1)} %collective-permute-done.m1), channel_id=1, source_target_pairs={{0,16},{16,32},{32,48},{48,64},{64,80},{80,96},{96,112},{1,17},{17... | collective-permute-start | bytes 2211848 | tf_op jit(solution)/shard_map/ppermute | solution.py:292
  33.1 12.9 %collective-permute-done.4.p2 = bf16[720,512]{1,0:T(8,128)(2,1)S(1)} collective-permute-done((bf16[720,512]{1,0:T(8,128)(2,1)S(1)}, bf16[720,512]{1,0:T(8,128)(2,1)S(1)}, u32[]{:S(2)}, u32[]{:S(2)}) %collective-permute-start.4) | collective-permute-done | bytes 737312 | tf_op jit(solution)/shard_map/ppermute | solution.py:292
  46.1 6.5 %collective-permute-start.5 = (bf16[144,512]{1,0:T(8,128)(2,1)S(1)}, bf16[144,512]{1,0:T(8,128)(2,1)S(1)}, u32[]{:S(2)}, u32[]{:S(2)}) collective-permute-start(bf16[144,512]{1,0:T(8,128)(2,1)S(1)} %slice.9), channel_id=1, source_target_pairs={{16,0},{32,16},{48,32},{64,48},{80,64},{96,80},{112,96},{17,1},{33... | collective-permute-start | bytes 442376 | tf_op jit(solution)/shard_map/ppermute | solution.py:292
  52.6 0.0 collective-permute-done.1.m2
  52.6 0.0 copy-done.3
  52.6 0.0 copy-start.1
  52.6 1.9 %collective-permute-start.2 = (bf16[144,512]{1,0:T(8,128)(2,1)S(1)}, bf16[144,512]{1,0:T(8,128)(2,1)S(1)}, u32[]{:S(2)}, u32[]{:S(2)}) collective-permute-start(bf16[144,512]{1,0:T(8,128)(2,1)S(1)} %slice.8), channel_id=1, source_target_pairs={{0,16},{16,32},{32,48},{48,64},{64,80},{80,96},{96,112},{1,17},{17... | collective-permute-start | bytes 442376 | tf_op jit(solution)/shard_map/ppermute | solution.py:292
  54.6 0.7 collective-permute-done.5.p3
  55.2 6.5 %collective-permute-done.2.m3 = bf16[144,512]{1,0:T(8,128)(2,1)S(1)} collective-permute-done((bf16[144,512]{1,0:T(8,128)(2,1)S(1)}, bf16[144,512]{1,0:T(8,128)(2,1)S(1)}, u32[]{:S(2)}, u32[]{:S(2)}) %collective-permute-start.2) | collective-permute-done | bytes 147488 | tf_op jit(solution)/shard_map/ppermute | solution.py:292
  61.8 0.0 copy-done.4
  61.8 0.6 copy-done.5
  62.4 29.2 %shard_map.96 = (f32[512,3584]{1,0:T(8,128)}, bf16[512,3712]{1,0:T(8,128)(2,1)}) custom-call(bf16[144,512]{1,0:T(8,128)(2,1)} %copy-done.5, bf16[720,512]{1,0:T(8,128)(2,1)} %copy-done.1, bf16[720,512]{1,0:T(8,128)(2,1)} %copy-done.3, bf16[720,512]{1,0:T(8,128)(2,1)} %shard_map.95.own, bf16[720,512]{1,0:T(8,128)(2,1)} %copy-done.2, ...), custom_call_target="tpu_custom_call" | custom-call | tf_op jit(solution)/shard_map/pallas_call | solution.py:199
  91.7 54.0 %all_to_all.10.x_ref = bf16[16,32,3712]{2,1,0:T(8,128)(2,1)} all-to-all(bf16[16,32,3712]{2,1,0:T(8,128)(2,1)} %bitcast.6), channel_id=1, replica_groups=mesh['slab'=8,'piece'=16] {'piece'}, dimensions={0} | all-to-all | bytes 7602176 | tf_op jit(solution)/shard_map/all_to_all | solution.py:301
  145.7 21.7 %shard_map.97 = bf16[256,1792]{1,0:T(8,128)(2,1)} custom-call(bf16[16,32,3712]{2,1,0:T(8,128)(2,1)} %all_to_all.10.x_ref), custom_call_target="tpu_custom_call" | custom-call | tf_op jit(solution)/shard_map/pallas_call | solution.py:256
  167.4 20.9 %all_to_all.11 = bf16[16,16,1792]{2,1,0:T(8,128)(2,1)} all-to-all(bf16[16,16,1792]{2,1,0:T(8,128)(2,1)} %bitcast.7), channel_id=1, replica_groups=mesh['slab'=8,'piece'=16] {'piece'}, dimensions={0} | all-to-all | bytes 1835008 | tf_op jit(solution)/shard_map/all_to_all | solution.py:303
  188.3 3.2 %shard_map.98 = f32[1,64,7168]{2,1,0:T(8,128)} custom-call(bf16[256,1792]{1,0:T(8,128)(2,1)} %bitcast.8), custom_call_target="tpu_custom_call" | custom-call | tf_op jit(solution)/shard_map/pallas_call | solution.py:280
  (8 shorter events, 0.0 us)
Async XLA Ops:
  2.8 22.0 %collective-permute-start.3 = (bf16[720,512]{1,0:T(8,128)(2,1)}, bf16[720,512]{1,0:T(8,128)(2,1)S(1)}, u32[]{:S(2)}, u32[]{:S(2)}) collective-permute-start(bf16[720,512]{1,0:T(8,128)(2,1)} %shard_map.95.own), channel_id=1, source_target_pairs={{16,0},{32,16},{48,32},{64,48},{80,64},{96,80},{112,96},{17,1},{33... | collective-permute-start | bytes 2211848 | tf_op jit(solution)/shard_map/ppermute | solution.py:292
  8.7 22.4 %collective-permute-start = (bf16[720,512]{1,0:T(8,128)(2,1)}, bf16[720,512]{1,0:T(8,128)(2,1)S(1)}, u32[]{:S(2)}, u32[]{:S(2)}) collective-permute-start(bf16[720,512]{1,0:T(8,128)(2,1)} %shard_map.95.own), channel_id=1, source_target_pairs={{0,16},{16,32},{32,48},{48,64},{64,80},{80,96},{96,112},{1,17},{17... | collective-permute-start | bytes 2211848 | tf_op jit(solution)/shard_map/ppermute | solution.py:292
  24.8 6.4 %copy-start.2 = (bf16[720,512]{1,0:T(8,128)(2,1)}, bf16[720,512]{1,0:T(8,128)(2,1)S(1)}, u32[]{:S(2)}) copy-start(bf16[720,512]{1,0:T(8,128)(2,1)S(1)} %collective-permute-done.3.p1) | copy-start | bytes 2211844
  24.8 21.3 %collective-permute-start.4 = (bf16[720,512]{1,0:T(8,128)(2,1)S(1)}, bf16[720,512]{1,0:T(8,128)(2,1)S(1)}, u32[]{:S(2)}, u32[]{:S(2)}) collective-permute-start(bf16[720,512]{1,0:T(8,128)(2,1)S(1)} %collective-permute-done.3.p1), channel_id=1, source_target_pairs={{16,0},{32,16},{48,32},{64,48},{80,64},{96,80},{112,96},{17,1},{33... | collective-permute-start | bytes 2211848 | tf_op jit(solution)/shard_map/ppermute | solution.py:292
  31.2 21.4 %copy-start.3 = (bf16[720,512]{1,0:T(8,128)(2,1)}, bf16[720,512]{1,0:T(8,128)(2,1)S(1)}, u32[]{:S(2)}) copy-start(bf16[720,512]{1,0:T(8,128)(2,1)S(1)} %collective-permute-done.m1) | copy-start | bytes 2211844
  31.2 21.4 %collective-permute-start.1 = (bf16[720,512]{1,0:T(8,128)(2,1)S(1)}, bf16[720,512]{1,0:T(8,128)(2,1)S(1)}, u32[]{:S(2)}, u32[]{:S(2)}) collective-permute-start(bf16[720,512]{1,0:T(8,128)(2,1)S(1)} %collective-permute-done.m1), channel_id=1, source_target_pairs={{0,16},{16,32},{32,48},{48,64},{64,80},{80,96},{96,112},{1,17},{17... | collective-permute-start | bytes 2211848 | tf_op jit(solution)/shard_map/ppermute | solution.py:292
  46.0 15.7 %copy-start = (bf16[720,512]{1,0:T(8,128)(2,1)}, bf16[720,512]{1,0:T(8,128)(2,1)S(1)}, u32[]{:S(2)}) copy-start(bf16[720,512]{1,0:T(8,128)(2,1)S(1)} %collective-permute-done.4.p2) | copy-start | bytes 2211844
  46.1 9.2 %collective-permute-start.5 = (bf16[144,512]{1,0:T(8,128)(2,1)S(1)}, bf16[144,512]{1,0:T(8,128)(2,1)S(1)}, u32[]{:S(2)}, u32[]{:S(2)}) collective-permute-start(bf16[144,512]{1,0:T(8,128)(2,1)S(1)} %slice.9), channel_id=1, source_target_pairs={{16,0},{32,16},{48,32},{64,48},{80,64},{96,80},{112,96},{17,1},{33... | collective-permute-start | bytes 442376 | tf_op jit(solution)/shard_map/ppermute | solution.py:292
  52.6 9.2 %copy-start.1 = (bf16[720,512]{1,0:T(8,128)(2,1)}, bf16[720,512]{1,0:T(8,128)(2,1)S(1)}, u32[]{:S(2)}) copy-start(bf16[720,512]{1,0:T(8,128)(2,1)S(1)} %collective-permute-done.1.m2) | copy-start | bytes 2211844
  52.6 9.1 %collective-permute-start.2 = (bf16[144,512]{1,0:T(8,128)(2,1)S(1)}, bf16[144,512]{1,0:T(8,128)(2,1)S(1)}, u32[]{:S(2)}, u32[]{:S(2)}) collective-permute-start(bf16[144,512]{1,0:T(8,128)(2,1)S(1)} %slice.8), channel_id=1, source_target_pairs={{0,16},{16,32},{32,48},{48,64},{64,80},{80,96},{96,112},{1,17},{17... | collective-permute-start | bytes 442376 | tf_op jit(solution)/shard_map/ppermute | solution.py:292
  55.2 6.5 %copy-start.4 = (bf16[144,512]{1,0:T(8,128)(2,1)}, bf16[144,512]{1,0:T(8,128)(2,1)S(1)}, u32[]{:S(2)}) copy-start(bf16[144,512]{1,0:T(8,128)(2,1)S(1)} %collective-permute-done.5.p3) | copy-start | bytes 442372
  61.8 0.7 copy-start.5

commit v2 on v1

v2 whole, which is shorter than its diff:
```python
import functools

import jax
import jax.numpy as jnp
from jax import lax
from jax.experimental import pallas as pl
from jax.experimental.pallas import tpu as pltpu
from jax.sharding import PartitionSpec as P

DAMPING = 2.0 / 3.0
TILE = 64
N = 8
W = N * TILE
LANES = 128
TRASH = 3 * N
WIDE = 3 * W + LANES
ROW_D, ROW_Q, ROW_T, ROW_META, ROWS = W, W + 64, W + 128, W + 192, W + 208
ANY = pl.BlockSpec(memory_space=pl.ANY)
VMEM = pl.BlockSpec(memory_space=pltpu.VMEM)
BF16, F32, I32 = jnp.bfloat16, jnp.float32, jnp.int32
GROUPS = 16
PART = 4
CHUNK = N * PART
DENSE = 7 * GROUPS * TILE
QUARTER = GROUPS * TILE // 4
TAIL = pl.BlockSpec((144, W), lambda i: (ROW_Q // 144, 0))
TAIL_Q, TAIL_T, TAIL_META = 0, 64, 128


def params():
    return pltpu.CompilerParams(vmem_limit_bytes=62 << 20)


def dot(a, b):
    return jnp.dot(a, b, preferred_element_type=F32)


def iota(shape, dim):
    return lax.broadcasted_iota(I32, shape, dim)


def pack_kernel(a_ref, d_ref, q_ref, t_ref, cols_ref, mask_ref, agg_ref, agg2_ref, out_ref, meta):
    for i in range(N):
        out_ref[i * TILE:(i + 1) * TILE, :] = a_ref[i]
    for row, ref in ((ROW_D, d_ref), (ROW_Q, q_ref), (ROW_T, t_ref)):
        for w in range(N // 2):
            pair = jnp.concatenate([ref[2 * w], ref[2 * w + 1]], axis=1)
            out_ref[row:row + TILE, w * LANES:(w + 1) * LANES] = pair
    meta[...] = jnp.zeros_like(meta)
    meta[0:8, 0:8] = jnp.where(mask_ref[...] > 0, cols_ref[...], TRASH).astype(F32)
    meta[8:9, 0:8] = agg_ref[...].astype(F32)
    meta[9:10, 0:8] = agg2_ref[...].astype(F32)
    out_ref[ROW_META:ROWS, :] = meta[...].astype(BF16)


def pack(a, d, q, t, cols, mask, agg, agg2):
    return pl.pallas_call(
        pack_kernel,
        out_shape=jax.ShapeDtypeStruct((ROWS, W), BF16),
        in_specs=[VMEM] * 8,
        out_specs=VMEM,
        scratch_shapes=[pltpu.VMEM((16, W), F32)],
        compiler_params=params(),
    )(a, d, q, t, cols, mask, agg.reshape(1, N), agg2.reshape(1, N))


def halves(x):
    high = iota(x.shape, 1) >= TILE
    swapped = jnp.concatenate([x[:, TILE:], x[:, :TILE]], axis=1)
    zero = jnp.zeros_like(x)
    return (
        (jnp.where(high, zero, x), jnp.where(high, swapped, zero)),
        (jnp.where(high, zero, swapped), jnp.where(high, x, zero)),
    )


def window(index):
    return pl.ds(pl.multiple_of((index // 2) * LANES, LANES), LANES)


def pick(variants, index):
    return jnp.where(index % 2 == 1, variants[1], variants[0])


def block_diagonal(row):
    block = iota(row.shape, 1) // TILE
    zero = jnp.zeros_like(row)
    return jnp.concatenate([jnp.where(block == i, row, zero) for i in range(N)], axis=0)


def to_scalars(pairs, sem):
    copies = [pltpu.make_async_copy(v, s, sem.at[n]) for n, (v, s) in enumerate(pairs)]
    for c in copies:
        c.start()
    for c in copies:
        c.wait()


def read_meta(tails, meta_v, meta_s, sem):
    for n, (ref, top) in enumerate(tails):
        meta_v[n] = ref[top:top + 16, 0:LANES].astype(F32).astype(I32)
    to_scalars([(meta_v.at[n], meta_s.at[n]) for n in range(len(tails))], sem)


def place_q(out, ref, top, meta_s, n):
    out[...] = jnp.zeros((W, W), BF16)
    for w in range(N // 2):
        sides = halves(ref[top:top + TILE, w * LANES:(w + 1) * LANES])
        for h in range(2):
            c = 2 * w + h
            g = meta_s[n, 8, c]
            out[c * TILE:(c + 1) * TILE, window(g)] = pick(sides[h], g)


def pair_diagonal(pair):
    high = iota(pair.shape, 1) >= TILE
    zero = jnp.zeros_like(pair)
    return jnp.concatenate([jnp.where(high, zero, pair), jnp.where(high, pair, zero)], axis=0)


def place_a(refs, outs, sms, meta_s, metas):
    def place_row(i, carry):
        rows = pl.ds(pl.multiple_of(i * TILE, TILE), TILE)
        for out in outs:
            out[rows, :] = jnp.zeros((TILE, WIDE), BF16)
        for w in range(N // 2):
            sides = [halves(ref[rows, w * LANES:(w + 1) * LANES]) for ref in refs]
            for h in range(2):
                for out, side, n in zip(outs, sides, metas):
                    c = meta_s[n, i, 2 * w + h]
                    out[rows, window(c)] = out[rows, window(c)] + pick(side[h], c)
        return carry

    lax.fori_loop(0, N, place_row, 0)

    def smooth(w, carry):
        rows = pl.ds(pl.multiple_of(w * LANES, LANES), LANES)
        for ref, out, sm in zip(refs, outs, sms):
            diag = pair_diagonal(ref[ROW_D:ROW_D + TILE, rows])
            sm[rows, :] = (DAMPING * dot(diag, out[rows, 0:3 * W])).astype(BF16)
        return carry

    lax.fori_loop(0, N // 2, smooth, 0)


def write_term(term, n, tpt, c, ref, top):
    lhs = dot(tpt[...], c.astype(BF16)).astype(BF16)
    for w in range(N // 2):
        diag = pair_diagonal(ref[top:top + TILE, w * LANES:(w + 1) * LANES])
        at = n * W + w * LANES
        term[:, at:at + LANES] = dot(lhs[:, w * LANES:(w + 1) * LANES], diag).astype(BF16)


def write_ids(term, count, ids_v, meta_v, order):
    ids_v[...] = jnp.zeros_like(ids_v)
    for row, n in enumerate(order):
        ids_v[row:row + 1, :] = meta_v[n, 9:10, :].astype(F32)
    for q in range(GROUPS):
        term[q * CHUNK:(q + 1) * CHUNK, count * W:] = ids_v[...].astype(BF16)


def block(j):
    return slice(j * W, (j + 1) * W)


def own_kernel(own, ad, sm, qs, r0, tpt, meta_v, meta_s, sem):
    read_meta([(own, ROW_META)], meta_v, meta_s, sem)
    place_q(qs, own, ROW_Q, meta_s, 0)
    place_a((own,), (ad,), (sm,), meta_s, (0,))
    r0[...] = (qs[...].astype(F32) - dot(sm[:, block(1)], qs[...])).astype(BF16)
    left = block_diagonal(own[ROW_T:ROW_T + TILE, :])
    lead = iota((W, W), 0)
    target = ((lead >> 2) & 7) * TILE + (lead >> 5) * PART + (lead & 3)
    turn = (target == iota((W, W), 1)).astype(F32).astype(BF16)
    tpt[...] = lax.dot_general(turn, left, (((1,), (1,)), ((), ())), preferred_element_type=F32).astype(BF16)


def start_own(own):
    shape = jax.ShapeDtypeStruct
    return pl.pallas_call(
        own_kernel,
        out_shape=(
            shape((W, WIDE), BF16), shape((W, 3 * W), BF16), shape((W, W), BF16),
            shape((W, W), BF16), shape((W, W), BF16),
        ),
        in_specs=[VMEM],
        out_specs=(VMEM,) * 5,
        scratch_shapes=[
            pltpu.VMEM((1, 16, LANES), I32),
            pltpu.SMEM((1, 16, LANES), I32),
            pltpu.SemaphoreType.DMA((1,)),
        ],
        compiler_params=params(),
        cost_estimate=pl.CostEstimate(flops=3_000_000_000, bytes_accessed=6 << 20, transcendentals=0),
    )(own)


def fetch(pairs, sem):
    copies = [pltpu.make_async_copy(src, dst, sem.at[n]) for n, (src, dst) in enumerate(pairs)]
    for c in copies:
        c.start()
    return copies


def near_kernel(m1, p1, ad_h, sm_h, qs_h, r0_h, tpt_h, own, c_ref, term_ref, part, ra_out, smo,
                ad0, ad1, ad2, sm0, sm1, sm2, qs0, qs1, qs2, rm, r0, rp, pw, tpt, ra, cbuf, tbuf,
                meta_v, meta_s, sem, in_sem, out_sem):
    ins = fetch(((qs_h, qs1), (r0_h, r0), (ad_h, ad1), (tpt_h, tpt), (sm_h, sm1)), in_sem)
    ads, sms, qss = (ad0, ad1, ad2), (sm0, sm1, sm2), (qs0, qs1, qs2)
    read_meta([(m1, ROW_META), (p1, ROW_META)], meta_v, meta_s, sem)
    place_q(qs0, m1, ROW_Q, meta_s, 0)
    place_q(qs2, p1, ROW_Q, meta_s, 1)
    place_a((m1, p1), (ad0, ad2), (sm0, sm2), meta_s, (0, 1))
    for copy in ins:
        copy.wait()

    rm[...] = (-dot(sm0[:, block(2)], qs1[...])).astype(BF16)
    rp[...] = (-dot(sm2[:, block(0)], qs1[...])).astype(BF16)
    turned = (rm[...].T, r0[...].T, rp[...].T)
    for f in range(5):
        total = None
        for t in range(3):
            if 0 <= f - t < 3:
                piece = dot(turned[t], ads[t][:, block(f - t)])
                total = piece if total is None else total + piece
        ra[:, block(f)] = total.astype(BF16)
    for n, f in enumerate((0, 1, 3, 4)):
        ra_out[:, block(n)] = ra[:, block(f)]
    smo[:, block(0)] = sm0[:, block(0)]
    smo[:, block(1)] = sm2[:, block(2)]

    cbuf[...] = dot(ra[:, block(1)], rm[...]) + dot(ra[:, block(2)], r0[...]) + dot(ra[:, block(3)], rp[...])
    out = pltpu.make_async_copy(cbuf, c_ref.at[:, block(3)], out_sem.at[0])
    out.start()
    write_term(tbuf, 0, tpt, cbuf[...], own, TAIL_T)
    sent = pltpu.make_async_copy(tbuf, term_ref.at[:, block(0)], out_sem.at[1])
    sent.start()

    for n, (t, f, g) in enumerate(((0, 1, 0), (2, 3, 2))):
        pw[...] = (qss[t][...].astype(F32) - dot(sms[t][:, block(1)], qss[t][...])).astype(BF16)
        known = dot(ra[:, block(f)], pw[...])
        pw[...] = (-dot(sm1[:, block(g)], qss[t][...])).astype(BF16)
        part[:, block(n)] = known + dot(ra[:, block(2)], pw[...])
    out.wait()
    sent.wait()


def near(m1, p1, ad, sm, qs, r0, tpt, own):
    shape = jax.ShapeDtypeStruct
    return pl.pallas_call(
        near_kernel,
        grid=(1,),
        out_shape=(
            shape((W, 7 * W), F32), shape((W, 3 * W + LANES), BF16), shape((W, 2 * W), F32),
            shape((W, 4 * W), BF16), shape((W, 2 * W), BF16),
        ),
        in_specs=[VMEM, VMEM] + [ANY] * 5 + [TAIL],
        out_specs=(ANY, ANY, VMEM, VMEM, VMEM),
        scratch_shapes=[pltpu.VMEM((W, WIDE), BF16)] * 3
        + [pltpu.VMEM((W, 3 * W), BF16)] * 3
        + [pltpu.VMEM((W, W), BF16)] * 8
        + [
            pltpu.VMEM((W, 5 * W), BF16),
            pltpu.VMEM((W, W), F32),
            pltpu.VMEM((W, W), BF16),
            pltpu.VMEM((2, 16, LANES), I32),
            pltpu.SMEM((2, 16, LANES), I32),
            pltpu.SemaphoreType.DMA((2,)),
            pltpu.SemaphoreType.DMA((5,)),
            pltpu.SemaphoreType.DMA((2,)),
        ],
        compiler_params=params(),
        cost_estimate=pl.CostEstimate(flops=9_000_000_000, bytes_accessed=14 << 20, transcendentals=0),
    )(m1, p1, ad, sm, qs, r0, tpt, own)


def second_kernel(m2, p2, m1, p1, own, m3, p3, part_h, ra_h, tpt_h, c_in, term_in, c_ref, term_ref, smm_out, smp_out,
                  flat, smm, smp, qs, pw, part, ra, tpt, cbuf, tbuf, meta_v, meta_s, ids_v, sem, in_sem, out_sem):
    del c_in, term_in, m3, p3
    ins = fetch(((part_h, part), (ra_h, ra), (tpt_h, tpt)), in_sem)
    read_meta([(m2, ROW_META), (p2, ROW_META), (m1, TAIL_META), (p1, TAIL_META), (own, TAIL_META)],
              meta_v, meta_s, sem)
    write_ids(tbuf, 2, ids_v, meta_v, (4, 4, 2, 3))

    for n, ref in enumerate((m2, p2)):
        for w in range(N // 2):
            rows = slice(w * LANES, (w + 1) * LANES)
            diag = pair_diagonal(ref[ROW_D:ROW_D + TILE, rows])
            flat[n, rows, :] = (DAMPING * dot(diag, ref[rows, :])).astype(BF16)

    def place_row(i, carry):
        rows = pl.ds(pl.multiple_of(i * TILE, TILE), TILE)
        for out in (smm, smp):
            out[rows, :] = jnp.zeros((TILE, WIDE), BF16)
        for w in range(N // 2):
            sides = [halves(flat[n, rows, w * LANES:(w + 1) * LANES]) for n in range(2)]
            for h in range(2):
                for n, out in enumerate((smm, smp)):
                    c = meta_s[n, i, 2 * w + h]
                    out[rows, window(c)] = out[rows, window(c)] + pick(sides[n][h], c)
        return carry

    lax.fori_loop(0, N, place_row, 0)
    for copy in ins:
        copy.wait()
    outs = []
    for n, (ref, sm, j, f, o) in enumerate(((m1, smm, 2, 0, 2), (p1, smp, 0, 3, 4))):
        place_q(qs, ref, TAIL_Q, meta_s, 2 + n)
        pw[...] = (-dot(sm[:, block(j)], qs[...])).astype(BF16)
        cbuf[n] = part[:, block(n)] + dot(ra[:, block(f)], pw[...])
        outs.append(pltpu.make_async_copy(cbuf.at[n], c_ref.at[:, block(o)], out_sem.at[n]))
        outs[n].start()
        write_term(tbuf, n, tpt, cbuf[n], ref, TAIL_T)
    outs.append(pltpu.make_async_copy(tbuf, term_ref.at[:, W:], out_sem.at[2]))
    outs[2].start()
    smm_out[...] = smm[:, 0:2 * W]
    smp_out[...] = smp[:, W:3 * W]
    for out in outs:
        out.wait()


def second(m2, p2, m1, p1, own, m3, p3, part, ra, tpt, c, term):
    shape = jax.ShapeDtypeStruct
    return pl.pallas_call(
        second_kernel,
        out_shape=(
            shape((W, 7 * W), F32), shape((W, 3 * W + LANES), BF16),
            shape((W, 2 * W), BF16), shape((W, 2 * W), BF16),
        ),
        grid=(1,),
        in_specs=[VMEM, VMEM, TAIL, TAIL, TAIL] + [ANY] * 7,
        out_specs=(ANY, ANY, VMEM, VMEM),
        input_output_aliases={10: 0, 11: 1},
        scratch_shapes=[
            pltpu.VMEM((2, W, W), BF16),
            pltpu.VMEM((W, WIDE), BF16),
            pltpu.VMEM((W, WIDE), BF16),
            pltpu.VMEM((W, W), BF16),
            pltpu.VMEM((W, W), BF16),
            pltpu.VMEM((W, 2 * W), F32),
            pltpu.VMEM((W, 4 * W), BF16),
            pltpu.VMEM((W, W), BF16),
            pltpu.VMEM((2, W, W), F32),
            pltpu.VMEM((W, 2 * W + LANES), BF16),
            pltpu.VMEM((5, 16, LANES), I32),
            pltpu.SMEM((5, 16, LANES), I32),
            pltpu.VMEM((CHUNK, LANES), F32),
            pltpu.SemaphoreType.DMA((5,)),
            pltpu.SemaphoreType.DMA((3,)),
            pltpu.SemaphoreType.DMA((3,)),
        ],
        compiler_params=params(),
        cost_estimate=pl.CostEstimate(flops=6_000_000_000, bytes_accessed=12 << 20, transcendentals=0),
    )(m2, p2, m1, p1, own, m3, p3, part, ra, tpt, c, term)


def third_kernel(m3, m2, p2, p3, own, smm, smp, smo, ra, tpt, c_in, c_ref, term,
                 qa, qb, pw, cbuf, meta_v, meta_s, ids_v, sem, out_sem):
    del c_in
    read_meta([(ref, TAIL_META) for ref in (m3, m2, p2, p3, own)], meta_v, meta_s, sem)
    outs = []

    def finish_block(n, value, o, ref):
        cbuf[n] = value
        outs.append(pltpu.make_async_copy(cbuf.at[n], c_ref.at[:, block(o)], out_sem.at[n]))
        outs[-1].start()
        write_term(term, n, tpt, cbuf[n], ref, TAIL_T)

    for two, three, sm, s, mid, far, f1, f2, n2, n3, o2, o3 in (
        (m2, m3, smm, 0, 1, 0, 1, 0, 1, 0, 1, 0),
        (p2, p3, smp, 1, 0, 1, 2, 3, 2, 3, 5, 6),
    ):
        place_q(qa, two, TAIL_Q, meta_s, 1 + s)
        place_q(qb, three, TAIL_Q, meta_s, 3 * s)
        pw[...] = (-dot(smo[:, block(s)], qa[...])).astype(BF16)
        value = dot(ra[:, block(f1)], pw[...])
        pw[...] = (qa[...].astype(F32) - dot(sm[:, block(mid)], qa[...])).astype(BF16)
        finish_block(n2, value + dot(ra[:, block(f2)], pw[...]), o2, two)
        pw[...] = (-dot(sm[:, block(far)], qb[...])).astype(BF16)
        finish_block(n3, dot(ra[:, block(f2)], pw[...]), o3, three)
    write_ids(term, 4, ids_v, meta_v, (4, 0, 1, 2, 3))
    for out in outs:
        out.wait()


def third(m3, m2, p2, p3, own, smm, smp, smo, ra, tpt, c):
    shape = jax.ShapeDtypeStruct
    return pl.pallas_call(
        third_kernel,
        out_shape=(shape((W, 7 * W), F32), shape((W, 4 * W + LANES), BF16)),
        grid=(1,),
        in_specs=[VMEM, TAIL, TAIL, VMEM, TAIL] + [VMEM] * 5 + [ANY],
        out_specs=(ANY, VMEM),
        input_output_aliases={10: 0},
        scratch_shapes=[pltpu.VMEM((W, W), BF16)] * 3
        + [
            pltpu.VMEM((4, W, W), F32),
            pltpu.VMEM((5, 16, LANES), I32),
            pltpu.SMEM((5, 16, LANES), I32),
            pltpu.VMEM((CHUNK, LANES), F32),
            pltpu.SemaphoreType.DMA((5,)),
            pltpu.SemaphoreType.DMA((4,)),
        ],
        compiler_params=params(),
        cost_estimate=pl.CostEstimate(flops=7_000_000_000, bytes_accessed=18 << 20, transcendentals=0),
    )(m3, m2, p2, p3, own, smm, smp, smo, ra, tpt, c)


def gather_pieces(count, x_ref, lows, highs, ids_v, ids_s, sem):
    for p in range(GROUPS):
        ids_v[p] = x_ref[p, 0:8, count * W:].astype(F32).astype(I32)
    to_scalars([(ids_v, ids_s)], sem)
    for y in lows + highs:
        y[...] = jnp.zeros_like(y)

    def one(p, carry):
        rows = pl.ds(pl.multiple_of(p * CHUNK, CHUNK), CHUNK)
        for w in range(N // 2):
            sides = [
                [halves(x_ref[p + d, :, o * W + w * LANES:o * W + (w + 1) * LANES]) for d in (0, GROUPS // 2)]
                for o in range(count)
            ]
            for h in range(2):
                for o in range(count):
                    for y, side, d in ((lows[o], sides[o][0], 0), (highs[o], sides[o][1], GROUPS // 2)):
                        g = ids_s[p + d, 1 + o, 2 * w + h]
                        y[rows, window(g)] = y[rows, window(g)] + pick(side[h], g)
        return carry

    lax.fori_loop(0, GROUPS // 2, one, 0)


def add_pieces(count, first, takes, lows, highs, out_ref):
    for o in range(count):
        total = None
        for cq in range(4):
            cols = slice(cq * QUARTER, (cq + 1) * QUARTER)
            piece = dot(takes[cq, :, 0:256], lows[o][:, cols]) + dot(takes[cq, :, 256:W], highs[o][:, cols])
            total = piece if total is None else total + piece
        out_ref[:, (first + o) * QUARTER:(first + o + 1) * QUARTER] = total.astype(BF16)


def merge_first_kernel(count, x_ref, out_ref, takes, *rest):
    lows, highs, (ids_v, ids_s, sem) = rest[:count], rest[count:2 * count], rest[2 * count:]
    gather_pieces(count, x_ref, lows, highs, ids_v, ids_s, sem)
    groups = jnp.concatenate([ids_v[p, 0:1, :] for p in range(GROUPS)], axis=0).astype(F32).astype(BF16)
    spread = (((iota((LANES, W), 1) >> 2) & 7) == iota((LANES, W), 0)).astype(F32).astype(BF16)
    each = dot(groups, spread)
    mine = (iota((GROUPS, W), 1) >> 5) == iota((GROUPS, W), 0)
    group = jnp.sum(jnp.where(mine, each, 0.0), axis=0, keepdims=True).astype(I32)
    row, col = iota((256, W), 0), iota((256, W), 1)
    hit = ((row >> 4) == group) & ((row & 3) == (col & 3))
    for cq in range(4):
        takes[cq] = (hit & (((row >> 2) & 3) == cq)).astype(F32).astype(BF16)
    add_pieces(count, 0, takes, lows, highs, out_ref)


def merge_last_kernel(count, x_ref, done, takes, out_ref, *rest):
    lows, highs, (ids_v, ids_s, sem) = rest[:count], rest[count:2 * count], rest[2 * count:]
    out_ref[:, 0:done.shape[1]] = done[...]
    gather_pieces(count, x_ref, lows, highs, ids_v, ids_s, sem)
    add_pieces(count, done.shape[1] // QUARTER, takes, lows, highs, out_ref)


def merge(x, done=None, takes=None):
    count = x.shape[2] // W
    shape = jax.ShapeDtypeStruct
    first = done is None
    earlier = 0 if first else done.shape[1] // QUARTER
    out = shape((256, (earlier + count) * QUARTER), BF16)
    return pl.pallas_call(
        functools.partial(merge_first_kernel if first else merge_last_kernel, count),
        out_shape=(out, shape((4, 256, W), BF16)) if first else out,
        in_specs=[VMEM] * (1 if first else 3),
        out_specs=(VMEM, VMEM) if first else VMEM,
        scratch_shapes=[pltpu.VMEM((GROUPS * CHUNK // 2, GROUPS * TILE), BF16)] * (2 * count)
        + [
            pltpu.VMEM((GROUPS, 8, LANES), I32),
            pltpu.SMEM((GROUPS, 8, LANES), I32),
            pltpu.SemaphoreType.DMA((1,)),
        ],
        compiler_params=params(),
        cost_estimate=pl.CostEstimate(flops=1_000_000_000 * count, bytes_accessed=count << 20, transcendentals=0),
    )(*((x,) if first else (x, done, takes)))


def finish_kernel(orders, *refs):
    out_ref = refs[-1]
    row, col = iota((TILE, 256), 0), iota((TILE, 256), 1)
    same = ((row >> 2) == (col >> 4)) & ((row & 3) == (col & 3))
    takes = [(same & (((col >> 2) & 3) == cq)).astype(F32).astype(BF16) for cq in range(4)]
    for order, x_ref in zip(orders, refs):
        for n, o in enumerate(order):
            for cq in range(4):
                at = o * 4 * QUARTER + cq * QUARTER
                out_ref[0, :, at:at + QUARTER] = dot(takes[cq], x_ref[:, n * QUARTER:(n + 1) * QUARTER])


def finish(orders, *parts):
    return pl.pallas_call(
        functools.partial(finish_kernel, orders),
        out_shape=jax.ShapeDtypeStruct((1, TILE, DENSE), F32),
        in_specs=[VMEM] * len(parts),
        out_specs=VMEM,
        compiler_params=params(),
    )(*parts)


def along(block, step):
    count = lax.axis_size("slab")
    route = [(i, i + step) for i in range(count) if 0 <= i + step < count]
    return lax.ppermute(block, "slab", route)


def exchange(term):
    return lax.all_to_all(term.reshape(GROUPS, CHUNK, term.shape[1]), "piece", 0, 0)


def hand_over(dense):
    back = lax.all_to_all(dense.reshape(GROUPS, 16, dense.shape[1]), "piece", 0, 0)
    return back.reshape(256, dense.shape[1])


def per_device(fine_tiles, fine_cols, bond_mask, diag_inv, tentative, aggregate, tentative_two, aggregate_two):
    own = pack(fine_tiles, diag_inv, tentative, tentative_two, fine_cols, bond_mask, aggregate, aggregate_two)
    m1, p1 = along(own, 1), along(own, -1)
    ad, sm, qs, r0, tpt = start_own(own)
    m2, p2 = along(m1, 1), along(p1, -1)
    m3, p3 = along(m1[ROW_Q:], 2), along(p1[ROW_Q:], -2)
    c, term, part, ra, smo = near(m1, p1, ad, sm, qs, r0, tpt, own)
    c, term, smm, smp = second(m2, p2, m1, p1, own, m3, p3, part, ra, tpt, c, term)
    got = exchange(term)
    c, term = third(m3, m2, p2, p3, own, smm, smp, smo, ra, tpt, c)
    last = exchange(term)
    done, takes = merge(got)
    level_two = finish(((3, 2, 4, 0, 1, 5, 6),), hand_over(merge(last, done, takes)))
    return c.reshape(N, TILE, 7 * W), level_two


def solution(mesh):
    both = ("slab", "piece")
    placed = (
        P(both, None, None), P(both, None), P(both, None), P(both, None, None),
        P(both, None, None), P(both), P(both, None, None), P(both),
    )
    return jax.shard_map(
        per_device,
        mesh=mesh,
        in_specs=placed,
        out_specs=(P(both, None, None), P(both, None, None)),
        check_vma=False,
    )
```

time: 192 us -> 173 us (0.901)
  blocking collectives: 74.9 us -> 20.9 us
  waiting for transfers between devices: 34.2 us -> 50.7 us
  Pallas kernels: 56.3 us -> 66.6 us
  starting transfers between devices: 24.5 us -> 32.2 us
    all_to_all x2 -> x1, blocking collectives: 74.9 us -> 20.9 us  [hand_over(): lax.all_to_all(dense.reshape(GROUPS, 16, dense.shape[1]), 'piece', 0, 0)]
    all_to_all x0 -> x2, waiting for transfers between devices: none -> 35.5 us  [exchange(): lax.all_to_all(term.reshape(GROUPS, CHUNK, term.shape[1]), 'piece', 0, 0)]
    ppermute x6, waiting for transfers between devices: 34.2 us -> 15.2 us  [along(): return lax.ppermute(block, 'slab', route)]
    all_to_all x0 -> x2, starting transfers between devices: none -> 10.9 us  [exchange(): lax.all_to_all(term.reshape(GROUPS, CHUNK, term.shape[1]), 'piece', 0, 0)]
    pallas_call x3 -> x7, Pallas kernels: 54.1 us -> 64.3 us  [the longest x2 18.6 us: merge(): pl.pallas_call(functools.partial(merge_first_kernel if first else merge_l...]
    ppermute x6, starting transfers between devices: 24.5 us -> 21.3 us  [along(): return lax.ppermute(block, 'slab', route)]
  transfers between devices with their start and end apart: 6 -> 8, of which waited for: 4 -> 5; matrix products, arithmetic and copies ran while one was open for 0% -> 0% of each run, Pallas kernels for 0% -> 24%
where the time goes in v2:
time: 173 us; the launch traced here: 172 us
  Pallas kernels  66.6 us (38%)
  waiting for transfers between devices  50.7 us (29%)
  starting transfers between devices  32.2 us (19%)
  blocking collectives  20.9 us (12%)
    all_to_all x2, waiting for transfers between devices, exchange(): lax.all_to_all(term.reshape(GROUPS, CHUNK, term.shape[1]), 'piece', 0, 0)  35.5 us
    ppermute x6, starting transfers between devices, along(): return lax.ppermute(block, 'slab', route)  21.3 us
    all_to_all x1, blocking collectives, hand_over(): lax.all_to_all(dense.reshape(GROUPS, 16, dense.shape[1]), 'piece', 0, 0)  20.9 us
    pallas_call x2, Pallas kernels, merge(): pl.pallas_call(functools.partial(merge_first_kernel if first else merge_l...  18.6 us
    ppermute x6, waiting for transfers between devices, along(): return lax.ppermute(block, 'slab', route)  15.2 us
    pallas_call x1, Pallas kernels, near(): pl.pallas_call(near_kernel, grid=(1,), out_shape=(shape((W, 7 * W), F32),...  14.5 us
    pallas_call x1, Pallas kernels, third(): pl.pallas_call(third_kernel, out_shape=(shape((W, 7 * W), F32), shape((W,...  12.1 us
    all_to_all x2, starting transfers between devices, exchange(): lax.all_to_all(term.reshape(GROUPS, CHUNK, term.shape[1]), 'piece', 0, 0)  10.9 us
  transfers between devices with their start and end apart: 8, of which 5 were waited for; matrix products, arithmetic and copies ran while one was open for 0% of the time, Pallas kernels for 24%

profile of v2, /device:TPU:2, one launch (start us, length us, event | category | flops | bytes accessed | tf_op | source)
XLA Modules:
  0.0 172.4 jit_solution(15102820858321868662)
XLA Ops:
  0.6 2.2 %shard_map.95.own = bf16[720,512]{1,0:T(8,128)(2,1)} custom-call(bf16[8,64,512]{2,1,0:T(8,128)(2,1)} %a_ref.1, bf16[8,64,64]{2,1,0:T(8,128)(2,1)} %d_ref.1, bf16[8,64,64]{2,1,0:T(8,128)(2,1)} %q_ref.1, bf16[8,64,64]{2,1,0:T(8,128)(2,1)} %t_ref.1, s32[8,8]{1,0:T(8,128)} %cols_ref.1, s32[8,8]{1,0:T(8,128)} %mask_ref.1, s32[1,8]{1,0:T(1,128)} %bitcast.11, ...), custom_call_target="tpu_custom_call" | custom-call | tf_op jit(solution)/shard_map/pallas_call | solution.py:57
  2.9 5.9 %collective-permute-start.3 = (bf16[720,512]{1,0:T(8,128)(2,1)}, bf16[720,512]{1,0:T(8,128)(2,1)S(1)}, u32[]{:S(2)}, u32[]{:S(2)}) collective-permute-start(bf16[720,512]{1,0:T(8,128)(2,1)} %shard_map.95.own), channel_id=1, source_target_pairs={{16,0},{32,16},{48,32},{64,48},{80,64},{96,80},{112,96},{17,1},{33... | collective-permute-start | bytes 2211848 | tf_op jit(solution)/shard_map/ppermute | solution.py:512
  8.8 1.9 %collective-permute-start = (bf16[720,512]{1,0:T(8,128)(2,1)}, bf16[720,512]{1,0:T(8,128)(2,1)S(1)}, u32[]{:S(2)}, u32[]{:S(2)}) collective-permute-start(bf16[720,512]{1,0:T(8,128)(2,1)} %shard_map.95.own), channel_id=1, source_target_pairs={{0,16},{16,32},{32,48},{48,64},{64,80},{80,96},{96,112},{1,17},{17... | collective-permute-start | bytes 2211848 | tf_op jit(solution)/shard_map/ppermute | solution.py:512
  10.7 6.1 %shard_map.96 = (bf16[512,1664]{1,0:T(8,128)(2,1)}, bf16[512,1536]{1,0:T(8,128)(2,1)}, bf16[512,512]{1,0:T(8,128)(2,1)}, bf16[512,512]{1,0:T(8,128)(2,1)}, bf16[512,512]{1,0:T(8,128)(2,1)}) custom-call(bf16[720,512]{1,0:T(8,128)(2,1)} %shard_map.95.own), custom_call_target="tpu_custom_call" | custom-call | flops 3000000000 | bytes 6291456 | tf_op jit(solution)/shard_map/pallas_call | solution.py:180
  16.8 8.0 %collective-permute-done.3.p1 = bf16[720,512]{1,0:T(8,128)(2,1)S(1)} collective-permute-done((bf16[720,512]{1,0:T(8,128)(2,1)}, bf16[720,512]{1,0:T(8,128)(2,1)S(1)}, u32[]{:S(2)}, u32[]{:S(2)}) %collective-permute-start.3) | collective-permute-done | bytes 737312 | tf_op jit(solution)/shard_map/ppermute | solution.py:512
  24.8 4.1 %collective-permute-start.5 = (bf16[144,512]{1,0:T(8,128)(2,1)S(1)}, bf16[144,512]{1,0:T(8,128)(2,1)S(1)}, u32[]{:S(2)}, u32[]{:S(2)}) collective-permute-start(bf16[144,512]{1,0:T(8,128)(2,1)S(1)} %slice.9), channel_id=1, source_target_pairs={{32,0},{48,16},{64,32},{80,48},{96,64},{112,80},{33,1},{49,17},{65... | collective-permute-start | bytes 442376 | tf_op jit(solution)/shard_map/ppermute | solution.py:512
  29.0 3.1 %collective-permute-done.m1 = bf16[720,512]{1,0:T(8,128)(2,1)S(1)} collective-permute-done((bf16[720,512]{1,0:T(8,128)(2,1)}, bf16[720,512]{1,0:T(8,128)(2,1)S(1)}, u32[]{:S(2)}, u32[]{:S(2)}) %collective-permute-start) | collective-permute-done | bytes 737312 | tf_op jit(solution)/shard_map/ppermute | solution.py:512
  32.1 1.9 %collective-permute-start.1 = (bf16[144,512]{1,0:T(8,128)(2,1)S(1)}, bf16[144,512]{1,0:T(8,128)(2,1)}, u32[]{:S(2)}, u32[]{:S(2)}) collective-permute-start(bf16[144,512]{1,0:T(8,128)(2,1)S(1)} %slice.8), channel_id=1, source_target_pairs={{0,32},{16,48},{32,64},{48,80},{64,96},{80,112},{1,33},{17,49},{33... | collective-permute-start | bytes 442376 | tf_op jit(solution)/shard_map/ppermute | solution.py:512
  34.0 5.5 %collective-permute-start.4 = (bf16[720,512]{1,0:T(8,128)(2,1)S(1)}, bf16[720,512]{1,0:T(8,128)(2,1)}, u32[]{:S(2)}, u32[]{:S(2)}) collective-permute-start(bf16[720,512]{1,0:T(8,128)(2,1)S(1)} %collective-permute-done.3.p1), channel_id=1, source_target_pairs={{16,0},{32,16},{48,32},{64,48},{80,64},{96,80},{112,96},{17,1},{33... | collective-permute-start | bytes 2211848 | tf_op jit(solution)/shard_map/ppermute | solution.py:512
  39.5 1.9 %collective-permute-start.2 = (bf16[720,512]{1,0:T(8,128)(2,1)S(1)}, bf16[720,512]{1,0:T(8,128)(2,1)}, u32[]{:S(2)}, u32[]{:S(2)}) collective-permute-start(bf16[720,512]{1,0:T(8,128)(2,1)S(1)} %collective-permute-done.m1), channel_id=1, source_target_pairs={{0,16},{16,32},{32,48},{48,64},{64,80},{80,96},{96,112},{1,17},{17... | collective-permute-start | bytes 2211848 | tf_op jit(solution)/shard_map/ppermute | solution.py:512
  41.5 14.5 %shard_map.97 = (f32[512,3584]{1,0:T(8,128)}, bf16[512,1664]{1,0:T(8,128)(2,1)}, f32[512,1024]{1,0:T(8,128)}, bf16[512,2048]{1,0:T(8,128)(2,1)}, bf16[512,1024]{1,0:T(8,128)(2,1)}) custom-call(bf16[720,512]{1,0:T(8,128)(2,1)} %copy-done.2, bf16[720,512]{1,0:T(8,128)(2,1)} %copy-done.1, bf16[512,1664]{1,0:T(8,128)(2,1)} %get-tuple-element.20.ad_h, ...), custom_call_target="tpu_custom_call" | custom-call | flops 8999999488 | bytes 14680064 | tf_op jit(solution)/shard_map/pallas_call | solution.py:250
  56.0 0.0 collective-permute-done.5.p3
  56.1 4.1 %collective-permute-done.2.m2 = bf16[720,512]{1,0:T(8,128)(2,1)} collective-permute-done((bf16[720,512]{1,0:T(8,128)(2,1)S(1)}, bf16[720,512]{1,0:T(8,128)(2,1)}, u32[]{:S(2)}, u32[]{:S(2)}) %collective-permute-start.2) | collective-permute-done | bytes 737312 | tf_op jit(solution)/shard_map/ppermute | solution.py:512
  60.2 9.8 %shard_map.98 = (f32[512,3584]{1,0:T(8,128)}, bf16[512,1664]{1,0:T(8,128)(2,1)}, bf16[512,1024]{1,0:T(8,128)(2,1)}, bf16[512,1024]{1,0:T(8,128)(2,1)}) custom-call(bf16[720,512]{1,0:T(8,128)(2,1)} %collective-permute-done.2.m2, bf16[720,512]{1,0:T(8,128)(2,1)} %collective-permute-done.4.p2, ...), custom_call_target="tpu_custom_call", output_to_operand_aliasing={{0}: (10, {}), {1}: (11, {})} | custom-call | flops 6000000000 | bytes 12582912 | tf_op jit(solution)/shard_map/pallas_call | solution.py:324
  70.0 6.4 %all-to-all-start.1 = ((bf16[16,32,1664]{2,1,0:T(8,128)(2,1)}), bf16[16,32,1664]{2,1,0:T(8,128)(2,1)S(1)}, u32[]{:S(2)}, u32[]{:S(2)}) async-start(bf16[16,32,1664]{2,1,0:T(8,128)(2,1)} %bitcast.9), calls=%async_computation.1 | async-start | bytes 3407872 | tf_op jit(solution)/shard_map/all_to_all | solution.py:516
  76.5 12.1 %shard_map.99 = (f32[512,3584]{1,0:T(8,128)}, bf16[512,2176]{1,0:T(8,128)(2,1)}) custom-call(bf16[144,512]{1,0:T(8,128)(2,1)} %collective-permute-done.1.m3, bf16[720,512]{1,0:T(8,128)(2,1)} %collective-permute-done.2.m2, bf16[720,512]{1,0:T(8,128)(2,1)} %collective-permute-done.4.p2, bf16[144,512]{1,0:T(8,128)(2,1)} %copy-done.3, ...), custom_call_target="tpu_custom_call", output_to_operand_aliasing={{0}: (10, {})} | custom-call | flops 7000000000 | bytes 18874368 | tf_op jit(solution)/shard_map/pallas_call | solution.py:388
  88.6 12.9 %all-to-all-done.1.x_ref = bf16[16,32,1664]{2,1,0:T(8,128)(2,1)S(1)} async-done(((bf16[16,32,1664]{2,1,0:T(8,128)(2,1)}), bf16[16,32,1664]{2,1,0:T(8,128)(2,1)S(1)}, u32[]{:S(2)}, u32[]{:S(2)}) %all-to-all-start.1) | async-done | bytes 1703968 | tf_op jit(solution)/shard_map/all_to_all | solution.py:516
  101.5 1.2 copy-done
  102.7 4.5 %all-to-all-start = ((bf16[16,32,2176]{2,1,0:T(8,128)(2,1)}), bf16[16,32,2176]{2,1,0:T(8,128)(2,1)}, u32[]{:S(2)}, u32[]{:S(2)}) async-start(bf16[16,32,2176]{2,1,0:T(8,128)(2,1)} %bitcast.8), calls=%async_computation | async-start | bytes 4456448 | tf_op jit(solution)/shard_map/all_to_all | solution.py:516
  107.2 8.4 %shard_map.100 = (bf16[256,768]{1,0:T(8,128)(2,1)}, bf16[4,256,512]{2,1,0:T(8,128)(2,1)}) custom-call(bf16[16,32,1664]{2,1,0:T(8,128)(2,1)} %copy-done), custom_call_target="tpu_custom_call" | custom-call | flops 3000000000 | bytes 3145728 | tf_op jit(solution)/shard_map/pallas_call | solution.py:471
  115.5 22.5 %all-to-all-done.x_ref = bf16[16,32,2176]{2,1,0:T(8,128)(2,1)} async-done(((bf16[16,32,2176]{2,1,0:T(8,128)(2,1)}), bf16[16,32,2176]{2,1,0:T(8,128)(2,1)}, u32[]{:S(2)}, u32[]{:S(2)}) %all-to-all-start) | async-done | bytes 2228256 | tf_op jit(solution)/shard_map/all_to_all | solution.py:516
  138.1 10.3 %shard_map.101 = bf16[256,1792]{1,0:T(8,128)(2,1)} custom-call(bf16[16,32,2176]{2,1,0:T(8,128)(2,1)} %all-to-all-done.x_ref, bf16[256,768]{1,0:T(8,128)(2,1)} %get-tuple-element.36.done, bf16[4,256,512]{2,1,0:T(8,128)(2,1)} %get-tuple-element.37.takes), custom_call_target="tpu_custom_call" | custom-call | flops 4000000000 | bytes 4194304 | tf_op jit(solution)/shard_map/pallas_call | solution.py:471
  148.3 20.9 %all_to_all.15 = bf16[16,16,1792]{2,1,0:T(8,128)(2,1)} all-to-all(bf16[16,16,1792]{2,1,0:T(8,128)(2,1)} %bitcast.10), channel_id=1, replica_groups=mesh['slab'=8,'piece'=16] {'piece'}, dimensions={0} | all-to-all | bytes 1835008 | tf_op jit(solution)/shard_map/all_to_all | solution.py:520
  169.2 3.2 %shard_map.102 = f32[1,64,7168]{2,1,0:T(8,128)} custom-call(bf16[256,1792]{1,0:T(8,128)(2,1)} %bitcast.7), custom_call_target="tpu_custom_call" | custom-call | tf_op jit(solution)/shard_map/pallas_call | solution.py:500
  (11 shorter events, 0.0 us)
Async XLA Ops:
  2.9 22.0 %collective-permute-start.3 = (bf16[720,512]{1,0:T(8,128)(2,1)}, bf16[720,512]{1,0:T(8,128)(2,1)S(1)}, u32[]{:S(2)}, u32[]{:S(2)}) collective-permute-start(bf16[720,512]{1,0:T(8,128)(2,1)} %shard_map.95.own), channel_id=1, source_target_pairs={{16,0},{32,16},{48,32},{64,48},{80,64},{96,80},{112,96},{17,1},{33... | collective-permute-start | bytes 2211848 | tf_op jit(solution)/shard_map/ppermute | solution.py:512
  8.8 23.3 %collective-permute-start = (bf16[720,512]{1,0:T(8,128)(2,1)}, bf16[720,512]{1,0:T(8,128)(2,1)S(1)}, u32[]{:S(2)}, u32[]{:S(2)}) collective-permute-start(bf16[720,512]{1,0:T(8,128)(2,1)} %shard_map.95.own), channel_id=1, source_target_pairs={{0,16},{16,32},{32,48},{48,64},{64,80},{80,96},{96,112},{1,17},{17... | collective-permute-start | bytes 2211848 | tf_op jit(solution)/shard_map/ppermute | solution.py:512
  24.8 16.7 %copy-start.1 = (bf16[720,512]{1,0:T(8,128)(2,1)}, bf16[720,512]{1,0:T(8,128)(2,1)S(1)}, u32[]{:S(2)}) copy-start(bf16[720,512]{1,0:T(8,128)(2,1)S(1)} %collective-permute-done.3.p1) | copy-start | bytes 2211844
  24.8 31.2 %collective-permute-start.5 = (bf16[144,512]{1,0:T(8,128)(2,1)S(1)}, bf16[144,512]{1,0:T(8,128)(2,1)S(1)}, u32[]{:S(2)}, u32[]{:S(2)}) collective-permute-start(bf16[144,512]{1,0:T(8,128)(2,1)S(1)} %slice.9), channel_id=1, source_target_pairs={{32,0},{48,16},{64,32},{80,48},{96,64},{112,80},{33,1},{49,17},{65... | collective-permute-start | bytes 442376 | tf_op jit(solution)/shard_map/ppermute | solution.py:512
  32.1 9.4 %copy-start.2 = (bf16[720,512]{1,0:T(8,128)(2,1)}, bf16[720,512]{1,0:T(8,128)(2,1)S(1)}, u32[]{:S(2)}) copy-start(bf16[720,512]{1,0:T(8,128)(2,1)S(1)} %collective-permute-done.m1) | copy-start | bytes 2211844
  32.1 23.9 %collective-permute-start.1 = (bf16[144,512]{1,0:T(8,128)(2,1)S(1)}, bf16[144,512]{1,0:T(8,128)(2,1)}, u32[]{:S(2)}, u32[]{:S(2)}) collective-permute-start(bf16[144,512]{1,0:T(8,128)(2,1)S(1)} %slice.8), channel_id=1, source_target_pairs={{0,32},{16,48},{32,64},{48,80},{64,96},{80,112},{1,33},{17,49},{33... | collective-permute-start | bytes 442376 | tf_op jit(solution)/shard_map/ppermute | solution.py:512
  34.0 22.0 %collective-permute-start.4 = (bf16[720,512]{1,0:T(8,128)(2,1)S(1)}, bf16[720,512]{1,0:T(8,128)(2,1)}, u32[]{:S(2)}, u32[]{:S(2)}) collective-permute-start(bf16[720,512]{1,0:T(8,128)(2,1)S(1)} %collective-permute-done.3.p1), channel_id=1, source_target_pairs={{16,0},{32,16},{48,32},{64,48},{80,64},{96,80},{112,96},{17,1},{33... | collective-permute-start | bytes 2211848 | tf_op jit(solution)/shard_map/ppermute | solution.py:512
  39.5 20.6 %collective-permute-start.2 = (bf16[720,512]{1,0:T(8,128)(2,1)S(1)}, bf16[720,512]{1,0:T(8,128)(2,1)}, u32[]{:S(2)}, u32[]{:S(2)}) collective-permute-start(bf16[720,512]{1,0:T(8,128)(2,1)S(1)} %collective-permute-done.m1), channel_id=1, source_target_pairs={{0,16},{16,32},{32,48},{48,64},{64,80},{80,96},{96,112},{1,17},{17... | collective-permute-start | bytes 2211848 | tf_op jit(solution)/shard_map/ppermute | solution.py:512
  56.0 4.2 %copy-start.3 = (bf16[144,512]{1,0:T(8,128)(2,1)}, bf16[144,512]{1,0:T(8,128)(2,1)S(1)}, u32[]{:S(2)}) copy-start(bf16[144,512]{1,0:T(8,128)(2,1)S(1)} %collective-permute-done.5.p3) | copy-start | bytes 442372
  70.0 31.5 %all-to-all-start.1 = ((bf16[16,32,1664]{2,1,0:T(8,128)(2,1)}), bf16[16,32,1664]{2,1,0:T(8,128)(2,1)S(1)}, u32[]{:S(2)}, u32[]{:S(2)}) async-start(bf16[16,32,1664]{2,1,0:T(8,128)(2,1)} %bitcast.9), calls=%async_computation.1 | async-start | bytes 3407872 | tf_op jit(solution)/shard_map/all_to_all | solution.py:516
  101.5 1.2 copy-start
  102.7 35.4 %all-to-all-start = ((bf16[16,32,2176]{2,1,0:T(8,128)(2,1)}), bf16[16,32,2176]{2,1,0:T(8,128)(2,1)}, u32[]{:S(2)}, u32[]{:S(2)}) async-start(bf16[16,32,2176]{2,1,0:T(8,128)(2,1)} %bitcast.8), calls=%async_computation | async-start | bytes 4456448 | tf_op jit(solution)/shard_map/all_to_all | solution.py:516

commit v3 on v2

--- a/solution.py
+++ b/solution.py
@@ -6,6 +6,7 @@
 from jax.experimental import pallas as pl
 from jax.experimental.pallas import tpu as pltpu
 from jax.sharding import PartitionSpec as P
+
 
 DAMPING = 2.0 / 3.0
 TILE = 64
@@ -75,11 +76,11 @@
 
 
 def window(index):
-    return pl.ds(pl.multiple_of((index // 2) * LANES, LANES), LANES)
+    return pl.ds(pl.multiple_of((index >> 1) * LANES, LANES), LANES)
 
 
 def pick(variants, index):
-    return jnp.where(index % 2 == 1, variants[1], variants[0])
+    return jnp.where((index & 1) == 1, variants[1], variants[0])
 
 
 def block_diagonal(row):
@@ -163,11 +164,14 @@
     return slice(j * W, (j + 1) * W)
 
 
-def own_kernel(own, ad, sm, qs, r0, tpt, meta_v, meta_s, sem):
+def own_kernel(own, rap, sm, qs, r0, tpt, ad, meta_v, meta_s, sem):
     read_meta([(own, ROW_META)], meta_v, meta_s, sem)
     place_q(qs, own, ROW_Q, meta_s, 0)
     place_a((own,), (ad,), (sm,), meta_s, (0,))
     r0[...] = (qs[...].astype(F32) - dot(sm[:, block(1)], qs[...])).astype(BF16)
+    turned = r0[...].T
+    for j in range(3):
+        rap[:, block(j)] = dot(turned, ad[:, block(j)])
     left = block_diagonal(own[ROW_T:ROW_T + TILE, :])
     lead = iota((W, W), 0)
     target = ((lead >> 2) & 7) * TILE + (lead >> 5) * PART + (lead & 3)
@@ -180,12 +184,13 @@
     return pl.pallas_call(
         own_kernel,
         out_shape=(
-            shape((W, WIDE), BF16), shape((W, 3 * W), BF16), shape((W, W), BF16),
+            shape((W, 3 * W), F32), shape((W, 3 * W), BF16), shape((W, W), BF16),
             shape((W, W), BF16), shape((W, W), BF16),
         ),
         in_specs=[VMEM],
         out_specs=(VMEM,) * 5,
         scratch_shapes=[
+            pltpu.VMEM((W, WIDE), BF16),
             pltpu.VMEM((1, 16, LANES), I32),
             pltpu.SMEM((1, 16, LANES), I32),
             pltpu.SemaphoreType.DMA((1,)),
@@ -202,28 +207,25 @@
     return copies
 
 
-def near_kernel(m1, p1, ad_h, sm_h, qs_h, r0_h, tpt_h, own, c_ref, term_ref, part, ra_out, smo,
-                ad0, ad1, ad2, sm0, sm1, sm2, qs0, qs1, qs2, rm, r0, rp, pw, tpt, ra, cbuf, tbuf,
+def near_kernel(m1, p1, rap_h, sm_h, qs_h, r0_h, tpt_h, own, c_ref, term_ref, part, ra_out, smo, m1_tail, p1_tail,
+                ad0, ad2, sm0, sm1, sm2, qs0, qs1, qs2, rm, r0, rp, tpt, rap, ra, cbuf, tbuf,
                 meta_v, meta_s, sem, in_sem, out_sem):
-    ins = fetch(((qs_h, qs1), (r0_h, r0), (ad_h, ad1), (tpt_h, tpt), (sm_h, sm1)), in_sem)
-    ads, sms, qss = (ad0, ad1, ad2), (sm0, sm1, sm2), (qs0, qs1, qs2)
+    ins = fetch(((qs_h, qs1), (rap_h, rap), (r0_h, r0), (tpt_h, tpt), (sm_h, sm1)), in_sem)
+    m1_tail[...] = m1[ROW_Q:ROWS, :]
+    p1_tail[...] = p1[ROW_Q:ROWS, :]
     read_meta([(m1, ROW_META), (p1, ROW_META)], meta_v, meta_s, sem)
-    place_q(qs0, m1, ROW_Q, meta_s, 0)
-    place_q(qs2, p1, ROW_Q, meta_s, 1)
     place_a((m1, p1), (ad0, ad2), (sm0, sm2), meta_s, (0, 1))
     for copy in ins:
         copy.wait()
 
     rm[...] = (-dot(sm0[:, block(2)], qs1[...])).astype(BF16)
     rp[...] = (-dot(sm2[:, block(0)], qs1[...])).astype(BF16)
-    turned = (rm[...].T, r0[...].T, rp[...].T)
-    for f in range(5):
-        total = None
-        for t in range(3):
-            if 0 <= f - t < 3:
-                piece = dot(turned[t], ads[t][:, block(f - t)])
-                total = piece if total is None else total + piece
-        ra[:, block(f)] = total.astype(BF16)
+    before, after = rm[...].T, rp[...].T
+    ra[:, block(0)] = dot(before, ad0[:, block(0)]).astype(BF16)
+    ra[:, block(1)] = (dot(before, ad0[:, block(1)]) + rap[:, block(0)]).astype(BF16)
+    ra[:, block(2)] = (dot(before, ad0[:, block(2)]) + dot(after, ad2[:, block(0)]) + rap[:, block(1)]).astype(BF16)
+    ra[:, block(3)] = (dot(after, ad2[:, block(1)]) + rap[:, block(2)]).astype(BF16)
+    ra[:, block(4)] = dot(after, ad2[:, block(2)]).astype(BF16)
     for n, f in enumerate((0, 1, 3, 4)):
         ra_out[:, block(n)] = ra[:, block(f)]
     smo[:, block(0)] = sm0[:, block(0)]
@@ -236,30 +238,30 @@
     sent = pltpu.make_async_copy(tbuf, term_ref.at[:, block(0)], out_sem.at[1])
     sent.start()
 
-    for n, (t, f, g) in enumerate(((0, 1, 0), (2, 3, 2))):
-        pw[...] = (qss[t][...].astype(F32) - dot(sms[t][:, block(1)], qss[t][...])).astype(BF16)
-        known = dot(ra[:, block(f)], pw[...])
-        pw[...] = (-dot(sm1[:, block(g)], qss[t][...])).astype(BF16)
-        part[:, block(n)] = known + dot(ra[:, block(2)], pw[...])
+    for n, (f, sm, g) in enumerate(((1, sm0, 0), (3, sm2, 2))):
+        lead = ra[:, block(f)]
+        known = dot(lead, sm[:, block(1)]) + dot(ra[:, block(2)], sm1[:, block(g)])
+        part[:, block(n)] = lead.astype(F32) - known
     out.wait()
     sent.wait()
 
 
-def near(m1, p1, ad, sm, qs, r0, tpt, own):
+def near(m1, p1, rap, sm, qs, r0, tpt, own):
     shape = jax.ShapeDtypeStruct
     return pl.pallas_call(
         near_kernel,
         grid=(1,),
         out_shape=(
-            shape((W, 7 * W), F32), shape((W, 3 * W + LANES), BF16), shape((W, 2 * W), F32),
-            shape((W, 4 * W), BF16), shape((W, 2 * W), BF16),
+            shape((W, 7 * W), F32), shape((W, 2 * W + LANES), BF16), shape((W, 2 * W), F32),
+            shape((W, 4 * W), BF16), shape((W, 2 * W), BF16), shape((144, W), BF16), shape((144, W), BF16),
         ),
         in_specs=[VMEM, VMEM] + [ANY] * 5 + [TAIL],
-        out_specs=(ANY, ANY, VMEM, VMEM, VMEM),
-        scratch_shapes=[pltpu.VMEM((W, WIDE), BF16)] * 3
+        out_specs=(ANY, ANY) + (VMEM,) * 5,
+        scratch_shapes=[pltpu.VMEM((W, WIDE), BF16)] * 2
         + [pltpu.VMEM((W, 3 * W), BF16)] * 3
-        + [pltpu.VMEM((W, W), BF16)] * 8
+        + [pltpu.VMEM((W, W), BF16)] * 7
         + [
+            pltpu.VMEM((W, 3 * W), F32),
             pltpu.VMEM((W, 5 * W), BF16),
             pltpu.VMEM((W, W), F32),
             pltpu.VMEM((W, W), BF16),
@@ -271,139 +273,136 @@
         ],
         compiler_params=params(),
         cost_estimate=pl.CostEstimate(flops=9_000_000_000, bytes_accessed=14 << 20, transcendentals=0),
-    )(m1, p1, ad, sm, qs, r0, tpt, own)
-
-
-def second_kernel(m2, p2, m1, p1, own, m3, p3, part_h, ra_h, tpt_h, c_in, term_in, c_ref, term_ref, smm_out, smp_out,
-                  flat, smm, smp, qs, pw, part, ra, tpt, cbuf, tbuf, meta_v, meta_s, ids_v, sem, in_sem, out_sem):
-    del c_in, term_in, m3, p3
-    ins = fetch(((part_h, part), (ra_h, ra), (tpt_h, tpt)), in_sem)
-    read_meta([(m2, ROW_META), (p2, ROW_META), (m1, TAIL_META), (p1, TAIL_META), (own, TAIL_META)],
-              meta_v, meta_s, sem)
-    write_ids(tbuf, 2, ids_v, meta_v, (4, 4, 2, 3))
-
-    for n, ref in enumerate((m2, p2)):
+    )(m1, p1, rap, sm, qs, r0, tpt, own)
+
+
+def smooth_far(ref, flat, sm, meta_s, n):
+    for w in range(N // 2):
+        rows = slice(w * LANES, (w + 1) * LANES)
+        diag = pair_diagonal(ref[ROW_D:ROW_D + TILE, rows])
+        flat[rows, :] = (DAMPING * dot(diag, ref[rows, :])).astype(BF16)
+    tops = (0, W // 2)
+
+    def place_row(i, carry):
+        starts = [pl.ds(pl.multiple_of(top + i * TILE, TILE), TILE) for top in tops]
+        for rows in starts:
+            sm[rows, :] = jnp.zeros((TILE, WIDE), BF16)
         for w in range(N // 2):
-            rows = slice(w * LANES, (w + 1) * LANES)
-            diag = pair_diagonal(ref[ROW_D:ROW_D + TILE, rows])
-            flat[n, rows, :] = (DAMPING * dot(diag, ref[rows, :])).astype(BF16)
-
-    def place_row(i, carry):
-        rows = pl.ds(pl.multiple_of(i * TILE, TILE), TILE)
-        for out in (smm, smp):
-            out[rows, :] = jnp.zeros((TILE, WIDE), BF16)
-        for w in range(N // 2):
-            sides = [halves(flat[n, rows, w * LANES:(w + 1) * LANES]) for n in range(2)]
+            sides = [halves(flat[rows, w * LANES:(w + 1) * LANES]) for rows in starts]
             for h in range(2):
-                for n, out in enumerate((smm, smp)):
-                    c = meta_s[n, i, 2 * w + h]
-                    out[rows, window(c)] = out[rows, window(c)] + pick(sides[n][h], c)
+                for d, rows in enumerate(starts):
+                    c = meta_s[n, i + d * N // 2, 2 * w + h]
+                    sm[rows, window(c)] = sm[rows, window(c)] + pick(sides[d][h], c)
         return carry
 
-    lax.fori_loop(0, N, place_row, 0)
+    lax.fori_loop(0, N // 2, place_row, 0)
+
+
+def second_kernel(m2, m1, own, part_h, ra_h, tpt_h, c_in, term_in, c_ref, term_ref, smm_out,
+                  flat, smm, qs, pw, part, ra, tpt, cbuf, tbuf, meta_v, meta_s, ids_v, sem, in_sem, out_sem):
+    del c_in, term_in
+    ins = fetch(((part_h.at[:, block(0)], part), (ra_h.at[:, block(0)], ra), (tpt_h, tpt)), in_sem)
+    read_meta([(m2, ROW_META), (m1, TAIL_META), (own, TAIL_META)], meta_v, meta_s, sem)
+    write_ids(tbuf, 1, ids_v, meta_v, (2, 2, 1))
+    smooth_far(m2, flat, smm, meta_s, 0)
+    place_q(qs, m1, TAIL_Q, meta_s, 1)
     for copy in ins:
         copy.wait()
+    pw[...] = (part[...] - dot(ra[...], smm[:, block(2)])).astype(BF16)
+    cbuf[...] = dot(pw[...], qs[...])
+    out = pltpu.make_async_copy(cbuf, c_ref.at[:, block(2)], out_sem.at[0])
+    out.start()
+    write_term(tbuf, 0, tpt, cbuf[...], m1, TAIL_T)
+    sent = pltpu.make_async_copy(tbuf, term_ref.at[:, W:], out_sem.at[1])
+    sent.start()
+    smm_out[...] = smm[:, 0:2 * W]
+    out.wait()
+    sent.wait()
+
+
+def second(m2, m1, own, part, ra, tpt, c, term):
+    shape = jax.ShapeDtypeStruct
+    return pl.pallas_call(
+        second_kernel,
+        out_shape=(shape((W, 7 * W), F32), shape((W, 2 * W + LANES), BF16), shape((W, 2 * W), BF16)),
+        grid=(1,),
+        in_specs=[VMEM, TAIL, TAIL] + [ANY] * 5,
+        out_specs=(ANY, ANY, VMEM),
+        input_output_aliases={6: 0, 7: 1},
+        scratch_shapes=[
+            pltpu.VMEM((W, W), BF16),
+            pltpu.VMEM((W, WIDE), BF16),
+            pltpu.VMEM((W, W), BF16),
+            pltpu.VMEM((W, W), BF16),
+            pltpu.VMEM((W, W), F32),
+            pltpu.VMEM((W, W), BF16),
+            pltpu.VMEM((W, W), BF16),
+            pltpu.VMEM((W, W), F32),
+            pltpu.VMEM((W, W + LANES), BF16),
+            pltpu.VMEM((3, 16, LANES), I32),
+            pltpu.SMEM((3, 16, LANES), I32),
+            pltpu.VMEM((CHUNK, LANES), F32),
+            pltpu.SemaphoreType.DMA((3,)),
+            pltpu.SemaphoreType.DMA((3,)),
+            pltpu.SemaphoreType.DMA((2,)),
+        ],
+        compiler_params=params(),
+        cost_estimate=pl.CostEstimate(flops=4_000_000_000, bytes_accessed=8 << 20, transcendentals=0),
+    )(m2, m1, own, part, ra, tpt, c, term)
+
+
+def third_kernel(p2, p1, m3, m2, p3, own, part, smm, smo, ra, tpt, c_in, c_ref, term,
+                 flat, smp, qs, pw, cbuf, meta_v, meta_s, ids_v, sem, out_sem):
+    del c_in
+    read_meta([(p2, ROW_META)] + [(ref, TAIL_META) for ref in (p1, m2, m3, p3, own)], meta_v, meta_s, sem)
+    write_ids(term, 5, ids_v, meta_v, (5, 1, 2, 0, 3, 4))
+    smooth_far(p2, flat, smp, meta_s, 0)
     outs = []
-    for n, (ref, sm, j, f, o) in enumerate(((m1, smm, 2, 0, 2), (p1, smp, 0, 3, 4))):
-        place_q(qs, ref, TAIL_Q, meta_s, 2 + n)
-        pw[...] = (-dot(sm[:, block(j)], qs[...])).astype(BF16)
-        cbuf[n] = part[:, block(n)] + dot(ra[:, block(f)], pw[...])
+
+    def columns(n, value, o, ref, top, at):
+        pw[...] = value.astype(BF16)
+        place_q(qs, ref, top, meta_s, at)
+        cbuf[n] = dot(pw[...], qs[...])
         outs.append(pltpu.make_async_copy(cbuf.at[n], c_ref.at[:, block(o)], out_sem.at[n]))
-        outs[n].start()
-        write_term(tbuf, n, tpt, cbuf[n], ref, TAIL_T)
-    outs.append(pltpu.make_async_copy(tbuf, term_ref.at[:, W:], out_sem.at[2]))
-    outs[2].start()
-    smm_out[...] = smm[:, 0:2 * W]
-    smp_out[...] = smp[:, W:3 * W]
+        outs[-1].start()
+        write_term(term, n, tpt, cbuf[n], ref, top + TILE)
+
+    first, last = ra[:, block(0)], ra[:, block(3)]
+    columns(0, part[:, block(1)] - dot(last, smp[:, block(0)]), 4, p1, TAIL_Q, 1)
+    value = first.astype(F32) - dot(first, smm[:, block(1)]) - dot(ra[:, block(1)], smo[:, block(0)])
+    columns(1, value, 1, m2, TAIL_Q, 2)
+    value = last.astype(F32) - dot(last, smp[:, block(1)]) - dot(ra[:, block(2)], smo[:, block(1)])
+    columns(2, value, 5, p2, ROW_Q, 0)
+    columns(3, -dot(first, smm[:, block(0)]), 0, m3, TAIL_Q, 3)
+    columns(4, -dot(last, smp[:, block(2)]), 6, p3, TAIL_Q, 4)
     for out in outs:
         out.wait()
 
 
-def second(m2, p2, m1, p1, own, m3, p3, part, ra, tpt, c, term):
+def third(p2, p1, m3, m2, p3, own, part, smm, smo, ra, tpt, c):
     shape = jax.ShapeDtypeStruct
     return pl.pallas_call(
-        second_kernel,
-        out_shape=(
-            shape((W, 7 * W), F32), shape((W, 3 * W + LANES), BF16),
-            shape((W, 2 * W), BF16), shape((W, 2 * W), BF16),
-        ),
+        third_kernel,
+        out_shape=(shape((W, 7 * W), F32), shape((W, 5 * W + LANES), BF16)),
         grid=(1,),
-        in_specs=[VMEM, VMEM, TAIL, TAIL, TAIL] + [ANY] * 7,
-        out_specs=(ANY, ANY, VMEM, VMEM),
-        input_output_aliases={10: 0, 11: 1},
+        in_specs=[VMEM, TAIL, VMEM, TAIL, VMEM, TAIL] + [VMEM] * 5 + [ANY],
+        out_specs=(ANY, VMEM),
+        input_output_aliases={11: 0},
         scratch_shapes=[
-            pltpu.VMEM((2, W, W), BF16),
+            pltpu.VMEM((W, W), BF16),
             pltpu.VMEM((W, WIDE), BF16),
-            pltpu.VMEM((W, WIDE), BF16),
-            pltpu.VMEM((W, W), BF16),
-            pltpu.VMEM((W, W), BF16),
-            pltpu.VMEM((W, 2 * W), F32),
-            pltpu.VMEM((W, 4 * W), BF16),
-            pltpu.VMEM((W, W), BF16),
-            pltpu.VMEM((2, W, W), F32),
-            pltpu.VMEM((W, 2 * W + LANES), BF16),
-            pltpu.VMEM((5, 16, LANES), I32),
-            pltpu.SMEM((5, 16, LANES), I32),
+            pltpu.VMEM((W, W), BF16),
+            pltpu.VMEM((W, W), BF16),
+            pltpu.VMEM((5, W, W), F32),
+            pltpu.VMEM((6, 16, LANES), I32),
+            pltpu.SMEM((6, 16, LANES), I32),
             pltpu.VMEM((CHUNK, LANES), F32),
+            pltpu.SemaphoreType.DMA((6,)),
             pltpu.SemaphoreType.DMA((5,)),
-            pltpu.SemaphoreType.DMA((3,)),
-            pltpu.SemaphoreType.DMA((3,)),
         ],
         compiler_params=params(),
-        cost_estimate=pl.CostEstimate(flops=6_000_000_000, bytes_accessed=12 << 20, transcendentals=0),
-    )(m2, p2, m1, p1, own, m3, p3, part, ra, tpt, c, term)
-
-
-def third_kernel(m3, m2, p2, p3, own, smm, smp, smo, ra, tpt, c_in, c_ref, term,
-                 qa, qb, pw, cbuf, meta_v, meta_s, ids_v, sem, out_sem):
-    del c_in
-    read_meta([(ref, TAIL_META) for ref in (m3, m2, p2, p3, own)], meta_v, meta_s, sem)
-    outs = []
-
-    def finish_block(n, value, o, ref):
-        cbuf[n] = value
-        outs.append(pltpu.make_async_copy(cbuf.at[n], c_ref.at[:, block(o)], out_sem.at[n]))
-        outs[-1].start()
-        write_term(term, n, tpt, cbuf[n], ref, TAIL_T)
-
-    for two, three, sm, s, mid, far, f1, f2, n2, n3, o2, o3 in (
-        (m2, m3, smm, 0, 1, 0, 1, 0, 1, 0, 1, 0),
-        (p2, p3, smp, 1, 0, 1, 2, 3, 2, 3, 5, 6),
-    ):
-        place_q(qa, two, TAIL_Q, meta_s, 1 + s)
-        place_q(qb, three, TAIL_Q, meta_s, 3 * s)
-        pw[...] = (-dot(smo[:, block(s)], qa[...])).astype(BF16)
-        value = dot(ra[:, block(f1)], pw[...])
-        pw[...] = (qa[...].astype(F32) - dot(sm[:, block(mid)], qa[...])).astype(BF16)
-        finish_block(n2, value + dot(ra[:, block(f2)], pw[...]), o2, two)
-        pw[...] = (-dot(sm[:, block(far)], qb[...])).astype(BF16)
-        finish_block(n3, dot(ra[:, block(f2)], pw[...]), o3, three)
-    write_ids(term, 4, ids_v, meta_v, (4, 0, 1, 2, 3))
-    for out in outs:
-        out.wait()
-
-
-def third(m3, m2, p2, p3, own, smm, smp, smo, ra, tpt, c):
-    shape = jax.ShapeDtypeStruct
-    return pl.pallas_call(
-        third_kernel,
-        out_shape=(shape((W, 7 * W), F32), shape((W, 4 * W + LANES), BF16)),
-        grid=(1,),
-        in_specs=[VMEM, TAIL, TAIL, VMEM, TAIL] + [VMEM] * 5 + [ANY],
-        out_specs=(ANY, VMEM),
-        input_output_aliases={10: 0},
-        scratch_shapes=[pltpu.VMEM((W, W), BF16)] * 3
-        + [
-            pltpu.VMEM((4, W, W), F32),
-            pltpu.VMEM((5, 16, LANES), I32),
-            pltpu.SMEM((5, 16, LANES), I32),
-            pltpu.VMEM((CHUNK, LANES), F32),
-            pltpu.SemaphoreType.DMA((5,)),
-            pltpu.SemaphoreType.DMA((4,)),
-        ],
-        compiler_params=params(),
         cost_estimate=pl.CostEstimate(flops=7_000_000_000, bytes_accessed=18 << 20, transcendentals=0),
-    )(m3, m2, p2, p3, own, smm, smp, smo, ra, tpt, c)
+    )(p2, p1, m3, m2, p3, own, part, smm, smo, ra, tpt, c)
 
 
 def gather_pieces(count, x_ref, lows, highs, ids_v, ids_s, sem):
@@ -521,19 +520,21 @@
     return back.reshape(256, dense.shape[1])
 
 
-def per_device(fine_tiles, fine_cols, bond_mask, diag_inv, tentative, aggregate, tentative_two, aggregate_two):
+def device_part(fine_tiles, fine_cols, bond_mask, diag_inv, tentative, aggregate, tentative_two, aggregate_two):
     own = pack(fine_tiles, diag_inv, tentative, tentative_two, fine_cols, bond_mask, aggregate, aggregate_two)
     m1, p1 = along(own, 1), along(own, -1)
-    ad, sm, qs, r0, tpt = start_own(own)
-    m2, p2 = along(m1, 1), along(p1, -1)
-    m3, p3 = along(m1[ROW_Q:], 2), along(p1[ROW_Q:], -2)
-    c, term, part, ra, smo = near(m1, p1, ad, sm, qs, r0, tpt, own)
-    c, term, smm, smp = second(m2, p2, m1, p1, own, m3, p3, part, ra, tpt, c, term)
+    rap, sm, qs, r0, tpt = start_own(own)
+    m2 = along(m1, 1)
+    p2 = along(p1, -1)
+    c, term, part, ra, smo, m1_tail, p1_tail = near(m1, p1, rap, sm, qs, r0, tpt, own)
+    m3 = along(m1_tail, 2)
+    p3 = along(p1_tail, -2)
+    c, term, smm = second(m2, m1, own, part, ra, tpt, c, term)
     got = exchange(term)
-    c, term = third(m3, m2, p2, p3, own, smm, smp, smo, ra, tpt, c)
+    c, term = third(p2, p1, m3, m2, p3, own, part, smm, smo, ra, tpt, c)
     last = exchange(term)
     done, takes = merge(got)
-    level_two = finish(((3, 2, 4, 0, 1, 5, 6),), hand_over(merge(last, done, takes)))
+    level_two = finish(((3, 2, 4, 1, 5, 0, 6),), hand_over(merge(last, done, takes)))
     return c.reshape(N, TILE, 7 * W), level_two
 
 
@@ -544,7 +545,7 @@
         P(both, None, None), P(both), P(both, None, None), P(both),
     )
     return jax.shard_map(
-        per_device,
+        device_part,
         mesh=mesh,
         in_specs=placed,
         out_specs=(P(both, None, None), P(both, None, None)),

time: 173 us -> 173 us (level); the launches traced: 172 us -> 170 us
  Pallas kernels: 66.6 us -> 60.6 us
  starting transfers between devices: 32.2 us -> 37 us
  waiting for transfers between devices: 50.7 us -> 48.5 us
    all_to_all x2, waiting for transfers between devices: 35.5 us -> 30.4 us  [exchange(): lax.all_to_all(term.reshape(GROUPS, CHUNK, term.shape[1]), 'piece', 0, 0)]
    pallas_call x2, Pallas kernels: 18.6 us -> 15.1 us  [merge(): pl.pallas_call(functools.partial(merge_first_kernel if first else merge_l...]
    pallas_call x1, Pallas kernels: 9.8 us -> 6.44 us  [second(): pl.pallas_call(second_kernel, out_shape=(shape((W, 7 * W), F32), shape((W...]
    ppermute x6, starting transfers between devices: 21.3 us -> 24.3 us  [along(): return lax.ppermute(block, 'slab', route)]
    ppermute x6, waiting for transfers between devices: 15.2 us -> 18.1 us  [along(): return lax.ppermute(block, 'slab', route)]
    pallas_call x1, Pallas kernels: 12.1 us -> 14.3 us  [third(): pl.pallas_call(third_kernel, out_shape=(shape((W, 7 * W), F32), shape((W,...]
    pallas_call x1, Pallas kernels: 14.5 us -> 12.3 us  [near(): pl.pallas_call(near_kernel, grid=(1,), out_shape=(shape((W, 7 * W), F32),...]
    all_to_all x2, starting transfers between devices: 10.9 us -> 12.7 us  [exchange(): lax.all_to_all(term.reshape(GROUPS, CHUNK, term.shape[1]), 'piece', 0, 0)]
  transfers between devices with their start and end apart: 8 -> 8, of which waited for: 5 -> 4; matrix products, arithmetic and copies ran while one was open for 0% -> 0% of each run, Pallas kernels for 24% -> 27%
where the time goes in v3:
time: 173 us; the launch traced here: 170 us
  Pallas kernels  60.6 us (35%)
  waiting for transfers between devices  48.5 us (28%)
  starting transfers between devices  37 us (21%)
  blocking collectives  20.9 us (12%)
  local copies, waits for them, and re-layouts  2.62 us (2%)
    all_to_all x2, waiting for transfers between devices, exchange(): lax.all_to_all(term.reshape(GROUPS, CHUNK, term.shape[1]), 'piece', 0, 0)  30.4 us
    ppermute x6, starting transfers between devices, along(): return lax.ppermute(block, 'slab', route)  24.3 us
    all_to_all x1, blocking collectives, hand_over(): lax.all_to_all(dense.reshape(GROUPS, 16, dense.shape[1]), 'piece', 0, 0)  20.9 us
    ppermute x6, waiting for transfers between devices, along(): return lax.ppermute(block, 'slab', route)  18.1 us
    pallas_call x2, Pallas kernels, merge(): pl.pallas_call(functools.partial(merge_first_kernel if first else merge_l...  15.1 us
    pallas_call x1, Pallas kernels, third(): pl.pallas_call(third_kernel, out_shape=(shape((W, 7 * W), F32), shape((W,...  14.3 us
    all_to_all x2, starting transfers between devices, exchange(): lax.all_to_all(term.reshape(GROUPS, CHUNK, term.shape[1]), 'piece', 0, 0)  12.7 us
    pallas_call x1, Pallas kernels, near(): pl.pallas_call(near_kernel, grid=(1,), out_shape=(shape((W, 7 * W), F32),...  12.3 us
  transfers between devices with their start and end apart: 8, of which 4 were waited for; matrix products, arithmetic and copies ran while one was open for 0% of the time, Pallas kernels for 27%

profile of v3, /device:TPU:2, one launch (start us, length us, event | category | flops | bytes accessed | tf_op | source)
XLA Modules:
  0.0 170.4 jit_solution(17615369536029825789)
XLA Ops:
  0.6 2.2 %shard_map.95.own = bf16[720,512]{1,0:T(8,128)(2,1)} custom-call(bf16[8,64,512]{2,1,0:T(8,128)(2,1)} %a_ref.1, bf16[8,64,64]{2,1,0:T(8,128)(2,1)} %d_ref.1, bf16[8,64,64]{2,1,0:T(8,128)(2,1)} %q_ref.1, bf16[8,64,64]{2,1,0:T(8,128)(2,1)} %t_ref.1, s32[8,8]{1,0:T(8,128)} %cols_ref.1, s32[8,8]{1,0:T(8,128)} %mask_ref.1, s32[1,8]{1,0:T(1,128)} %bitcast.12, ...), custom_call_target="tpu_custom_call" | custom-call | tf_op jit(solution)/shard_map/pallas_call | solution.py:58
  2.8 3.8 %collective-permute-start.2 = (bf16[720,512]{1,0:T(8,128)(2,1)}, bf16[720,512]{1,0:T(8,128)(2,1)S(1)}, u32[]{:S(2)}, u32[]{:S(2)}) collective-permute-start(bf16[720,512]{1,0:T(8,128)(2,1)} %shard_map.95.own), channel_id=1, source_target_pairs={{0,16},{16,32},{32,48},{48,64},{64,80},{80,96},{96,112},{1,17},{17... | collective-permute-start | bytes 2211848 | tf_op jit(solution)/shard_map/ppermute | solution.py:511
  6.7 4.1 %collective-permute-start = (bf16[720,512]{1,0:T(8,128)(2,1)}, bf16[720,512]{1,0:T(8,128)(2,1)}, u32[]{:S(2)}, u32[]{:S(2)}) collective-permute-start(bf16[720,512]{1,0:T(8,128)(2,1)} %shard_map.95.own), channel_id=1, source_target_pairs={{16,0},{32,16},{48,32},{64,48},{80,64},{96,80},{112,96},{17,1},{33... | collective-permute-start | bytes 2211848 | tf_op jit(solution)/shard_map/ppermute | solution.py:511
  10.8 7.1 %shard_map.96 = (f32[512,1536]{1,0:T(8,128)}, bf16[512,1536]{1,0:T(8,128)(2,1)}, bf16[512,512]{1,0:T(8,128)(2,1)}, bf16[512,512]{1,0:T(8,128)(2,1)}, bf16[512,512]{1,0:T(8,128)(2,1)}) custom-call(bf16[720,512]{1,0:T(8,128)(2,1)} %shard_map.95.own), custom_call_target="tpu_custom_call" | custom-call | flops 3000000000 | bytes 6291456 | tf_op jit(solution)/shard_map/pallas_call | solution.py:184
  17.9 7.6 %collective-permute-done.2.m1 = bf16[720,512]{1,0:T(8,128)(2,1)S(1)} collective-permute-done((bf16[720,512]{1,0:T(8,128)(2,1)}, bf16[720,512]{1,0:T(8,128)(2,1)S(1)}, u32[]{:S(2)}, u32[]{:S(2)}) %collective-permute-start.2) | collective-permute-done | bytes 737312 | tf_op jit(solution)/shard_map/ppermute | solution.py:511
  25.4 1.9 %collective-permute-start.4 = (bf16[720,512]{1,0:T(8,128)(2,1)S(1)}, bf16[720,512]{1,0:T(8,128)(2,1)S(1)}, u32[]{:S(2)}, u32[]{:S(2)}) collective-permute-start(bf16[720,512]{1,0:T(8,128)(2,1)S(1)} %collective-permute-done.2.m1), channel_id=1, source_target_pairs={{0,16},{16,32},{32,48},{48,64},{64,80},{80,96},{96,112},{1,17},{17... | collective-permute-start | bytes 2211848 | tf_op jit(solution)/shard_map/ppermute | solution.py:511
  27.4 6.0 %collective-permute-start.1 = (bf16[720,512]{1,0:T(8,128)(2,1)}, bf16[720,512]{1,0:T(8,128)(2,1)}, u32[]{:S(2)}, u32[]{:S(2)}) collective-permute-start(bf16[720,512]{1,0:T(8,128)(2,1)} %collective-permute-done.p1), channel_id=1, source_target_pairs={{16,0},{32,16},{48,32},{64,48},{80,64},{96,80},{112,96},{17,1},{33... | collective-permute-start | bytes 2211848 | tf_op jit(solution)/shard_map/ppermute | solution.py:511
  33.4 12.3 %shard_map.97 = (f32[512,3584]{1,0:T(8,128)}, bf16[512,1152]{1,0:T(8,128)(2,1)}, f32[512,1024]{1,0:T(8,128)}, bf16[512,2048]{1,0:T(8,128)(2,1)}, bf16[512,1024]{...) custom-call(bf16[720,512]{1,0:T(8,128)(2,1)} %copy-done.2, ...), custom_call_target="tpu_custom_call" | custom-call | flops 8999999488 | bytes 14680064 | tf_op jit(solution)/shard_map/pallas_call | solution.py:251
  45.7 1.2 collective-permute-done.4.m2
  47.0 0.9 copy-done.1
  47.8 6.4 %shard_map.98 = (f32[512,3584]{1,0:T(8,128)}, bf16[512,1152]{1,0:T(8,128)(2,1)}, bf16[512,1024]{1,0:T(8,128)(2,1)}) custom-call(bf16[720,512]{1,0:T(8,128)(2,1)} %copy-done.1, bf16[720,512]{1,0:T(8,128)(2,1)} %copy-done.2, bf16[720,512]{1,0:T(8,128)(2,1)} %shard_map.95.own, ...), custom_call_target="tpu_custom_call", output_to_operand_aliasing={{0}: (6, {}), {1}: (7, {})} | custom-call | flops 4000000000 | bytes 8388608 | tf_op jit(solution)/shard_map/pallas_call | solution.py:325
  54.3 6.7 %all-to-all-start.1 = ((bf16[16,32,1152]{2,1,0:T(8,128)(2,1)}), bf16[16,32,1152]{2,1,0:T(8,128)(2,1)S(1)}, u32[]{:S(2)}, u32[]{:S(2)}) async-start(bf16[16,32,1152]{2,1,0:T(8,128)(2,1)} %bitcast.8), calls=%async_computation.1 | async-start | bytes 2359296 | tf_op jit(solution)/shard_map/all_to_all | solution.py:515
  61.0 1.9 %collective-permute-start.3 = (bf16[144,512]{1,0:T(8,128)(2,1)S(1)}, bf16[144,512]{1,0:T(8,128)(2,1)S(1)}, u32[]{:S(2)}, u32[]{:S(2)}) collective-permute-start(bf16[144,512]{1,0:T(8,128)(2,1)S(1)} %copy-done.4), channel_id=1, source_target_pairs={{0,32},{16,48},{32,64},{48,80},{64,96},{80,112},{1,33},{17,49},{33... | collective-permute-start | bytes 442376 | tf_op jit(solution)/shard_map/ppermute | solution.py:511
  63.0 6.5 %collective-permute-start.5 = (bf16[144,512]{1,0:T(8,128)(2,1)S(1)}, bf16[144,512]{1,0:T(8,128)(2,1)S(1)}, u32[]{:S(2)}, u32[]{:S(2)}) collective-permute-start(bf16[144,512]{1,0:T(8,128)(2,1)S(1)} %copy-done.3), channel_id=1, source_target_pairs={{32,0},{48,16},{64,32},{80,48},{96,64},{112,80},{33,1},{49,17},{65... | collective-permute-start | bytes 442376 | tf_op jit(solution)/shard_map/ppermute | solution.py:511
  69.5 9.3 %collective-permute-done.3.m3 = bf16[144,512]{1,0:T(8,128)(2,1)S(1)} collective-permute-done((bf16[144,512]{1,0:T(8,128)(2,1)S(1)}, bf16[144,512]{1,0:T(8,128)(2,1)S(1)}, u32[]{:S(2)}, u32[]{:S(2)}) %collective-permute-start.3) | collective-permute-done | bytes 147488 | tf_op jit(solution)/shard_map/ppermute | solution.py:511
  78.8 0.7 copy-done.5
  79.5 14.3 %shard_map.99 = (f32[512,3584]{1,0:T(8,128)}, bf16[512,2688]{1,0:T(8,128)(2,1)}) custom-call(bf16[720,512]{1,0:T(8,128)(2,1)} %collective-permute-done.1.p2, bf16[720,512]{1,0:T(8,128)(2,1)} %collective-permute-done.p1, bf16[144,512]{1,0:T(8,128)(2,1)} %copy-done.5, bf16[720,512]{1,0:T(8,128)(2,1)} %copy-done.1, ...), custom_call_target="tpu_custom_call", output_to_operand_aliasing={{0}: (11, {})} | custom-call | flops 7000000000 | bytes 18874368 | tf_op jit(solution)/shard_map/pallas_call | solution.py:384
  93.9 1.0 copy-done
  94.9 6.0 %all-to-all-start = ((bf16[16,32,2688]{2,1,0:T(8,128)(2,1)}), bf16[16,32,2688]{2,1,0:T(8,128)(2,1)}, u32[]{:S(2)}, u32[]{:S(2)}) async-start(bf16[16,32,2688]{2,1,0:T(8,128)(2,1)} %bitcast.10), calls=%async_computation | async-start | bytes 5505024 | tf_op jit(solution)/shard_map/all_to_all | solution.py:515
  100.9 6.0 %shard_map.100 = (bf16[256,512]{1,0:T(8,128)(2,1)}, bf16[4,256,512]{2,1,0:T(8,128)(2,1)}) custom-call(bf16[16,32,1152]{2,1,0:T(8,128)(2,1)} %copy-done), custom_call_target="tpu_custom_call" | custom-call | flops 2000000000 | bytes 2097152 | tf_op jit(solution)/shard_map/pallas_call | solution.py:470
  106.8 30.4 %all-to-all-done.x_ref = bf16[16,32,2688]{2,1,0:T(8,128)(2,1)} async-done(((bf16[16,32,2688]{2,1,0:T(8,128)(2,1)}), bf16[16,32,2688]{2,1,0:T(8,128)(2,1)}, u32[]{:S(2)}, u32[]{:S(2)}) %all-to-all-start) | async-done | bytes 2752544 | tf_op jit(solution)/shard_map/all_to_all | solution.py:515
  137.2 9.1 %shard_map.101 = bf16[256,1792]{1,0:T(8,128)(2,1)} custom-call(bf16[16,32,2688]{2,1,0:T(8,128)(2,1)} %all-to-all-done.x_ref, bf16[256,512]{1,0:T(8,128)(2,1)} %get-tuple-element.38.done, bf16[4,256,512]{2,1,0:T(8,128)(2,1)} %get-tuple-element.39.takes), custom_call_target="tpu_custom_call" | custom-call | flops 5000000000 | bytes 5242880 | tf_op jit(solution)/shard_map/pallas_call | solution.py:470
  146.4 20.9 %all_to_all.15 = bf16[16,16,1792]{2,1,0:T(8,128)(2,1)} all-to-all(bf16[16,16,1792]{2,1,0:T(8,128)(2,1)} %bitcast.11), channel_id=1, replica_groups=mesh['slab'=8,'piece'=16] {'piece'}, dimensions={0} | all-to-all | bytes 1835008 | tf_op jit(solution)/shard_map/all_to_all | solution.py:519
  167.2 3.2 %shard_map.102 = f32[1,64,7168]{2,1,0:T(8,128)} custom-call(bf16[256,1792]{1,0:T(8,128)(2,1)} %bitcast.9), custom_call_target="tpu_custom_call" | custom-call | tf_op jit(solution)/shard_map/pallas_call | solution.py:499
  (15 shorter events, 0.1 us)
Async XLA Ops:
  2.8 22.6 %collective-permute-start.2 = (bf16[720,512]{1,0:T(8,128)(2,1)}, bf16[720,512]{1,0:T(8,128)(2,1)S(1)}, u32[]{:S(2)}, u32[]{:S(2)}) collective-permute-start(bf16[720,512]{1,0:T(8,128)(2,1)} %shard_map.95.own), channel_id=1, source_target_pairs={{0,16},{16,32},{32,48},{48,64},{64,80},{80,96},{96,112},{1,17},{17... | collective-permute-start | bytes 2211848 | tf_op jit(solution)/shard_map/ppermute | solution.py:511
  6.7 20.7 %collective-permute-start = (bf16[720,512]{1,0:T(8,128)(2,1)}, bf16[720,512]{1,0:T(8,128)(2,1)}, u32[]{:S(2)}, u32[]{:S(2)}) collective-permute-start(bf16[720,512]{1,0:T(8,128)(2,1)} %shard_map.95.own), channel_id=1, source_target_pairs={{16,0},{32,16},{48,32},{64,48},{80,64},{96,80},{112,96},{17,1},{33... | collective-permute-start | bytes 2211848 | tf_op jit(solution)/shard_map/ppermute | solution.py:511
  25.4 8.0 %copy-start.2 = (bf16[720,512]{1,0:T(8,128)(2,1)}, bf16[720,512]{1,0:T(8,128)(2,1)S(1)}, u32[]{:S(2)}) copy-start(bf16[720,512]{1,0:T(8,128)(2,1)S(1)} %collective-permute-done.2.m1) | copy-start | bytes 2211844
  25.4 21.5 %collective-permute-start.4 = (bf16[720,512]{1,0:T(8,128)(2,1)S(1)}, bf16[720,512]{1,0:T(8,128)(2,1)S(1)}, u32[]{:S(2)}, u32[]{:S(2)}) collective-permute-start(bf16[720,512]{1,0:T(8,128)(2,1)S(1)} %collective-permute-done.2.m1), channel_id=1, source_target_pairs={{0,16},{16,32},{32,48},{48,64},{64,80},{80,96},{96,112},{1,17},{17... | collective-permute-start | bytes 2211848 | tf_op jit(solution)/shard_map/ppermute | solution.py:511
  27.4 51.4 %collective-permute-start.1 = (bf16[720,512]{1,0:T(8,128)(2,1)}, bf16[720,512]{1,0:T(8,128)(2,1)}, u32[]{:S(2)}, u32[]{:S(2)}) collective-permute-start(bf16[720,512]{1,0:T(8,128)(2,1)} %collective-permute-done.p1), channel_id=1, source_target_pairs={{16,0},{32,16},{48,32},{64,48},{80,64},{96,80},{112,96},{17,1},{33... | collective-permute-start | bytes 2211848 | tf_op jit(solution)/shard_map/ppermute | solution.py:511
  47.0 0.9 copy-start.1
  54.3 6.7 %copy-start.4 = (bf16[144,512]{1,0:T(8,128)(2,1)S(1)}, bf16[144,512]{1,0:T(8,128)(2,1)}, u32[]{:S(2)}) copy-start(bf16[144,512]{1,0:T(8,128)(2,1)} %get-tuple-element.26) | copy-start | bytes 442372
  54.3 8.7 %copy-start.3 = (bf16[144,512]{1,0:T(8,128)(2,1)S(1)}, bf16[144,512]{1,0:T(8,128)(2,1)}, u32[]{:S(2)}) copy-start(bf16[144,512]{1,0:T(8,128)(2,1)} %get-tuple-element.27) | copy-start | bytes 442372
  54.3 39.6 %all-to-all-start.1 = ((bf16[16,32,1152]{2,1,0:T(8,128)(2,1)}), bf16[16,32,1152]{2,1,0:T(8,128)(2,1)S(1)}, u32[]{:S(2)}, u32[]{:S(2)}) async-start(bf16[16,32,1152]{2,1,0:T(8,128)(2,1)} %bitcast.8), calls=%async_computation.1 | async-start | bytes 2359296 | tf_op jit(solution)/shard_map/all_to_all | solution.py:515
  61.0 17.7 %collective-permute-start.3 = (bf16[144,512]{1,0:T(8,128)(2,1)S(1)}, bf16[144,512]{1,0:T(8,128)(2,1)S(1)}, u32[]{:S(2)}, u32[]{:S(2)}) collective-permute-start(bf16[144,512]{1,0:T(8,128)(2,1)S(1)} %copy-done.4), channel_id=1, source_target_pairs={{0,32},{16,48},{32,64},{48,80},{64,96},{80,112},{1,33},{17,49},{33... | collective-permute-start | bytes 442376 | tf_op jit(solution)/shard_map/ppermute | solution.py:511
  63.0 15.8 %collective-permute-start.5 = (bf16[144,512]{1,0:T(8,128)(2,1)S(1)}, bf16[144,512]{1,0:T(8,128)(2,1)S(1)}, u32[]{:S(2)}, u32[]{:S(2)}) collective-permute-start(bf16[144,512]{1,0:T(8,128)(2,1)S(1)} %copy-done.3), channel_id=1, source_target_pairs={{32,0},{48,16},{64,32},{80,48},{96,64},{112,80},{33,1},{49,17},{65... | collective-permute-start | bytes 442376 | tf_op jit(solution)/shard_map/ppermute | solution.py:511
  78.8 0.7 copy-start.5
  78.8 0.7 copy-start.6
  93.9 1.0 copy-start
  94.9 42.3 %all-to-all-start = ((bf16[16,32,2688]{2,1,0:T(8,128)(2,1)}), bf16[16,32,2688]{2,1,0:T(8,128)(2,1)}, u32[]{:S(2)}, u32[]{:S(2)}) async-start(bf16[16,32,2688]{2,1,0:T(8,128)(2,1)} %bitcast.10), calls=%async_computation | async-start | bytes 5505024 | tf_op jit(solution)/shard_map/all_to_all | solution.py:515

commit v4 on v3

--- a/solution.py
+++ b/solution.py
@@ -18,6 +18,7 @@
 ROW_D, ROW_Q, ROW_T, ROW_META, ROWS = W, W + 64, W + 128, W + 192, W + 208
 ANY = pl.BlockSpec(memory_space=pl.ANY)
 VMEM = pl.BlockSpec(memory_space=pltpu.VMEM)
+SMEM = pl.BlockSpec(memory_space=pltpu.SMEM)
 BF16, F32, I32 = jnp.bfloat16, jnp.float32, jnp.int32
 GROUPS = 16
 PART = 4
@@ -103,7 +104,12 @@
     to_scalars([(meta_v.at[n], meta_s.at[n]) for n in range(len(tails))], sem)
 
 
-def place_q(out, ref, top, meta_s, n):
+def inside(slab, step, slabs):
+    at = slab[0] + step
+    return (at >= 0) & (at < slabs)
+
+
+def place_q(out, ref, top, meta_s, n, valid=None):
     out[...] = jnp.zeros((W, W), BF16)
     for w in range(N // 2):
         sides = halves(ref[top:top + TILE, w * LANES:(w + 1) * LANES])
@@ -111,6 +117,10 @@
             c = 2 * w + h
             g = meta_s[n, 8, c]
             out[c * TILE:(c + 1) * TILE, window(g)] = pick(sides[h], g)
+    if valid is not None:
+        @pl.when(jnp.logical_not(valid))
+        def _():
+            out[...] = jnp.zeros((W, W), BF16)
 
 
 def pair_diagonal(pair):
@@ -119,7 +129,7 @@
     return jnp.concatenate([jnp.where(high, zero, pair), jnp.where(high, pair, zero)], axis=0)
 
 
-def place_a(refs, outs, sms, meta_s, metas):
+def place_a(refs, outs, sms, meta_s, metas, valids=None):
     def place_row(i, carry):
         rows = pl.ds(pl.multiple_of(i * TILE, TILE), TILE)
         for out in outs:
@@ -129,6 +139,8 @@
             for h in range(2):
                 for out, side, n in zip(outs, sides, metas):
                     c = meta_s[n, i, 2 * w + h]
+                    if valids is not None:
+                        c = jnp.where(valids[n], c, TRASH)
                     out[rows, window(c)] = out[rows, window(c)] + pick(side[h], c)
         return carry
 
@@ -207,14 +219,24 @@
     return copies
 
 
-def near_kernel(m1, p1, rap_h, sm_h, qs_h, r0_h, tpt_h, own, c_ref, term_ref, part, ra_out, smo, m1_tail, p1_tail,
-                ad0, ad2, sm0, sm1, sm2, qs0, qs1, qs2, rm, r0, rp, tpt, rap, ra, cbuf, tbuf,
+def near_kernel(slabs, slab, m1, p1, rap_h, sm_h, qs_h, r0_h, tpt_h, own,
+                c_ref, term_ref, part_h, ra_h, smo_h, m1_tail, p1_tail,
+                ad0, ad2, sm0, sm1, sm2, qs1, rm, r0, rp, tpt, rap, ra, part, cbuf, tbuf,
                 meta_v, meta_s, sem, in_sem, out_sem):
     ins = fetch(((qs_h, qs1), (rap_h, rap), (r0_h, r0), (tpt_h, tpt), (sm_h, sm1)), in_sem)
-    m1_tail[...] = m1[ROW_Q:ROWS, :]
-    p1_tail[...] = p1[ROW_Q:ROWS, :]
+    outs = []
+
+    def send(src, dst):
+        outs.append(pltpu.make_async_copy(src, dst, out_sem.at[len(outs)]))
+        outs[-1].start()
+
+    send(m1.at[ROW_Q:ROWS, :], m1_tail)
+    send(p1.at[ROW_Q:ROWS, :], p1_tail)
     read_meta([(m1, ROW_META), (p1, ROW_META)], meta_v, meta_s, sem)
-    place_a((m1, p1), (ad0, ad2), (sm0, sm2), meta_s, (0, 1))
+    valids = (inside(slab, -1, slabs), inside(slab, 1, slabs))
+    place_a((m1, p1), (ad0, ad2), (sm0, sm2), meta_s, (0, 1), valids)
+    send(sm0.at[:, block(0)], smo_h.at[:, block(0)])
+    send(sm2.at[:, W:3 * W], smo_h.at[:, W:3 * W])
     for copy in ins:
         copy.wait()
 
@@ -226,57 +248,51 @@
     ra[:, block(2)] = (dot(before, ad0[:, block(2)]) + dot(after, ad2[:, block(0)]) + rap[:, block(1)]).astype(BF16)
     ra[:, block(3)] = (dot(after, ad2[:, block(1)]) + rap[:, block(2)]).astype(BF16)
     ra[:, block(4)] = dot(after, ad2[:, block(2)]).astype(BF16)
-    for n, f in enumerate((0, 1, 3, 4)):
-        ra_out[:, block(n)] = ra[:, block(f)]
-    smo[:, block(0)] = sm0[:, block(0)]
-    smo[:, block(1)] = sm2[:, block(2)]
-
+    send(ra, ra_h)
+
+    lead = ra[:, block(1)]
+    part[...] = lead.astype(F32) - dot(lead, sm0[:, block(1)]) - dot(ra[:, block(2)], sm1[:, block(0)])
+    send(part, part_h)
     cbuf[...] = dot(ra[:, block(1)], rm[...]) + dot(ra[:, block(2)], r0[...]) + dot(ra[:, block(3)], rp[...])
-    out = pltpu.make_async_copy(cbuf, c_ref.at[:, block(3)], out_sem.at[0])
-    out.start()
+    send(cbuf, c_ref.at[:, block(3)])
     write_term(tbuf, 0, tpt, cbuf[...], own, TAIL_T)
-    sent = pltpu.make_async_copy(tbuf, term_ref.at[:, block(0)], out_sem.at[1])
-    sent.start()
-
-    for n, (f, sm, g) in enumerate(((1, sm0, 0), (3, sm2, 2))):
-        lead = ra[:, block(f)]
-        known = dot(lead, sm[:, block(1)]) + dot(ra[:, block(2)], sm1[:, block(g)])
-        part[:, block(n)] = lead.astype(F32) - known
-    out.wait()
-    sent.wait()
-
-
-def near(m1, p1, rap, sm, qs, r0, tpt, own):
+    send(tbuf, term_ref.at[:, block(0)])
+    for copy in outs:
+        copy.wait()
+
+
+def near(slab, m1, p1, rap, sm, qs, r0, tpt, own):
     shape = jax.ShapeDtypeStruct
     return pl.pallas_call(
-        near_kernel,
+        functools.partial(near_kernel, lax.axis_size("slab")),
         grid=(1,),
         out_shape=(
-            shape((W, 7 * W), F32), shape((W, 2 * W + LANES), BF16), shape((W, 2 * W), F32),
-            shape((W, 4 * W), BF16), shape((W, 2 * W), BF16), shape((144, W), BF16), shape((144, W), BF16),
+            shape((W, 7 * W), F32), shape((W, 2 * W + LANES), BF16), shape((W, W), F32),
+            shape((W, 5 * W), BF16), shape((W, 3 * W), BF16), shape((144, W), BF16), shape((144, W), BF16),
         ),
-        in_specs=[VMEM, VMEM] + [ANY] * 5 + [TAIL],
-        out_specs=(ANY, ANY) + (VMEM,) * 5,
+        in_specs=[SMEM, VMEM, VMEM] + [ANY] * 5 + [TAIL],
+        out_specs=(ANY,) * 7,
         scratch_shapes=[pltpu.VMEM((W, WIDE), BF16)] * 2
         + [pltpu.VMEM((W, 3 * W), BF16)] * 3
-        + [pltpu.VMEM((W, W), BF16)] * 7
+        + [pltpu.VMEM((W, W), BF16)] * 5
         + [
             pltpu.VMEM((W, 3 * W), F32),
             pltpu.VMEM((W, 5 * W), BF16),
             pltpu.VMEM((W, W), F32),
+            pltpu.VMEM((W, W), F32),
             pltpu.VMEM((W, W), BF16),
             pltpu.VMEM((2, 16, LANES), I32),
             pltpu.SMEM((2, 16, LANES), I32),
             pltpu.SemaphoreType.DMA((2,)),
             pltpu.SemaphoreType.DMA((5,)),
-            pltpu.SemaphoreType.DMA((2,)),
+            pltpu.SemaphoreType.DMA((8,)),
         ],
         compiler_params=params(),
         cost_estimate=pl.CostEstimate(flops=9_000_000_000, bytes_accessed=14 << 20, transcendentals=0),
-    )(m1, p1, rap, sm, qs, r0, tpt, own)
-
-
-def smooth_far(ref, flat, sm, meta_s, n):
+    )(slab, m1, p1, rap, sm, qs, r0, tpt, own)
+
+
+def smooth_far(ref, flat, sm, meta_s, n, valid):
     for w in range(N // 2):
         rows = slice(w * LANES, (w + 1) * LANES)
         diag = pair_diagonal(ref[ROW_D:ROW_D + TILE, rows])
@@ -291,21 +307,21 @@
             sides = [halves(flat[rows, w * LANES:(w + 1) * LANES]) for rows in starts]
             for h in range(2):
                 for d, rows in enumerate(starts):
-                    c = meta_s[n, i + d * N // 2, 2 * w + h]
+                    c = jnp.where(valid, meta_s[n, i + d * N // 2, 2 * w + h], TRASH)
                     sm[rows, window(c)] = sm[rows, window(c)] + pick(sides[d][h], c)
         return carry
 
     lax.fori_loop(0, N // 2, place_row, 0)
 
 
-def second_kernel(m2, m1, own, part_h, ra_h, tpt_h, c_in, term_in, c_ref, term_ref, smm_out,
+def second_kernel(slabs, slab, m2, m1, own, part_h, ra_h, tpt_h, c_in, term_in, c_ref, term_ref, smm_out,
                   flat, smm, qs, pw, part, ra, tpt, cbuf, tbuf, meta_v, meta_s, ids_v, sem, in_sem, out_sem):
     del c_in, term_in
-    ins = fetch(((part_h.at[:, block(0)], part), (ra_h.at[:, block(0)], ra), (tpt_h, tpt)), in_sem)
+    ins = fetch(((part_h, part), (ra_h.at[:, block(0)], ra), (tpt_h, tpt)), in_sem)
     read_meta([(m2, ROW_META), (m1, TAIL_META), (own, TAIL_META)], meta_v, meta_s, sem)
     write_ids(tbuf, 1, ids_v, meta_v, (2, 2, 1))
-    smooth_far(m2, flat, smm, meta_s, 0)
-    place_q(qs, m1, TAIL_Q, meta_s, 1)
+    smooth_far(m2, flat, smm, meta_s, 0, inside(slab, -2, slabs))
+    place_q(qs, m1, TAIL_Q, meta_s, 1, inside(slab, -1, slabs))
     for copy in ins:
         copy.wait()
     pw[...] = (part[...] - dot(ra[...], smm[:, block(2)])).astype(BF16)
@@ -320,15 +336,15 @@
     sent.wait()
 
 
-def second(m2, m1, own, part, ra, tpt, c, term):
+def second(slab, m2, m1, own, part, ra, tpt, c, term):
     shape = jax.ShapeDtypeStruct
     return pl.pallas_call(
-        second_kernel,
+        functools.partial(second_kernel, lax.axis_size("slab")),
         out_shape=(shape((W, 7 * W), F32), shape((W, 2 * W + LANES), BF16), shape((W, 2 * W), BF16)),
         grid=(1,),
-        in_specs=[VMEM, TAIL, TAIL] + [ANY] * 5,
+        in_specs=[SMEM, VMEM, TAIL, TAIL] + [ANY] * 5,
         out_specs=(ANY, ANY, VMEM),
-        input_output_aliases={6: 0, 7: 1},
+        input_output_aliases={7: 0, 8: 1},
         scratch_shapes=[
             pltpu.VMEM((W, W), BF16),
             pltpu.VMEM((W, WIDE), BF16),
@@ -348,30 +364,35 @@
         ],
         compiler_params=params(),
         cost_estimate=pl.CostEstimate(flops=4_000_000_000, bytes_accessed=8 << 20, transcendentals=0),
-    )(m2, m1, own, part, ra, tpt, c, term)
-
-
-def third_kernel(p2, p1, m3, m2, p3, own, part, smm, smo, ra, tpt, c_in, c_ref, term,
-                 flat, smp, qs, pw, cbuf, meta_v, meta_s, ids_v, sem, out_sem):
+    )(slab, m2, m1, own, part, ra, tpt, c, term)
+
+
+def third_kernel(slabs, slab, p2, p1, m3, m2, p3, own, sm_h, smm_h, smo_h, ra_h, tpt_h, c_in, c_ref, term,
+                 flat, smp, qs, pw, cbuf, sm1, smm, smo, ra, tpt, meta_v, meta_s, ids_v, sem, in_sem, out_sem):
     del c_in
+    ins = fetch(((sm_h.at[:, block(2)], sm1), (smm_h, smm), (smo_h, smo), (ra_h, ra), (tpt_h, tpt)), in_sem)
     read_meta([(p2, ROW_META)] + [(ref, TAIL_META) for ref in (p1, m2, m3, p3, own)], meta_v, meta_s, sem)
     write_ids(term, 5, ids_v, meta_v, (5, 1, 2, 0, 3, 4))
-    smooth_far(p2, flat, smp, meta_s, 0)
+    smooth_far(p2, flat, smp, meta_s, 0, inside(slab, 2, slabs))
+    for copy in ins:
+        copy.wait()
     outs = []
 
     def columns(n, value, o, ref, top, at):
         pw[...] = value.astype(BF16)
-        place_q(qs, ref, top, meta_s, at)
+        place_q(qs, ref, top, meta_s, at, inside(slab, o - 3, slabs))
         cbuf[n] = dot(pw[...], qs[...])
         outs.append(pltpu.make_async_copy(cbuf.at[n], c_ref.at[:, block(o)], out_sem.at[n]))
         outs[-1].start()
         write_term(term, n, tpt, cbuf[n], ref, top + TILE)
 
-    first, last = ra[:, block(0)], ra[:, block(3)]
-    columns(0, part[:, block(1)] - dot(last, smp[:, block(0)]), 4, p1, TAIL_Q, 1)
+    first, last = ra[:, block(0)], ra[:, block(4)]
+    near = ra[:, block(3)]
+    value = near.astype(F32) - dot(near, smo[:, block(1)]) - dot(ra[:, block(2)], sm1[...])
+    columns(0, value - dot(last, smp[:, block(0)]), 4, p1, TAIL_Q, 1)
     value = first.astype(F32) - dot(first, smm[:, block(1)]) - dot(ra[:, block(1)], smo[:, block(0)])
     columns(1, value, 1, m2, TAIL_Q, 2)
-    value = last.astype(F32) - dot(last, smp[:, block(1)]) - dot(ra[:, block(2)], smo[:, block(1)])
+    value = last.astype(F32) - dot(last, smp[:, block(1)]) - dot(near, smo[:, block(2)])
     columns(2, value, 5, p2, ROW_Q, 0)
     columns(3, -dot(first, smm[:, block(0)]), 0, m3, TAIL_Q, 3)
     columns(4, -dot(last, smp[:, block(2)]), 6, p3, TAIL_Q, 4)
@@ -379,30 +400,36 @@
         out.wait()
 
 
-def third(p2, p1, m3, m2, p3, own, part, smm, smo, ra, tpt, c):
+def third(slab, p2, p1, m3, m2, p3, own, sm, smm, smo, ra, tpt, c):
     shape = jax.ShapeDtypeStruct
     return pl.pallas_call(
-        third_kernel,
+        functools.partial(third_kernel, lax.axis_size("slab")),
         out_shape=(shape((W, 7 * W), F32), shape((W, 5 * W + LANES), BF16)),
         grid=(1,),
-        in_specs=[VMEM, TAIL, VMEM, TAIL, VMEM, TAIL] + [VMEM] * 5 + [ANY],
+        in_specs=[SMEM, VMEM, TAIL, VMEM, TAIL, VMEM, TAIL] + [ANY] * 6,
         out_specs=(ANY, VMEM),
-        input_output_aliases={11: 0},
+        input_output_aliases={12: 0},
         scratch_shapes=[
             pltpu.VMEM((W, W), BF16),
             pltpu.VMEM((W, WIDE), BF16),
             pltpu.VMEM((W, W), BF16),
             pltpu.VMEM((W, W), BF16),
             pltpu.VMEM((5, W, W), F32),
+            pltpu.VMEM((W, W), BF16),
+            pltpu.VMEM((W, 2 * W), BF16),
+            pltpu.VMEM((W, 3 * W), BF16),
+            pltpu.VMEM((W, 5 * W), BF16),
+            pltpu.VMEM((W, W), BF16),
             pltpu.VMEM((6, 16, LANES), I32),
             pltpu.SMEM((6, 16, LANES), I32),
             pltpu.VMEM((CHUNK, LANES), F32),
             pltpu.SemaphoreType.DMA((6,)),
             pltpu.SemaphoreType.DMA((5,)),
+            pltpu.SemaphoreType.DMA((5,)),
         ],
         compiler_params=params(),
         cost_estimate=pl.CostEstimate(flops=7_000_000_000, bytes_accessed=18 << 20, transcendentals=0),
-    )(p2, p1, m3, m2, p3, own, part, smm, smo, ra, tpt, c)
+    )(slab, p2, p1, m3, m2, p3, own, sm, smm, smo, ra, tpt, c)
 
 
 def gather_pieces(count, x_ref, lows, highs, ids_v, ids_s, sem):
@@ -507,7 +534,7 @@
 
 def along(block, step):
     count = lax.axis_size("slab")
-    route = [(i, i + step) for i in range(count) if 0 <= i + step < count]
+    route = [(i, (i + step) % count) for i in range(count)]
     return lax.ppermute(block, "slab", route)
 
 
@@ -523,15 +550,16 @@
 def device_part(fine_tiles, fine_cols, bond_mask, diag_inv, tentative, aggregate, tentative_two, aggregate_two):
     own = pack(fine_tiles, diag_inv, tentative, tentative_two, fine_cols, bond_mask, aggregate, aggregate_two)
     m1, p1 = along(own, 1), along(own, -1)
+    slab = lax.axis_index("slab").astype(I32).reshape(1)
     rap, sm, qs, r0, tpt = start_own(own)
     m2 = along(m1, 1)
     p2 = along(p1, -1)
-    c, term, part, ra, smo, m1_tail, p1_tail = near(m1, p1, rap, sm, qs, r0, tpt, own)
+    c, term, part, ra, smo, m1_tail, p1_tail = near(slab, m1, p1, rap, sm, qs, r0, tpt, own)
     m3 = along(m1_tail, 2)
     p3 = along(p1_tail, -2)
-    c, term, smm = second(m2, m1, own, part, ra, tpt, c, term)
+    c, term, smm = second(slab, m2, m1, own, part, ra, tpt, c, term)
     got = exchange(term)
-    c, term = third(p2, p1, m3, m2, p3, own, part, smm, smo, ra, tpt, c)
+    c, term = third(slab, p2, p1, m3, m2, p3, own, sm, smm, smo, ra, tpt, c)
     last = exchange(term)
     done, takes = merge(got)
     level_two = finish(((3, 2, 4, 1, 5, 0, 6),), hand_over(merge(last, done, takes)))

time: 173 us -> 169 us (0.977)
  starting transfers between devices: 37 us -> 25.3 us
  waiting for transfers between devices: 48.5 us -> 58.5 us
  Pallas kernels: 60.6 us -> 58.2 us
    ppermute x6, starting transfers between devices: 24.3 us -> 12.8 us  [along(): return lax.ppermute(block, 'slab', route)]
    ppermute x6, waiting for transfers between devices: 18.1 us -> 28.1 us  [along(): return lax.ppermute(block, 'slab', route)]
    pallas_call x3, Pallas kernels: 33.1 us -> 30.7 us  [the longest x1 14 us: third(): pl.pallas_call(functools.partial(third_kernel, lax.axis_size('slab')), ou...]
  transfers between devices with their start and end apart: 8 -> 8, of which waited for: 4 -> 4; matrix products, arithmetic and copies ran while one was open for 0% -> 0% of each run, Pallas kernels for 27% -> 26%
where the time goes in v4:
time: 169 us; the launch traced here: 166 us
  waiting for transfers between devices  58.5 us (35%)
  Pallas kernels  58.2 us (34%)
  starting transfers between devices  25.3 us (15%)
  blocking collectives  20.9 us (12%)
  local copies, waits for them, and re-layouts  2.65 us (2%)
    all_to_all x2, waiting for transfers between devices, exchange(): lax.all_to_all(term.reshape(GROUPS, CHUNK, term.shape[1]), 'piece', 0, 0)  30.4 us
    ppermute x6, waiting for transfers between devices, along(): return lax.ppermute(block, 'slab', route)  28.1 us
    all_to_all x1, blocking collectives, hand_over(): lax.all_to_all(dense.reshape(GROUPS, 16, dense.shape[1]), 'piece', 0, 0)  20.9 us
    pallas_call x2, Pallas kernels, merge(): pl.pallas_call(functools.partial(merge_first_kernel if first else merge_l...  15.1 us
    pallas_call x1, Pallas kernels, third(): pl.pallas_call(functools.partial(third_kernel, lax.axis_size('slab')), ou...  14 us
    ppermute x6, starting transfers between devices, along(): return lax.ppermute(block, 'slab', route)  12.8 us
    all_to_all x2, starting transfers between devices, exchange(): lax.all_to_all(term.reshape(GROUPS, CHUNK, term.shape[1]), 'piece', 0, 0)  12.5 us
    pallas_call x1, Pallas kernels, near(): pl.pallas_call(functools.partial(near_kernel, lax.axis_size('slab')), gri...  10.1 us
  transfers between devices with their start and end apart: 8, of which 4 were waited for; matrix products, arithmetic and copies ran while one was open for 0% of the time, Pallas kernels for 26%

profile of v4, /device:TPU:2, one launch (start us, length us, event | category | flops | bytes accessed | tf_op | source)
XLA Modules:
  0.0 166.3 jit_solution(2420385547340024785)
XLA Ops:
  0.6 2.2 %shard_map.95.own = bf16[720,512]{1,0:T(8,128)(2,1)} custom-call(bf16[8,64,512]{2,1,0:T(8,128)(2,1)} %a_ref.1, bf16[8,64,64]{2,1,0:T(8,128)(2,1)} %d_ref.1, bf16[8,64,64]{2,1,0:T(8,128)(2,1)} %q_ref.1, bf16[8,64,64]{2,1,0:T(8,128)(2,1)} %t_ref.1, s32[8,8]{1,0:T(8,128)} %cols_ref.1, s32[8,8]{1,0:T(8,128)} %mask_ref.1, s32[1,8]{1,0:T(1,128)} %bitcast.13, ...), custom_call_target="tpu_custom_call" | custom-call | tf_op jit(solution)/shard_map/pallas_call | solution.py:59
  2.8 1.9 %collective-permute-start.2 = (bf16[720,512]{1,0:T(8,128)(2,1)}, bf16[720,512]{1,0:T(8,128)(2,1)S(1)}, u32[]{:S(2)}, u32[]{:S(2)}) collective-permute-start(bf16[720,512]{1,0:T(8,128)(2,1)} %shard_map.95.own), channel_id=1, source_target_pairs={{0,16},{16,32},{32,48},{48,64},{64,80},{80,96},{96,112},{112,0},{1... | collective-permute-start | bytes 2211848 | tf_op jit(solution)/shard_map/ppermute | solution.py:538
  4.8 2.2 %collective-permute-start = (bf16[720,512]{1,0:T(8,128)(2,1)}, bf16[720,512]{1,0:T(8,128)(2,1)}, u32[]{:S(2)}, u32[]{:S(2)}) collective-permute-start(bf16[720,512]{1,0:T(8,128)(2,1)} %shard_map.95.own), channel_id=1, source_target_pairs={{0,112},{16,0},{32,16},{48,32},{64,48},{80,64},{96,80},{112,96},{1... | collective-permute-start | bytes 2211848 | tf_op jit(solution)/shard_map/ppermute | solution.py:538
  7.0 7.1 %shard_map.96 = (f32[512,1536]{1,0:T(8,128)}, bf16[512,1536]{1,0:T(8,128)(2,1)}, bf16[512,512]{1,0:T(8,128)(2,1)}, bf16[512,512]{1,0:T(8,128)(2,1)}, bf16[512,512]{1,0:T(8,128)(2,1)}) custom-call(bf16[720,512]{1,0:T(8,128)(2,1)} %shard_map.95.own), custom_call_target="tpu_custom_call" | custom-call | flops 3000000000 | bytes 6291456 | tf_op jit(solution)/shard_map/pallas_call | solution.py:196
  14.1 9.4 %collective-permute-done.2.m1 = bf16[720,512]{1,0:T(8,128)(2,1)S(1)} collective-permute-done((bf16[720,512]{1,0:T(8,128)(2,1)}, bf16[720,512]{1,0:T(8,128)(2,1)S(1)}, u32[]{:S(2)}, u32[]{:S(2)}) %collective-permute-start.2) | collective-permute-done | bytes 737312 | tf_op jit(solution)/shard_map/ppermute | solution.py:538
  23.6 4.1 %collective-permute-start.1 = (bf16[720,512]{1,0:T(8,128)(2,1)}, bf16[720,512]{1,0:T(8,128)(2,1)}, u32[]{:S(2)}, u32[]{:S(2)}) collective-permute-start(bf16[720,512]{1,0:T(8,128)(2,1)} %collective-permute-done.p1), channel_id=1, source_target_pairs={{0,112},{16,0},{32,16},{48,32},{64,48},{80,64},{96,80},{112,96},{1... | collective-permute-start | bytes 2211848 | tf_op jit(solution)/shard_map/ppermute | solution.py:538
  27.7 10.1 %shard_map.97 = (f32[512,3584]{1,0:T(8,128)}, bf16[512,1152]{1,0:T(8,128)(2,1)}, f32[512,512]{1,0:T(8,128)}, bf16[512,2560]{1,0:T(8,128)(2,1)}, bf16[512,1536]{1...) custom-call(s32[1]{0:T(128)} %bitcast.slab, bf16[720,512]{1,0:T(8,128)(2,1)} %copy-done.2, ...), custom_call_target="tpu_custom_call" | custom-call | flops 8999999488 | bytes 14680064 | tf_op jit(solution)/shard_map/pallas_call | solution.py:266
  37.8 5.4 %collective-permute-done.4.m2 = bf16[720,512]{1,0:T(8,128)(2,1)S(1)} collective-permute-done((bf16[720,512]{1,0:T(8,128)(2,1)S(1)}, bf16[720,512]{1,0:T(8,128)(2,1)S(1)}, u32[]{:S(2)}, u32[]{:S(2)}) %collective-permute-start.4) | collective-permute-done | bytes 737312 | tf_op jit(solution)/shard_map/ppermute | solution.py:538
  43.2 0.9 copy-done.1
  44.1 6.6 %shard_map.98 = (f32[512,3584]{1,0:T(8,128)}, bf16[512,1152]{1,0:T(8,128)(2,1)}, bf16[512,1024]{1,0:T(8,128)(2,1)}) custom-call(s32[1]{0:T(128)} %bitcast.slab, bf16[720,512]{1,0:T(8,128)(2,1)} %copy-done.1, bf16[720,512]{1,0:T(8,128)(2,1)} %copy-done.2, bf16[720,512]{1,0:T(8,128)(2,1)} %shard_map.95.own, ...), custom_call_target="tpu_custom_call", output_to_operand_aliasing={{0}: (7, {}), {1}: (8, {})} | custom-call | flops 4000000000 | bytes 8388608 | tf_op jit(solution)/shard_map/pallas_call | solution.py:341
  50.7 6.6 %all-to-all-start.1 = ((bf16[16,32,1152]{2,1,0:T(8,128)(2,1)}), bf16[16,32,1152]{2,1,0:T(8,128)(2,1)S(1)}, u32[]{:S(2)}, u32[]{:S(2)}) async-start(bf16[16,32,1152]{2,1,0:T(8,128)(2,1)} %bitcast.9), calls=%async_computation.1 | async-start | bytes 2359296 | tf_op jit(solution)/shard_map/all_to_all | solution.py:542
  57.3 0.1 collective-permute-start.3
  57.3 4.4 %collective-permute-start.5 = (bf16[144,512]{1,0:T(8,128)(2,1)S(1)}, bf16[144,512]{1,0:T(8,128)(2,1)S(1)}, u32[]{:S(2)}, u32[]{:S(2)}) collective-permute-start(bf16[144,512]{1,0:T(8,128)(2,1)S(1)} %copy-done.3), channel_id=1, source_target_pairs={{0,96},{16,112},{32,0},{48,16},{64,32},{80,48},{96,64},{112,80},{1... | collective-permute-start | bytes 442376 | tf_op jit(solution)/shard_map/ppermute | solution.py:538
  61.8 13.3 %collective-permute-done.3.m3 = bf16[144,512]{1,0:T(8,128)(2,1)S(1)} collective-permute-done((bf16[144,512]{1,0:T(8,128)(2,1)S(1)}, bf16[144,512]{1,0:T(8,128)(2,1)S(1)}, u32[]{:S(2)}, u32[]{:S(2)}) %collective-permute-start.3) | collective-permute-done | bytes 147488 | tf_op jit(solution)/shard_map/ppermute | solution.py:538
  75.0 0.7 copy-done.5
  75.7 0.1 copy-done.6
  75.8 14.0 %shard_map.99 = (f32[512,3584]{1,0:T(8,128)}, bf16[512,2688]{1,0:T(8,128)(2,1)}) custom-call(s32[1]{0:T(128)} %bitcast.slab, bf16[720,512]{1,0:T(8,128)(2,1)} %collective-permute-done.1.p2, bf16[720,512]{1,0:T(8,128)(2,1)} %collective-permute-done.p1, bf16[144,512]{1,0:T(8,128)(2,1)} %copy-done.5, ...), custom_call_target="tpu_custom_call", output_to_operand_aliasing={{0}: (12, {})} | custom-call | flops 7000000000 | bytes 18874368 | tf_op jit(solution)/shard_map/pallas_call | solution.py:405
  89.8 1.0 copy-done
  90.8 6.0 %all-to-all-start = ((bf16[16,32,2688]{2,1,0:T(8,128)(2,1)}), bf16[16,32,2688]{2,1,0:T(8,128)(2,1)}, u32[]{:S(2)}, u32[]{:S(2)}) async-start(bf16[16,32,2688]{2,1,0:T(8,128)(2,1)} %bitcast.11), calls=%async_computation | async-start | bytes 5505024 | tf_op jit(solution)/shard_map/all_to_all | solution.py:542
  96.8 6.0 %shard_map.100 = (bf16[256,512]{1,0:T(8,128)(2,1)}, bf16[4,256,512]{2,1,0:T(8,128)(2,1)}) custom-call(bf16[16,32,1152]{2,1,0:T(8,128)(2,1)} %copy-done), custom_call_target="tpu_custom_call" | custom-call | flops 2000000000 | bytes 2097152 | tf_op jit(solution)/shard_map/pallas_call | solution.py:497
  102.8 30.4 %all-to-all-done.x_ref = bf16[16,32,2688]{2,1,0:T(8,128)(2,1)} async-done(((bf16[16,32,2688]{2,1,0:T(8,128)(2,1)}), bf16[16,32,2688]{2,1,0:T(8,128)(2,1)}, u32[]{:S(2)}, u32[]{:S(2)}) %all-to-all-start) | async-done | bytes 2752544 | tf_op jit(solution)/shard_map/all_to_all | solution.py:542
  133.2 9.1 %shard_map.101 = bf16[256,1792]{1,0:T(8,128)(2,1)} custom-call(bf16[16,32,2688]{2,1,0:T(8,128)(2,1)} %all-to-all-done.x_ref, bf16[256,512]{1,0:T(8,128)(2,1)} %get-tuple-element.38.done, bf16[4,256,512]{2,1,0:T(8,128)(2,1)} %get-tuple-element.39.takes), custom_call_target="tpu_custom_call" | custom-call | flops 5000000000 | bytes 5242880 | tf_op jit(solution)/shard_map/pallas_call | solution.py:497
  142.3 20.9 %all_to_all.15 = bf16[16,16,1792]{2,1,0:T(8,128)(2,1)} all-to-all(bf16[16,16,1792]{2,1,0:T(8,128)(2,1)} %bitcast.12), channel_id=1, replica_groups=mesh['slab'=8,'piece'=16] {'piece'}, dimensions={0} | all-to-all | bytes 1835008 | tf_op jit(solution)/shard_map/all_to_all | solution.py:546
  163.2 3.2 %shard_map.102 = f32[1,64,7168]{2,1,0:T(8,128)} custom-call(bf16[256,1792]{1,0:T(8,128)(2,1)} %bitcast.10), custom_call_target="tpu_custom_call" | custom-call | tf_op jit(solution)/shard_map/pallas_call | solution.py:526
  (15 shorter events, 0.0 us)
Async XLA Ops:
  2.8 20.7 %collective-permute-start.2 = (bf16[720,512]{1,0:T(8,128)(2,1)}, bf16[720,512]{1,0:T(8,128)(2,1)S(1)}, u32[]{:S(2)}, u32[]{:S(2)}) collective-permute-start(bf16[720,512]{1,0:T(8,128)(2,1)} %shard_map.95.own), channel_id=1, source_target_pairs={{0,16},{16,32},{32,48},{48,64},{64,80},{80,96},{96,112},{112,0},{1... | collective-permute-start | bytes 2211848 | tf_op jit(solution)/shard_map/ppermute | solution.py:538
  4.8 18.8 %collective-permute-start = (bf16[720,512]{1,0:T(8,128)(2,1)}, bf16[720,512]{1,0:T(8,128)(2,1)}, u32[]{:S(2)}, u32[]{:S(2)}) collective-permute-start(bf16[720,512]{1,0:T(8,128)(2,1)} %shard_map.95.own), channel_id=1, source_target_pairs={{0,112},{16,0},{32,16},{48,32},{64,48},{80,64},{96,80},{112,96},{1... | collective-permute-start | bytes 2211848 | tf_op jit(solution)/shard_map/ppermute | solution.py:538
  23.6 4.1 %copy-start.2 = (bf16[720,512]{1,0:T(8,128)(2,1)}, bf16[720,512]{1,0:T(8,128)(2,1)S(1)}, u32[]{:S(2)}) copy-start(bf16[720,512]{1,0:T(8,128)(2,1)S(1)} %collective-permute-done.2.m1) | copy-start | bytes 2211844
  23.6 19.6 %collective-permute-start.4 = (bf16[720,512]{1,0:T(8,128)(2,1)S(1)}, bf16[720,512]{1,0:T(8,128)(2,1)S(1)}, u32[]{:S(2)}, u32[]{:S(2)}) collective-permute-start(bf16[720,512]{1,0:T(8,128)(2,1)S(1)} %collective-permute-done.2.m1), channel_id=1, source_target_pairs={{0,16},{16,32},{32,48},{48,64},{64,80},{80,96},{96,112},{112,0},{1... | collective-permute-start | bytes 2211848 | tf_op jit(solution)/shard_map/ppermute | solution.py:538
  23.6 51.5 %collective-permute-start.1 = (bf16[720,512]{1,0:T(8,128)(2,1)}, bf16[720,512]{1,0:T(8,128)(2,1)}, u32[]{:S(2)}, u32[]{:S(2)}) collective-permute-start(bf16[720,512]{1,0:T(8,128)(2,1)} %collective-permute-done.p1), channel_id=1, source_target_pairs={{0,112},{16,0},{32,16},{48,32},{64,48},{80,64},{96,80},{112,96},{1... | collective-permute-start | bytes 2211848 | tf_op jit(solution)/shard_map/ppermute | solution.py:538
  43.2 0.9 copy-start.1
  44.1 13.2 %copy-start.4 = (bf16[144,512]{1,0:T(8,128)(2,1)S(1)}, bf16[144,512]{1,0:T(8,128)(2,1)}, u32[]{:S(2)}) copy-start(bf16[144,512]{1,0:T(8,128)(2,1)} %get-tuple-element.26) | copy-start | bytes 442372
  44.1 13.2 %copy-start.3 = (bf16[144,512]{1,0:T(8,128)(2,1)S(1)}, bf16[144,512]{1,0:T(8,128)(2,1)}, u32[]{:S(2)}) copy-start(bf16[144,512]{1,0:T(8,128)(2,1)} %get-tuple-element.27) | copy-start | bytes 442372
  50.7 39.1 %all-to-all-start.1 = ((bf16[16,32,1152]{2,1,0:T(8,128)(2,1)}), bf16[16,32,1152]{2,1,0:T(8,128)(2,1)S(1)}, u32[]{:S(2)}, u32[]{:S(2)}) async-start(bf16[16,32,1152]{2,1,0:T(8,128)(2,1)} %bitcast.9), calls=%async_computation.1 | async-start | bytes 2359296 | tf_op jit(solution)/shard_map/all_to_all | solution.py:542
  57.3 17.8 %collective-permute-start.3 = (bf16[144,512]{1,0:T(8,128)(2,1)S(1)}, bf16[144,512]{1,0:T(8,128)(2,1)S(1)}, u32[]{:S(2)}, u32[]{:S(2)}) collective-permute-start(bf16[144,512]{1,0:T(8,128)(2,1)S(1)} %copy-done.4), channel_id=1, source_target_pairs={{0,32},{16,48},{32,64},{48,80},{64,96},{80,112},{96,0},{112,16},{1... | collective-permute-start | bytes 442376 | tf_op jit(solution)/shard_map/ppermute | solution.py:538
  57.3 17.7 %collective-permute-start.5 = (bf16[144,512]{1,0:T(8,128)(2,1)S(1)}, bf16[144,512]{1,0:T(8,128)(2,1)S(1)}, u32[]{:S(2)}, u32[]{:S(2)}) collective-permute-start(bf16[144,512]{1,0:T(8,128)(2,1)S(1)} %copy-done.3), channel_id=1, source_target_pairs={{0,96},{16,112},{32,0},{48,16},{64,32},{80,48},{96,64},{112,80},{1... | collective-permute-start | bytes 442376 | tf_op jit(solution)/shard_map/ppermute | solution.py:538
  75.0 0.7 copy-start.5
  75.0 0.7 copy-start.6
  89.8 1.0 copy-start
  90.8 42.3 %all-to-all-start = ((bf16[16,32,2688]{2,1,0:T(8,128)(2,1)}), bf16[16,32,2688]{2,1,0:T(8,128)(2,1)}, u32[]{:S(2)}, u32[]{:S(2)}) async-start(bf16[16,32,2688]{2,1,0:T(8,128)(2,1)} %bitcast.11), calls=%async_computation | async-start | bytes 5505024 | tf_op jit(solution)/shard_map/all_to_all | solution.py:542

commit v5 on v4

--- a/solution.py
+++ b/solution.py
@@ -30,7 +30,7 @@
 
 
 def params():
-    return pltpu.CompilerParams(vmem_limit_bytes=62 << 20)
+    return pltpu.CompilerParams(vmem_limit_bytes=67_043_328)
 
 
 def dot(a, b):
@@ -314,10 +314,13 @@
     lax.fori_loop(0, N // 2, place_row, 0)
 
 
-def second_kernel(slabs, slab, m2, m1, own, part_h, ra_h, tpt_h, c_in, term_in, c_ref, term_ref, smm_out,
-                  flat, smm, qs, pw, part, ra, tpt, cbuf, tbuf, meta_v, meta_s, ids_v, sem, in_sem, out_sem):
+def second_kernel(slabs, slab, m2_h, m1, own, part_h, ra_h, tpt_h, c_in, term_in, c_ref, term_ref, smm_out,
+                  m2, flat, smm, qs, pw, part, ra, tpt, cbuf, tbuf, meta_v, meta_s, ids_v, sem, in_sem, out_sem):
     del c_in, term_in
+    landed = pltpu.make_async_copy(m2_h, m2, in_sem.at[3])
+    landed.start()
     ins = fetch(((part_h, part), (ra_h.at[:, block(0)], ra), (tpt_h, tpt)), in_sem)
+    landed.wait()
     read_meta([(m2, ROW_META), (m1, TAIL_META), (own, TAIL_META)], meta_v, meta_s, sem)
     write_ids(tbuf, 1, ids_v, meta_v, (2, 2, 1))
     smooth_far(m2, flat, smm, meta_s, 0, inside(slab, -2, slabs))
@@ -342,10 +345,11 @@
         functools.partial(second_kernel, lax.axis_size("slab")),
         out_shape=(shape((W, 7 * W), F32), shape((W, 2 * W + LANES), BF16), shape((W, 2 * W), BF16)),
         grid=(1,),
-        in_specs=[SMEM, VMEM, TAIL, TAIL] + [ANY] * 5,
+        in_specs=[SMEM, ANY, TAIL, TAIL] + [ANY] * 5,
         out_specs=(ANY, ANY, VMEM),
         input_output_aliases={7: 0, 8: 1},
         scratch_shapes=[
+            pltpu.VMEM((ROWS, W), BF16),
             pltpu.VMEM((W, W), BF16),
             pltpu.VMEM((W, WIDE), BF16),
             pltpu.VMEM((W, W), BF16),
@@ -359,7 +363,7 @@
             pltpu.SMEM((3, 16, LANES), I32),
             pltpu.VMEM((CHUNK, LANES), F32),
             pltpu.SemaphoreType.DMA((3,)),
-            pltpu.SemaphoreType.DMA((3,)),
+            pltpu.SemaphoreType.DMA((4,)),
             pltpu.SemaphoreType.DMA((2,)),
         ],
         compiler_params=params(),
@@ -432,12 +436,15 @@
     )(slab, p2, p1, m3, m2, p3, own, sm, smm, smo, ra, tpt, c)
 
 
-def gather_pieces(count, x_ref, lows, highs, ids_v, ids_s, sem):
+def gather_pieces(count, x_h, x_ref, lows, highs, ids_v, ids_s, sem):
+    landed = pltpu.make_async_copy(x_h, x_ref, sem.at[1])
+    landed.start()
+    for y in lows + highs:
+        y[...] = jnp.zeros_like(y)
+    landed.wait()
     for p in range(GROUPS):
         ids_v[p] = x_ref[p, 0:8, count * W:].astype(F32).astype(I32)
     to_scalars([(ids_v, ids_s)], sem)
-    for y in lows + highs:
-        y[...] = jnp.zeros_like(y)
 
     def one(p, carry):
         rows = pl.ds(pl.multiple_of(p * CHUNK, CHUNK), CHUNK)
@@ -466,9 +473,9 @@
         out_ref[:, (first + o) * QUARTER:(first + o + 1) * QUARTER] = total.astype(BF16)
 
 
-def merge_first_kernel(count, x_ref, out_ref, takes, *rest):
-    lows, highs, (ids_v, ids_s, sem) = rest[:count], rest[count:2 * count], rest[2 * count:]
-    gather_pieces(count, x_ref, lows, highs, ids_v, ids_s, sem)
+def merge_first_kernel(count, x_h, out_ref, takes, *rest):
+    lows, highs, (x_ref, ids_v, ids_s, sem) = rest[:count], rest[count:2 * count], rest[2 * count:]
+    gather_pieces(count, x_h, x_ref, lows, highs, ids_v, ids_s, sem)
     groups = jnp.concatenate([ids_v[p, 0:1, :] for p in range(GROUPS)], axis=0).astype(F32).astype(BF16)
     spread = (((iota((LANES, W), 1) >> 2) & 7) == iota((LANES, W), 0)).astype(F32).astype(BF16)
     each = dot(groups, spread)
@@ -481,10 +488,10 @@
     add_pieces(count, 0, takes, lows, highs, out_ref)
 
 
-def merge_last_kernel(count, x_ref, done, takes, out_ref, *rest):
-    lows, highs, (ids_v, ids_s, sem) = rest[:count], rest[count:2 * count], rest[2 * count:]
+def merge_last_kernel(count, x_h, done, takes, out_ref, *rest):
+    lows, highs, (x_ref, ids_v, ids_s, sem) = rest[:count], rest[count:2 * count], rest[2 * count:]
     out_ref[:, 0:done.shape[1]] = done[...]
-    gather_pieces(count, x_ref, lows, highs, ids_v, ids_s, sem)
+    gather_pieces(count, x_h, x_ref, lows, highs, ids_v, ids_s, sem)
     add_pieces(count, done.shape[1] // QUARTER, takes, lows, highs, out_ref)
 
 
@@ -497,39 +504,46 @@
     return pl.pallas_call(
         functools.partial(merge_first_kernel if first else merge_last_kernel, count),
         out_shape=(out, shape((4, 256, W), BF16)) if first else out,
-        in_specs=[VMEM] * (1 if first else 3),
+        in_specs=[ANY] if first else [ANY, VMEM, VMEM],
         out_specs=(VMEM, VMEM) if first else VMEM,
         scratch_shapes=[pltpu.VMEM((GROUPS * CHUNK // 2, GROUPS * TILE), BF16)] * (2 * count)
         + [
+            pltpu.VMEM(x.shape, BF16),
             pltpu.VMEM((GROUPS, 8, LANES), I32),
             pltpu.SMEM((GROUPS, 8, LANES), I32),
-            pltpu.SemaphoreType.DMA((1,)),
+            pltpu.SemaphoreType.DMA((2,)),
         ],
         compiler_params=params(),
         cost_estimate=pl.CostEstimate(flops=1_000_000_000 * count, bytes_accessed=count << 20, transcendentals=0),
     )(*((x,) if first else (x, done, takes)))
 
 
-def finish_kernel(orders, *refs):
-    out_ref = refs[-1]
+def finish_kernel(order, x_ref, out_h, out_ref, sem):
     row, col = iota((TILE, 256), 0), iota((TILE, 256), 1)
     same = ((row >> 2) == (col >> 4)) & ((row & 3) == (col & 3))
     takes = [(same & (((col >> 2) & 3) == cq)).astype(F32).astype(BF16) for cq in range(4)]
-    for order, x_ref in zip(orders, refs):
-        for n, o in enumerate(order):
-            for cq in range(4):
-                at = o * 4 * QUARTER + cq * QUARTER
-                out_ref[0, :, at:at + QUARTER] = dot(takes[cq], x_ref[:, n * QUARTER:(n + 1) * QUARTER])
-
-
-def finish(orders, *parts):
-    return pl.pallas_call(
-        functools.partial(finish_kernel, orders),
-        out_shape=jax.ShapeDtypeStruct((1, TILE, DENSE), F32),
-        in_specs=[VMEM] * len(parts),
-        out_specs=VMEM,
-        compiler_params=params(),
-    )(*parts)
+    copies = []
+    for n, o in enumerate(order):
+        for cq in range(4):
+            at = o * 4 * QUARTER + cq * QUARTER
+            out_ref[0, :, at:at + QUARTER] = dot(takes[cq], x_ref[:, n * QUARTER:(n + 1) * QUARTER])
+        cols = slice(o * 4 * QUARTER, (o + 1) * 4 * QUARTER)
+        copies.append(pltpu.make_async_copy(out_ref.at[:, :, cols], out_h.at[:, :, cols], sem.at[n]))
+        copies[n].start()
+    for copy in copies:
+        copy.wait()
+
+
+def finish(order, x):
+    shape = (1, TILE, DENSE)
+    return pl.pallas_call(
+        functools.partial(finish_kernel, order),
+        out_shape=jax.ShapeDtypeStruct(shape, F32),
+        in_specs=[VMEM],
+        out_specs=ANY,
+        scratch_shapes=[pltpu.VMEM(shape, F32), pltpu.SemaphoreType.DMA((len(order),))],
+        compiler_params=params(),
+    )(x)
 
 
 def along(block, step):
@@ -562,7 +576,7 @@
     c, term = third(slab, p2, p1, m3, m2, p3, own, sm, smm, smo, ra, tpt, c)
     last = exchange(term)
     done, takes = merge(got)
-    level_two = finish(((3, 2, 4, 1, 5, 0, 6),), hand_over(merge(last, done, takes)))
+    level_two = finish((3, 2, 4, 1, 5, 0, 6), hand_over(merge(last, done, takes)))
     return c.reshape(N, TILE, 7 * W), level_two
 
 

time: 169 us -> 168 us (level)
  local copies, waits for them, and re-layouts: 2.65 us -> 0 us
    unnamed x14 -> x0, local copies, waits for them, and re-layouts: 2.65 us -> none
  transfers between devices with their start and end apart: 8 -> 8, of which waited for: 4 -> 4; matrix products, arithmetic and copies ran while one was open for 0% -> 0% of each run, Pallas kernels for 26% -> 27%
where the time goes in v5:
time: 168 us; the launch traced here: 165 us
  waiting for transfers between devices  59.1 us (35%)
  Pallas kernels  59 us (35%)
  starting transfers between devices  25.5 us (15%)
  blocking collectives  20.9 us (12%)
    all_to_all x2, waiting for transfers between devices, exchange(): lax.all_to_all(term.reshape(GROUPS, CHUNK, term.shape[1]), 'piece', 0, 0)  30.5 us
    ppermute x6, waiting for transfers between devices, along(): return lax.ppermute(block, 'slab', route)  28.6 us
    all_to_all x1, blocking collectives, hand_over(): lax.all_to_all(dense.reshape(GROUPS, 16, dense.shape[1]), 'piece', 0, 0)  20.9 us
    pallas_call x2, Pallas kernels, merge(): pl.pallas_call(functools.partial(merge_first_kernel if first else merge_l...  15.5 us
    pallas_call x1, Pallas kernels, third(): pl.pallas_call(functools.partial(third_kernel, lax.axis_size('slab')), ou...  14 us
    all_to_all x2, starting transfers between devices, exchange(): lax.all_to_all(term.reshape(GROUPS, CHUNK, term.shape[1]), 'piece', 0, 0)  12.8 us
    ppermute x6, starting transfers between devices, along(): return lax.ppermute(block, 'slab', route)  12.8 us
    pallas_call x1, Pallas kernels, near(): pl.pallas_call(functools.partial(near_kernel, lax.axis_size('slab')), gri...  10 us
  transfers between devices with their start and end apart: 8, of which 4 were waited for; matrix products, arithmetic and copies ran while one was open for 0% of the time, Pallas kernels for 27%

profile of v5, /device:TPU:2, one launch (start us, length us, event | category | flops | bytes accessed | tf_op | source)
XLA Modules:
  0.0 165.4 jit_solution(13351715458478166248)
XLA Ops:
  0.6 2.2 %shard_map.95.own = bf16[720,512]{1,0:T(8,128)(2,1)} custom-call(bf16[8,64,512]{2,1,0:T(8,128)(2,1)} %a_ref.1, bf16[8,64,64]{2,1,0:T(8,128)(2,1)} %d_ref.1, bf16[8,64,64]{2,1,0:T(8,128)(2,1)} %q_ref.1, bf16[8,64,64]{2,1,0:T(8,128)(2,1)} %t_ref.1, s32[8,8]{1,0:T(8,128)} %cols_ref.1, s32[8,8]{1,0:T(8,128)} %mask_ref.1, s32[1,8]{1,0:T(1,128)} %bitcast.13, ...), custom_call_target="tpu_custom_call" | custom-call | tf_op jit(solution)/shard_map/pallas_call | solution.py:59
  2.8 1.9 %collective-permute-start.2 = (bf16[720,512]{1,0:T(8,128)(2,1)}, bf16[720,512]{1,0:T(8,128)(2,1)}, u32[]{:S(2)}, u32[]{:S(2)}) collective-permute-start(bf16[720,512]{1,0:T(8,128)(2,1)} %shard_map.95.own), channel_id=1, source_target_pairs={{0,16},{16,32},{32,48},{48,64},{64,80},{80,96},{96,112},{112,0},{1... | collective-permute-start | bytes 2211848 | tf_op jit(solution)/shard_map/ppermute | solution.py:552
  4.8 2.2 %collective-permute-start = (bf16[720,512]{1,0:T(8,128)(2,1)}, bf16[720,512]{1,0:T(8,128)(2,1)}, u32[]{:S(2)}, u32[]{:S(2)}) collective-permute-start(bf16[720,512]{1,0:T(8,128)(2,1)} %shard_map.95.own), channel_id=1, source_target_pairs={{0,112},{16,0},{32,16},{48,32},{64,48},{80,64},{96,80},{112,96},{1... | collective-permute-start | bytes 2211848 | tf_op jit(solution)/shard_map/ppermute | solution.py:552
  7.0 7.1 %shard_map.96 = (f32[512,1536]{1,0:T(8,128)}, bf16[512,1536]{1,0:T(8,128)(2,1)}, bf16[512,512]{1,0:T(8,128)(2,1)}, bf16[512,512]{1,0:T(8,128)(2,1)}, bf16[512,512]{1,0:T(8,128)(2,1)}) custom-call(bf16[720,512]{1,0:T(8,128)(2,1)} %shard_map.95.own), custom_call_target="tpu_custom_call" | custom-call | flops 3000000000 | bytes 6291456 | tf_op jit(solution)/shard_map/pallas_call | solution.py:196
  14.1 9.6 %collective-permute-done.2.m1 = bf16[720,512]{1,0:T(8,128)(2,1)} collective-permute-done((bf16[720,512]{1,0:T(8,128)(2,1)}, bf16[720,512]{1,0:T(8,128)(2,1)}, u32[]{:S(2)}, u32[]{:S(2)}) %collective-permute-start.2) | collective-permute-done | bytes 737312 | tf_op jit(solution)/shard_map/ppermute | solution.py:552
  23.7 0.0 collective-permute-start.4
  23.7 0.0 collective-permute-done.p1
  23.7 4.1 %collective-permute-start.1 = (bf16[720,512]{1,0:T(8,128)(2,1)}, bf16[720,512]{1,0:T(8,128)(2,1)}, u32[]{:S(2)}, u32[]{:S(2)}) collective-permute-start(bf16[720,512]{1,0:T(8,128)(2,1)} %collective-permute-done.p1), channel_id=1, source_target_pairs={{0,112},{16,0},{32,16},{48,32},{64,48},{80,64},{96,80},{112,96},{1... | collective-permute-start | bytes 2211848 | tf_op jit(solution)/shard_map/ppermute | solution.py:552
  27.8 10.0 %shard_map.97 = (f32[512,3584]{1,0:T(8,128)}, bf16[512,1152]{1,0:T(8,128)(2,1)}, f32[512,512]{1,0:T(8,128)}, bf16[512,2560]{1,0:T(8,128)(2,1)}, bf16[512,1536]{1...) custom-call(s32[1]{0:T(128)} %bitcast.slab, bf16[720,512]{1,0:T(8,128)(2,1)} %collective-permute-done.2.m1, ...), custom_call_target="tpu_custom_call" | custom-call | flops 8999999488 | bytes 14680064 | tf_op jit(solution)/shard_map/pallas_call | solution.py:266
  37.8 5.8 %collective-permute-done.4.m2_h.m2 = bf16[720,512]{1,0:T(8,128)(2,1)} collective-permute-done((bf16[720,512]{1,0:T(8,128)(2,1)}, bf16[720,512]{1,0:T(8,128)(2,1)}, u32[]{:S(2)}, u32[]{:S(2)}) %collective-permute-start.4) | collective-permute-done | bytes 737312 | tf_op jit(solution)/shard_map/ppermute | solution.py:552
  43.6 7.4 %shard_map.98 = (f32[512,3584]{1,0:T(8,128)}, bf16[512,1152]{1,0:T(8,128)(2,1)}, bf16[512,1024]{1,0:T(8,128)(2,1)}) custom-call(s32[1]{0:T(128)} %bitcast.slab, bf16[720,512]{1,0:T(8,128)(2,1)} %collective-permute-done.4.m2_h.m2, bf16[720,512]{1,0:T(8,128)(2,1)} %collective-permute-done.2.m1, ...), custom_call_target="tpu_custom_call", output_to_operand_aliasing={{0}: (7, {}), {1}: (8, {})} | custom-call | flops 4000000000 | bytes 8388608 | tf_op jit(solution)/shard_map/pallas_call | solution.py:344
  51.0 6.6 %all-to-all-start.1 = ((bf16[16,32,1152]{2,1,0:T(8,128)(2,1)}), bf16[16,32,1152]{2,1,0:T(8,128)(2,1)}, u32[]{:S(2)}, u32[]{:S(2)}) async-start(bf16[16,32,1152]{2,1,0:T(8,128)(2,1)} %bitcast.9), calls=%async_computation.1 | async-start | bytes 2359296 | tf_op jit(solution)/shard_map/all_to_all | solution.py:556
  57.6 0.1 collective-permute-start.3
  57.7 4.4 %collective-permute-start.5 = (bf16[144,512]{1,0:T(8,128)(2,1)}, bf16[144,512]{1,0:T(8,128)(2,1)}, u32[]{:S(2)}, u32[]{:S(2)}) collective-permute-start(bf16[144,512]{1,0:T(8,128)(2,1)} %get-tuple-element.27), channel_id=1, source_target_pairs={{0,96},{16,112},{32,0},{48,16},{64,32},{80,48},{96,64},{112,80},{1... | collective-permute-start | bytes 442376 | tf_op jit(solution)/shard_map/ppermute | solution.py:552
  62.1 13.2 %collective-permute-done.3.m3 = bf16[144,512]{1,0:T(8,128)(2,1)} collective-permute-done((bf16[144,512]{1,0:T(8,128)(2,1)}, bf16[144,512]{1,0:T(8,128)(2,1)}, u32[]{:S(2)}, u32[]{:S(2)}) %collective-permute-start.3) | collective-permute-done | bytes 147488 | tf_op jit(solution)/shard_map/ppermute | solution.py:552
  75.4 0.0 collective-permute-done.5.p3
  75.4 14.0 %shard_map.99 = (f32[512,3584]{1,0:T(8,128)}, bf16[512,2688]{1,0:T(8,128)(2,1)}) custom-call(s32[1]{0:T(128)} %bitcast.slab, bf16[720,512]{1,0:T(8,128)(2,1)} %collective-permute-done.1.p2, bf16[720,512]{1,0:T(8,128)(2,1)} %collective-permute-done.p1, bf16[144,512]{1,0:T(8,128)(2,1)} %collective-permute-done.3.m3, ...), custom_call_target="tpu_custom_call", output_to_operand_aliasing={{0}: (12, {})} | custom-call | flops 7000000000 | bytes 18874368 | tf_op jit(solution)/shard_map/pallas_call | solution.py:409
  89.4 0.0 all-to-all-done.1.x_h
  89.4 6.2 %all-to-all-start = ((bf16[16,32,2688]{2,1,0:T(8,128)(2,1)}), bf16[16,32,2688]{2,1,0:T(8,128)(2,1)}, u32[]{:S(2)}, u32[]{:S(2)}) async-start(bf16[16,32,2688]{2,1,0:T(8,128)(2,1)} %bitcast.11), calls=%async_computation | async-start | bytes 5505024 | tf_op jit(solution)/shard_map/all_to_all | solution.py:556
  95.6 5.8 %shard_map.100 = (bf16[256,512]{1,0:T(8,128)(2,1)}, bf16[4,256,512]{2,1,0:T(8,128)(2,1)}) custom-call(bf16[16,32,1152]{2,1,0:T(8,128)(2,1)} %all-to-all-done.1.x_h), custom_call_target="tpu_custom_call" | custom-call | flops 2000000000 | bytes 2097152 | tf_op jit(solution)/shard_map/pallas_call | solution.py:504
  101.4 30.5 %all-to-all-done.x_h = bf16[16,32,2688]{2,1,0:T(8,128)(2,1)} async-done(((bf16[16,32,2688]{2,1,0:T(8,128)(2,1)}), bf16[16,32,2688]{2,1,0:T(8,128)(2,1)}, u32[]{:S(2)}, u32[]{:S(2)}) %all-to-all-start) | async-done | bytes 2752544 | tf_op jit(solution)/shard_map/all_to_all | solution.py:556
  131.9 9.7 %shard_map.101 = bf16[256,1792]{1,0:T(8,128)(2,1)} custom-call(bf16[16,32,2688]{2,1,0:T(8,128)(2,1)} %all-to-all-done.x_h, bf16[256,512]{1,0:T(8,128)(2,1)} %get-tuple-element.38.done, bf16[4,256,512]{2,1,0:T(8,128)(2,1)} %get-tuple-element.39.takes), custom_call_target="tpu_custom_call" | custom-call | flops 5000000000 | bytes 5242880 | tf_op jit(solution)/shard_map/pallas_call | solution.py:504
  141.7 20.9 %all_to_all.15 = bf16[16,16,1792]{2,1,0:T(8,128)(2,1)} all-to-all(bf16[16,16,1792]{2,1,0:T(8,128)(2,1)} %bitcast.12), channel_id=1, replica_groups=mesh['slab'=8,'piece'=16] {'piece'}, dimensions={0} | all-to-all | bytes 1835008 | tf_op jit(solution)/shard_map/all_to_all | solution.py:560
  162.5 2.7 %shard_map.102 = f32[1,64,7168]{2,1,0:T(8,128)} custom-call(bf16[256,1792]{1,0:T(8,128)(2,1)} %bitcast.10), custom_call_target="tpu_custom_call" | custom-call | tf_op jit(solution)/shard_map/pallas_call | solution.py:539
  (1 shorter events, 0.0 us)
Async XLA Ops:
  2.8 20.8 %collective-permute-start.2 = (bf16[720,512]{1,0:T(8,128)(2,1)}, bf16[720,512]{1,0:T(8,128)(2,1)}, u32[]{:S(2)}, u32[]{:S(2)}) collective-permute-start(bf16[720,512]{1,0:T(8,128)(2,1)} %shard_map.95.own), channel_id=1, source_target_pairs={{0,16},{16,32},{32,48},{48,64},{64,80},{80,96},{96,112},{112,0},{1... | collective-permute-start | bytes 2211848 | tf_op jit(solution)/shard_map/ppermute | solution.py:552
  4.8 18.9 %collective-permute-start = (bf16[720,512]{1,0:T(8,128)(2,1)}, bf16[720,512]{1,0:T(8,128)(2,1)}, u32[]{:S(2)}, u32[]{:S(2)}) collective-permute-start(bf16[720,512]{1,0:T(8,128)(2,1)} %shard_map.95.own), channel_id=1, source_target_pairs={{0,112},{16,0},{32,16},{48,32},{64,48},{80,64},{96,80},{112,96},{1... | collective-permute-start | bytes 2211848 | tf_op jit(solution)/shard_map/ppermute | solution.py:552
  23.7 20.0 %collective-permute-start.4 = (bf16[720,512]{1,0:T(8,128)(2,1)}, bf16[720,512]{1,0:T(8,128)(2,1)}, u32[]{:S(2)}, u32[]{:S(2)}) collective-permute-start(bf16[720,512]{1,0:T(8,128)(2,1)} %collective-permute-done.2.m1), channel_id=1, source_target_pairs={{0,16},{16,32},{32,48},{48,64},{64,80},{80,96},{96,112},{112,0},{1... | collective-permute-start | bytes 2211848 | tf_op jit(solution)/shard_map/ppermute | solution.py:552
  23.7 51.7 %collective-permute-start.1 = (bf16[720,512]{1,0:T(8,128)(2,1)}, bf16[720,512]{1,0:T(8,128)(2,1)}, u32[]{:S(2)}, u32[]{:S(2)}) collective-permute-start(bf16[720,512]{1,0:T(8,128)(2,1)} %collective-permute-done.p1), channel_id=1, source_target_pairs={{0,112},{16,0},{32,16},{48,32},{64,48},{80,64},{96,80},{112,96},{1... | collective-permute-start | bytes 2211848 | tf_op jit(solution)/shard_map/ppermute | solution.py:552
  51.0 38.4 %all-to-all-start.1 = ((bf16[16,32,1152]{2,1,0:T(8,128)(2,1)}), bf16[16,32,1152]{2,1,0:T(8,128)(2,1)}, u32[]{:S(2)}, u32[]{:S(2)}) async-start(bf16[16,32,1152]{2,1,0:T(8,128)(2,1)} %bitcast.9), calls=%async_computation.1 | async-start | bytes 2359296 | tf_op jit(solution)/shard_map/all_to_all | solution.py:556
  57.6 17.7 %collective-permute-start.3 = (bf16[144,512]{1,0:T(8,128)(2,1)}, bf16[144,512]{1,0:T(8,128)(2,1)}, u32[]{:S(2)}, u32[]{:S(2)}) collective-permute-start(bf16[144,512]{1,0:T(8,128)(2,1)} %get-tuple-element.26), channel_id=1, source_target_pairs={{0,32},{16,48},{32,64},{48,80},{64,96},{80,112},{96,0},{112,16},{1... | collective-permute-start | bytes 442376 | tf_op jit(solution)/shard_map/ppermute | solution.py:552
  57.7 17.7 %collective-permute-start.5 = (bf16[144,512]{1,0:T(8,128)(2,1)}, bf16[144,512]{1,0:T(8,128)(2,1)}, u32[]{:S(2)}, u32[]{:S(2)}) collective-permute-start(bf16[144,512]{1,0:T(8,128)(2,1)} %get-tuple-element.27), channel_id=1, source_target_pairs={{0,96},{16,112},{32,0},{48,16},{64,32},{80,48},{96,64},{112,80},{1... | collective-permute-start | bytes 442376 | tf_op jit(solution)/shard_map/ppermute | solution.py:552
  89.4 42.5 %all-to-all-start = ((bf16[16,32,2688]{2,1,0:T(8,128)(2,1)}), bf16[16,32,2688]{2,1,0:T(8,128)(2,1)}, u32[]{:S(2)}, u32[]{:S(2)}) async-start(bf16[16,32,2688]{2,1,0:T(8,128)(2,1)} %bitcast.11), calls=%async_computation | async-start | bytes 5505024 | tf_op jit(solution)/shard_map/all_to_all | solution.py:556

commit v6 on v4

--- a/solution.py
+++ b/solution.py
@@ -30,7 +30,7 @@
 
 
 def params():
-    return pltpu.CompilerParams(vmem_limit_bytes=62 << 20)
+    return pltpu.CompilerParams(vmem_limit_bytes=67_043_328)
 
 
 def dot(a, b):
@@ -367,69 +367,113 @@
     )(slab, m2, m1, own, part, ra, tpt, c, term)
 
 
-def third_kernel(slabs, slab, p2, p1, m3, m2, p3, own, sm_h, smm_h, smo_h, ra_h, tpt_h, c_in, c_ref, term,
-                 flat, smp, qs, pw, cbuf, sm1, smm, smo, ra, tpt, meta_v, meta_s, ids_v, sem, in_sem, out_sem):
+def write_columns(slab, slabs, qs, pw, cbuf, c_ref, out_sem, tpt, meta_s, outs, term, n, value, o, ref, top, at):
+    pw[...] = value.astype(BF16)
+    place_q(qs, ref, top, meta_s, at, inside(slab, o - 3, slabs))
+    cbuf[n] = dot(pw[...], qs[...])
+    outs.append(pltpu.make_async_copy(cbuf.at[n], c_ref.at[:, block(o)], out_sem.at[n]))
+    outs[-1].start()
+    write_term(term, n, tpt, cbuf[n], ref, top + TILE)
+
+
+def third_kernel(slabs, slab, p2, p1, m2, sm_h, smm_h, smo_h, ra_h, tpt_h, c_in, c_ref, term_ref, smp_h,
+                 flat, smp, qs, pw, cbuf, tbuf, sm1, smm, smo, ra, tpt, meta_v, meta_s, sem, in_sem, out_sem):
     del c_in
-    ins = fetch(((sm_h.at[:, block(2)], sm1), (smm_h, smm), (smo_h, smo), (ra_h, ra), (tpt_h, tpt)), in_sem)
-    read_meta([(p2, ROW_META)] + [(ref, TAIL_META) for ref in (p1, m2, m3, p3, own)], meta_v, meta_s, sem)
-    write_ids(term, 5, ids_v, meta_v, (5, 1, 2, 0, 3, 4))
+    ins = fetch(((sm_h.at[:, block(2)], sm1), (smm_h.at[:, block(1)], smm), (smo_h, smo), (ra_h, ra), (tpt_h, tpt)), in_sem)
+    read_meta([(p2, ROW_META), (p1, TAIL_META), (m2, TAIL_META)], meta_v, meta_s, sem)
     smooth_far(p2, flat, smp, meta_s, 0, inside(slab, 2, slabs))
     for copy in ins:
         copy.wait()
-    outs = []
-
-    def columns(n, value, o, ref, top, at):
-        pw[...] = value.astype(BF16)
-        place_q(qs, ref, top, meta_s, at, inside(slab, o - 3, slabs))
-        cbuf[n] = dot(pw[...], qs[...])
-        outs.append(pltpu.make_async_copy(cbuf.at[n], c_ref.at[:, block(o)], out_sem.at[n]))
-        outs[-1].start()
-        write_term(term, n, tpt, cbuf[n], ref, top + TILE)
-
-    first, last = ra[:, block(0)], ra[:, block(4)]
-    near = ra[:, block(3)]
-    value = near.astype(F32) - dot(near, smo[:, block(1)]) - dot(ra[:, block(2)], sm1[...])
+    outs = [pltpu.make_async_copy(smp.at[:, block(2)], smp_h, out_sem.at[3])]
+    outs[0].start()
+    columns = functools.partial(write_columns, slab, slabs, qs, pw, cbuf, c_ref, out_sem, tpt, meta_s, outs, tbuf)
+    first, last, beside = ra[:, block(0)], ra[:, block(4)], ra[:, block(3)]
+    value = beside.astype(F32) - dot(beside, smo[:, block(1)]) - dot(ra[:, block(2)], sm1[...])
     columns(0, value - dot(last, smp[:, block(0)]), 4, p1, TAIL_Q, 1)
-    value = first.astype(F32) - dot(first, smm[:, block(1)]) - dot(ra[:, block(1)], smo[:, block(0)])
+    value = first.astype(F32) - dot(first, smm[...]) - dot(ra[:, block(1)], smo[:, block(0)])
     columns(1, value, 1, m2, TAIL_Q, 2)
-    value = last.astype(F32) - dot(last, smp[:, block(1)]) - dot(near, smo[:, block(2)])
+    value = last.astype(F32) - dot(last, smp[:, block(1)]) - dot(beside, smo[:, block(2)])
     columns(2, value, 5, p2, ROW_Q, 0)
-    columns(3, -dot(first, smm[:, block(0)]), 0, m3, TAIL_Q, 3)
-    columns(4, -dot(last, smp[:, block(2)]), 6, p3, TAIL_Q, 4)
+    outs.append(pltpu.make_async_copy(tbuf, term_ref.at[:, 0:3 * W], out_sem.at[4]))
+    outs[-1].start()
     for out in outs:
         out.wait()
 
 
-def third(slab, p2, p1, m3, m2, p3, own, sm, smm, smo, ra, tpt, c):
+def third(slab, p2, p1, m2, sm, smm, smo, ra, tpt, c):
     shape = jax.ShapeDtypeStruct
     return pl.pallas_call(
         functools.partial(third_kernel, lax.axis_size("slab")),
+        out_shape=(shape((W, 7 * W), F32), shape((W, 5 * W + LANES), BF16), shape((W, W), BF16)),
+        grid=(1,),
+        in_specs=[SMEM, VMEM, TAIL, TAIL] + [ANY] * 6,
+        out_specs=(ANY, ANY, ANY),
+        input_output_aliases={9: 0},
+        scratch_shapes=[
+            pltpu.VMEM((W, W), BF16),
+            pltpu.VMEM((W, WIDE), BF16),
+            pltpu.VMEM((W, W), BF16),
+            pltpu.VMEM((W, W), BF16),
+            pltpu.VMEM((3, W, W), F32),
+            pltpu.VMEM((W, 3 * W), BF16),
+            pltpu.VMEM((W, W), BF16),
+            pltpu.VMEM((W, W), BF16),
+            pltpu.VMEM((W, 3 * W), BF16),
+            pltpu.VMEM((W, 5 * W), BF16),
+            pltpu.VMEM((W, W), BF16),
+            pltpu.VMEM((3, 16, LANES), I32),
+            pltpu.SMEM((3, 16, LANES), I32),
+            pltpu.SemaphoreType.DMA((3,)),
+            pltpu.SemaphoreType.DMA((5,)),
+            pltpu.SemaphoreType.DMA((5,)),
+        ],
+        compiler_params=params(),
+        cost_estimate=pl.CostEstimate(flops=6_000_000_000, bytes_accessed=12 << 20, transcendentals=0),
+    )(slab, p2, p1, m2, sm, smm, smo, ra, tpt, c)
+
+
+def fourth_kernel(slabs, slab, m3, p3, p2, p1, m2, own, smm_h, smp_h, ra_h, tpt_h, c_in, term_in, c_ref, term_ref,
+                  qs, pw, cbuf, tbuf, smm, smp, ra0, ra4, tpt, meta_v, meta_s, ids_v, sem, in_sem, out_sem):
+    del c_in, term_in
+    ins = fetch(((smm_h.at[:, block(0)], smm), (smp_h, smp), (ra_h.at[:, block(0)], ra0),
+                 (ra_h.at[:, block(4)], ra4), (tpt_h, tpt)), in_sem)
+    read_meta([(ref, TAIL_META) for ref in (p2, p1, m2, m3, p3, own)], meta_v, meta_s, sem)
+    write_ids(tbuf, 2, ids_v, meta_v, (5, 1, 2, 0, 3, 4))
+    for copy in ins:
+        copy.wait()
+    outs = []
+    columns = functools.partial(write_columns, slab, slabs, qs, pw, cbuf, c_ref, out_sem, tpt, meta_s, outs, tbuf)
+    columns(0, -dot(ra0[...], smm[...]), 0, m3, TAIL_Q, 3)
+    columns(1, -dot(ra4[...], smp[...]), 6, p3, TAIL_Q, 4)
+    outs.append(pltpu.make_async_copy(tbuf, term_ref.at[:, 3 * W:], out_sem.at[2]))
+    outs[-1].start()
+    for out in outs:
+        out.wait()
+
+
+def fourth(slab, m3, p3, p2, p1, m2, own, smm, smp, ra, tpt, c, term):
+    shape = jax.ShapeDtypeStruct
+    return pl.pallas_call(
+        functools.partial(fourth_kernel, lax.axis_size("slab")),
         out_shape=(shape((W, 7 * W), F32), shape((W, 5 * W + LANES), BF16)),
         grid=(1,),
-        in_specs=[SMEM, VMEM, TAIL, VMEM, TAIL, VMEM, TAIL] + [ANY] * 6,
-        out_specs=(ANY, VMEM),
-        input_output_aliases={12: 0},
-        scratch_shapes=[
-            pltpu.VMEM((W, W), BF16),
-            pltpu.VMEM((W, WIDE), BF16),
-            pltpu.VMEM((W, W), BF16),
-            pltpu.VMEM((W, W), BF16),
-            pltpu.VMEM((5, W, W), F32),
-            pltpu.VMEM((W, W), BF16),
-            pltpu.VMEM((W, 2 * W), BF16),
-            pltpu.VMEM((W, 3 * W), BF16),
-            pltpu.VMEM((W, 5 * W), BF16),
-            pltpu.VMEM((W, W), BF16),
+        in_specs=[SMEM, VMEM, VMEM] + [TAIL] * 4 + [ANY] * 6,
+        out_specs=(ANY, ANY),
+        input_output_aliases={11: 0, 12: 1},
+        scratch_shapes=[pltpu.VMEM((W, W), BF16)] * 2
+        + [pltpu.VMEM((2, W, W), F32), pltpu.VMEM((W, 2 * W + LANES), BF16)]
+        + [pltpu.VMEM((W, W), BF16)] * 5
+        + [
             pltpu.VMEM((6, 16, LANES), I32),
             pltpu.SMEM((6, 16, LANES), I32),
             pltpu.VMEM((CHUNK, LANES), F32),
             pltpu.SemaphoreType.DMA((6,)),
             pltpu.SemaphoreType.DMA((5,)),
-            pltpu.SemaphoreType.DMA((5,)),
+            pltpu.SemaphoreType.DMA((3,)),
         ],
         compiler_params=params(),
-        cost_estimate=pl.CostEstimate(flops=7_000_000_000, bytes_accessed=18 << 20, transcendentals=0),
-    )(slab, p2, p1, m3, m2, p3, own, sm, smm, smo, ra, tpt, c)
+        cost_estimate=pl.CostEstimate(flops=3_000_000_000, bytes_accessed=8 << 20, transcendentals=0),
+    )(slab, m3, p3, p2, p1, m2, own, smm, smp, ra, tpt, c, term)
 
 
 def gather_pieces(count, x_ref, lows, highs, ids_v, ids_s, sem):
@@ -510,26 +554,32 @@
     )(*((x,) if first else (x, done, takes)))
 
 
-def finish_kernel(orders, *refs):
-    out_ref = refs[-1]
+def finish_kernel(order, x_ref, out_h, out_ref, sem):
     row, col = iota((TILE, 256), 0), iota((TILE, 256), 1)
     same = ((row >> 2) == (col >> 4)) & ((row & 3) == (col & 3))
     takes = [(same & (((col >> 2) & 3) == cq)).astype(F32).astype(BF16) for cq in range(4)]
-    for order, x_ref in zip(orders, refs):
-        for n, o in enumerate(order):
-            for cq in range(4):
-                at = o * 4 * QUARTER + cq * QUARTER
-                out_ref[0, :, at:at + QUARTER] = dot(takes[cq], x_ref[:, n * QUARTER:(n + 1) * QUARTER])
-
-
-def finish(orders, *parts):
-    return pl.pallas_call(
-        functools.partial(finish_kernel, orders),
-        out_shape=jax.ShapeDtypeStruct((1, TILE, DENSE), F32),
-        in_specs=[VMEM] * len(parts),
-        out_specs=VMEM,
-        compiler_params=params(),
-    )(*parts)
+    copies = []
+    for n, o in enumerate(order):
+        for cq in range(4):
+            at = o * 4 * QUARTER + cq * QUARTER
+            out_ref[0, :, at:at + QUARTER] = dot(takes[cq], x_ref[:, n * QUARTER:(n + 1) * QUARTER])
+        cols = slice(o * 4 * QUARTER, (o + 1) * 4 * QUARTER)
+        copies.append(pltpu.make_async_copy(out_ref.at[:, :, cols], out_h.at[:, :, cols], sem.at[n]))
+        copies[n].start()
+    for copy in copies:
+        copy.wait()
+
+
+def finish(order, x):
+    shape = (1, TILE, DENSE)
+    return pl.pallas_call(
+        functools.partial(finish_kernel, order),
+        out_shape=jax.ShapeDtypeStruct(shape, F32),
+        in_specs=[VMEM],
+        out_specs=ANY,
+        scratch_shapes=[pltpu.VMEM(shape, F32), pltpu.SemaphoreType.DMA((len(order),))],
+        compiler_params=params(),
+    )(x)
 
 
 def along(block, step):
@@ -559,10 +609,11 @@
     p3 = along(p1_tail, -2)
     c, term, smm = second(slab, m2, m1, own, part, ra, tpt, c, term)
     got = exchange(term)
-    c, term = third(slab, p2, p1, m3, m2, p3, own, sm, smm, smo, ra, tpt, c)
+    c, term, smp = third(slab, p2, p1, m2, sm, smm, smo, ra, tpt, c)
+    c, term = fourth(slab, m3, p3, p2, p1, m2, own, smm, smp, ra, tpt, c, term)
     last = exchange(term)
     done, takes = merge(got)
-    level_two = finish(((3, 2, 4, 1, 5, 0, 6),), hand_over(merge(last, done, takes)))
+    level_two = finish((3, 2, 4, 1, 5, 0, 6), hand_over(merge(last, done, takes)))
     return c.reshape(N, TILE, 7 * W), level_two
 
 

time: 169 us -> 162 us (0.959)
  waiting for transfers between devices: 58.5 us -> 50.7 us
  Pallas kernels: 58.2 us -> 61 us
  local copies, waits for them, and re-layouts: 2.65 us -> 0 us
    ppermute x6, waiting for transfers between devices: 28.1 us -> 20.3 us  [along(): return lax.ppermute(block, 'slab', route)]
    pallas_call x1 -> x2, Pallas kernels: 3.16 us -> 9.62 us  [the longest x1 6.89 us: fourth(): pl.pallas_call(functools.partial(fourth_kernel, lax.axis_size('slab')), o...]
    pallas_call x1, Pallas kernels: 14 us -> 10.5 us  [third(): pl.pallas_call(functools.partial(third_kernel, lax.axis_size('slab')), ou...]
    unnamed x14 -> x0, local copies, waits for them, and re-layouts: 2.65 us -> none
  transfers between devices with their start and end apart: 8 -> 8, of which waited for: 4 -> 5; matrix products, arithmetic and copies ran while one was open for 0% -> 0% of each run, Pallas kernels for 26% -> 29%
where the time goes in v6:
time: 162 us; the launch traced here: 160 us
  Pallas kernels  61 us (38%)
  waiting for transfers between devices  50.7 us (31%)
  starting transfers between devices  26.6 us (16%)
  blocking collectives  20.9 us (13%)
    all_to_all x2, waiting for transfers between devices, exchange(): lax.all_to_all(term.reshape(GROUPS, CHUNK, term.shape[1]), 'piece', 0, 0)  30.4 us
    all_to_all x1, blocking collectives, hand_over(): lax.all_to_all(dense.reshape(GROUPS, 16, dense.shape[1]), 'piece', 0, 0)  20.9 us
    ppermute x6, waiting for transfers between devices, along(): return lax.ppermute(block, 'slab', route)  20.3 us
    pallas_call x2, Pallas kernels, merge(): pl.pallas_call(functools.partial(merge_first_kernel if first else merge_l...  15.1 us
    all_to_all x2, starting transfers between devices, exchange(): lax.all_to_all(term.reshape(GROUPS, CHUNK, term.shape[1]), 'piece', 0, 0)  13.5 us
    ppermute x6, starting transfers between devices, along(): return lax.ppermute(block, 'slab', route)  13.1 us
    pallas_call x1, Pallas kernels, third(): pl.pallas_call(functools.partial(third_kernel, lax.axis_size('slab')), ou...  10.5 us
    pallas_call x1, Pallas kernels, near(): pl.pallas_call(functools.partial(near_kernel, lax.axis_size('slab')), gri...  10 us
  transfers between devices with their start and end apart: 8, of which 5 were waited for; matrix products, arithmetic and copies ran while one was open for 0% of the time, Pallas kernels for 29%

profile of v6, /device:TPU:2, one launch (start us, length us, event | category | flops | bytes accessed | tf_op | source)
XLA Modules:
  0.0 160.0 jit_solution(16593317088935482564)
XLA Ops:
  0.6 2.2 %shard_map.95.own = bf16[720,512]{1,0:T(8,128)(2,1)} custom-call(bf16[8,64,512]{2,1,0:T(8,128)(2,1)} %a_ref.1, bf16[8,64,64]{2,1,0:T(8,128)(2,1)} %d_ref.1, bf16[8,64,64]{2,1,0:T(8,128)(2,1)} %q_ref.1, bf16[8,64,64]{2,1,0:T(8,128)(2,1)} %t_ref.1, s32[8,8]{1,0:T(8,128)} %cols_ref.1, s32[8,8]{1,0:T(8,128)} %mask_ref.1, s32[1,8]{1,0:T(1,128)} %bitcast.13, ...), custom_call_target="tpu_custom_call" | custom-call | tf_op jit(solution)/shard_map/pallas_call | solution.py:59
  2.8 4.0 %collective-permute-start.1 = (bf16[720,512]{1,0:T(8,128)(2,1)}, bf16[720,512]{1,0:T(8,128)(2,1)}, u32[]{:S(2)}, u32[]{:S(2)}) collective-permute-start(bf16[720,512]{1,0:T(8,128)(2,1)} %shard_map.95.own), channel_id=1, source_target_pairs={{0,112},{16,0},{32,16},{48,32},{64,48},{80,64},{96,80},{112,96},{1... | collective-permute-start | bytes 2211848 | tf_op jit(solution)/shard_map/ppermute | solution.py:588
  6.9 7.1 %shard_map.96 = (f32[512,1536]{1,0:T(8,128)}, bf16[512,1536]{1,0:T(8,128)(2,1)}, bf16[512,512]{1,0:T(8,128)(2,1)}, bf16[512,512]{1,0:T(8,128)(2,1)}, bf16[512,512]{1,0:T(8,128)(2,1)}) custom-call(bf16[720,512]{1,0:T(8,128)(2,1)} %shard_map.95.own), custom_call_target="tpu_custom_call" | custom-call | flops 3000000000 | bytes 6291456 | tf_op jit(solution)/shard_map/pallas_call | solution.py:196
  14.0 8.9 %collective-permute-done.1.p1 = bf16[720,512]{1,0:T(8,128)(2,1)} collective-permute-done((bf16[720,512]{1,0:T(8,128)(2,1)}, bf16[720,512]{1,0:T(8,128)(2,1)}, u32[]{:S(2)}, u32[]{:S(2)}) %collective-permute-start.1) | collective-permute-done | bytes 737312 | tf_op jit(solution)/shard_map/ppermute | solution.py:588
  22.9 4.6 %collective-permute-start.4 = (bf16[720,512]{1,0:T(8,128)(2,1)}, bf16[720,512]{1,0:T(8,128)(2,1)}, u32[]{:S(2)}, u32[]{:S(2)}) collective-permute-start(bf16[720,512]{1,0:T(8,128)(2,1)} %collective-permute-done.1.p1), channel_id=1, source_target_pairs={{0,112},{16,0},{32,16},{48,32},{64,48},{80,64},{96,80},{112,96},{1... | collective-permute-start | bytes 2211848 | tf_op jit(solution)/shard_map/ppermute | solution.py:588
  27.5 0.0 collective-permute-done.m1
  27.5 0.0 collective-permute-start.5
  27.5 10.0 %shard_map.97 = (f32[512,3584]{1,0:T(8,128)}, bf16[512,1152]{1,0:T(8,128)(2,1)}, f32[512,512]{1,0:T(8,128)}, bf16[512,2560]{1,0:T(8,128)(2,1)}, bf16[512,1536]{1...) custom-call(s32[1]{0:T(128)} %bitcast.slab, bf16[720,512]{1,0:T(8,128)(2,1)} %collective-permute-done.m1, ...), custom_call_target="tpu_custom_call" | custom-call | flops 8999999488 | bytes 14680064 | tf_op jit(solution)/shard_map/pallas_call | solution.py:266
  37.5 9.5 %collective-permute-done.5.m2 = bf16[720,512]{1,0:T(8,128)(2,1)} collective-permute-done((bf16[720,512]{1,0:T(8,128)(2,1)}, bf16[720,512]{1,0:T(8,128)(2,1)}, u32[]{:S(2)}, u32[]{:S(2)}) %collective-permute-start.5) | collective-permute-done | bytes 737312 | tf_op jit(solution)/shard_map/ppermute | solution.py:588
  47.0 6.4 %shard_map.98 = (f32[512,3584]{1,0:T(8,128)}, bf16[512,1152]{1,0:T(8,128)(2,1)}, bf16[512,1024]{1,0:T(8,128)(2,1)}) custom-call(s32[1]{0:T(128)} %bitcast.slab, bf16[720,512]{1,0:T(8,128)(2,1)} %collective-permute-done.5.m2, bf16[720,512]{1,0:T(8,128)(2,1)} %collective-permute-done.m1, ...), custom_call_target="tpu_custom_call", output_to_operand_aliasing={{0}: (7, {}), {1}: (8, {})} | custom-call | flops 4000000000 | bytes 8388608 | tf_op jit(solution)/shard_map/pallas_call | solution.py:341
  53.5 6.5 %all-to-all-start.1 = ((bf16[16,32,1152]{2,1,0:T(8,128)(2,1)}), bf16[16,32,1152]{2,1,0:T(8,128)(2,1)}, u32[]{:S(2)}, u32[]{:S(2)}) async-start(bf16[16,32,1152]{2,1,0:T(8,128)(2,1)} %bitcast.10), calls=%async_computation.1 | async-start | bytes 2359296 | tf_op jit(solution)/shard_map/all_to_all | solution.py:592
  60.0 0.1 collective-permute-start.2
  60.1 4.4 %collective-permute-start.3 = (bf16[144,512]{1,0:T(8,128)(2,1)}, bf16[144,512]{1,0:T(8,128)(2,1)}, u32[]{:S(2)}, u32[]{:S(2)}) collective-permute-start(bf16[144,512]{1,0:T(8,128)(2,1)} %get-tuple-element.30), channel_id=1, source_target_pairs={{0,96},{16,112},{32,0},{48,16},{64,32},{80,48},{96,64},{112,80},{1... | collective-permute-start | bytes 442376 | tf_op jit(solution)/shard_map/ppermute | solution.py:588
  64.5 0.0 collective-permute-done.4.p2
  64.5 10.5 %shard_map.99 = (f32[512,3584]{1,0:T(8,128)}, bf16[512,2688]{1,0:T(8,128)(2,1)}, bf16[512,512]{1,0:T(8,128)(2,1)}) custom-call(s32[1]{0:T(128)} %bitcast.slab, bf16[720,512]{1,0:T(8,128)(2,1)} %collective-permute-done.4.p2, bf16[720,512]{1,0:T(8,128)(2,1)} %collective-permute-done.1.p1, ...), custom_call_target="tpu_custom_call", output_to_operand_aliasing={{0}: (9, {})} | custom-call | flops 6000000000 | bytes 12582912 | tf_op jit(solution)/shard_map/pallas_call | solution.py:405
  75.0 0.7 collective-permute-done.2.m3
  75.7 1.2 collective-permute-done.3.p3
  76.8 6.9 %shard_map.100 = (f32[512,3584]{1,0:T(8,128)}, bf16[512,2688]{1,0:T(8,128)(2,1)}) custom-call(s32[1]{0:T(128)} %bitcast.slab, bf16[144,512]{1,0:T(8,128)(2,1)} %collective-permute-done.2.m3, bf16[144,512]{1,0:T(8,128)(2,1)} %collective-permute-done.3.p3, bf16[720,512]{1,0:T(8,128)(2,1)} %collective-permute-done.4.p2, ...), custom_call_target="tpu_custom_call", output_to_operand_aliasing={{0}: (11, {}), {1}: (12, {})} | custom-call | flops 3000000000 | bytes 8388608 | tf_op jit(solution)/shard_map/pallas_call | solution.py:456
  83.7 7.0 %all-to-all-start = ((bf16[16,32,2688]{2,1,0:T(8,128)(2,1)}), bf16[16,32,2688]{2,1,0:T(8,128)(2,1)}, u32[]{:S(2)}, u32[]{:S(2)}) async-start(bf16[16,32,2688]{2,1,0:T(8,128)(2,1)} %bitcast.9), calls=%async_computation | async-start | bytes 5505024 | tf_op jit(solution)/shard_map/all_to_all | solution.py:592
  90.8 6.0 %shard_map.101 = (bf16[256,512]{1,0:T(8,128)(2,1)}, bf16[4,256,512]{2,1,0:T(8,128)(2,1)}) custom-call(bf16[16,32,1152]{2,1,0:T(8,128)(2,1)} %all-to-all-done.1.x_ref), custom_call_target="tpu_custom_call" | custom-call | flops 2000000000 | bytes 2097152 | tf_op jit(solution)/shard_map/pallas_call | solution.py:541
  96.8 30.4 %all-to-all-done.x_ref = bf16[16,32,2688]{2,1,0:T(8,128)(2,1)} async-done(((bf16[16,32,2688]{2,1,0:T(8,128)(2,1)}), bf16[16,32,2688]{2,1,0:T(8,128)(2,1)}, u32[]{:S(2)}, u32[]{:S(2)}) %all-to-all-start) | async-done | bytes 2752544 | tf_op jit(solution)/shard_map/all_to_all | solution.py:592
  127.1 9.1 %shard_map.102 = bf16[256,1792]{1,0:T(8,128)(2,1)} custom-call(bf16[16,32,2688]{2,1,0:T(8,128)(2,1)} %all-to-all-done.x_ref, bf16[256,512]{1,0:T(8,128)(2,1)} %get-tuple-element.44.done, bf16[4,256,512]{2,1,0:T(8,128)(2,1)} %get-tuple-element.45.takes), custom_call_target="tpu_custom_call" | custom-call | flops 5000000000 | bytes 5242880 | tf_op jit(solution)/shard_map/pallas_call | solution.py:541
  136.3 20.9 %all_to_all.15 = bf16[16,16,1792]{2,1,0:T(8,128)(2,1)} all-to-all(bf16[16,16,1792]{2,1,0:T(8,128)(2,1)} %bitcast.12), channel_id=1, replica_groups=mesh['slab'=8,'piece'=16] {'piece'}, dimensions={0} | all-to-all | bytes 1835008 | tf_op jit(solution)/shard_map/all_to_all | solution.py:596
  157.2 2.7 %shard_map.103 = f32[1,64,7168]{2,1,0:T(8,128)} custom-call(bf16[256,1792]{1,0:T(8,128)(2,1)} %bitcast.11), custom_call_target="tpu_custom_call" | custom-call | tf_op jit(solution)/shard_map/pallas_call | solution.py:575
  (2 shorter events, 0.0 us)
Async XLA Ops:
  2.8 20.1 %collective-permute-start.1 = (bf16[720,512]{1,0:T(8,128)(2,1)}, bf16[720,512]{1,0:T(8,128)(2,1)}, u32[]{:S(2)}, u32[]{:S(2)}) collective-permute-start(bf16[720,512]{1,0:T(8,128)(2,1)} %shard_map.95.own), channel_id=1, source_target_pairs={{0,112},{16,0},{32,16},{48,32},{64,48},{80,64},{96,80},{112,96},{1... | collective-permute-start | bytes 2211848 | tf_op jit(solution)/shard_map/ppermute | solution.py:588
  6.9 20.7 %collective-permute-start = (bf16[720,512]{1,0:T(8,128)(2,1)}, bf16[720,512]{1,0:T(8,128)(2,1)}, u32[]{:S(2)}, u32[]{:S(2)}) collective-permute-start(bf16[720,512]{1,0:T(8,128)(2,1)} %shard_map.95.own), channel_id=1, source_target_pairs={{0,16},{16,32},{32,48},{48,64},{64,80},{80,96},{96,112},{112,0},{1... | collective-permute-start | bytes 2211848 | tf_op jit(solution)/shard_map/ppermute | solution.py:588
  22.9 41.6 %collective-permute-start.4 = (bf16[720,512]{1,0:T(8,128)(2,1)}, bf16[720,512]{1,0:T(8,128)(2,1)}, u32[]{:S(2)}, u32[]{:S(2)}) collective-permute-start(bf16[720,512]{1,0:T(8,128)(2,1)} %collective-permute-done.1.p1), channel_id=1, source_target_pairs={{0,112},{16,0},{32,16},{48,32},{64,48},{80,64},{96,80},{112,96},{1... | collective-permute-start | bytes 2211848 | tf_op jit(solution)/shard_map/ppermute | solution.py:588
  27.5 19.5 %collective-permute-start.5 = (bf16[720,512]{1,0:T(8,128)(2,1)}, bf16[720,512]{1,0:T(8,128)(2,1)}, u32[]{:S(2)}, u32[]{:S(2)}) collective-permute-start(bf16[720,512]{1,0:T(8,128)(2,1)} %collective-permute-done.m1), channel_id=1, source_target_pairs={{0,16},{16,32},{32,48},{48,64},{64,80},{80,96},{96,112},{112,0},{1... | collective-permute-start | bytes 2211848 | tf_op jit(solution)/shard_map/ppermute | solution.py:588
  53.5 30.3 %all-to-all-start.1 = ((bf16[16,32,1152]{2,1,0:T(8,128)(2,1)}), bf16[16,32,1152]{2,1,0:T(8,128)(2,1)}, u32[]{:S(2)}, u32[]{:S(2)}) async-start(bf16[16,32,1152]{2,1,0:T(8,128)(2,1)} %bitcast.10), calls=%async_computation.1 | async-start | bytes 2359296 | tf_op jit(solution)/shard_map/all_to_all | solution.py:592
  60.0 15.7 %collective-permute-start.2 = (bf16[144,512]{1,0:T(8,128)(2,1)}, bf16[144,512]{1,0:T(8,128)(2,1)}, u32[]{:S(2)}, u32[]{:S(2)}) collective-permute-start(bf16[144,512]{1,0:T(8,128)(2,1)} %get-tuple-element.29), channel_id=1, source_target_pairs={{0,32},{16,48},{32,64},{48,80},{64,96},{80,112},{96,0},{112,16},{1... | collective-permute-start | bytes 442376 | tf_op jit(solution)/shard_map/ppermute | solution.py:588
  60.1 16.8 %collective-permute-start.3 = (bf16[144,512]{1,0:T(8,128)(2,1)}, bf16[144,512]{1,0:T(8,128)(2,1)}, u32[]{:S(2)}, u32[]{:S(2)}) collective-permute-start(bf16[144,512]{1,0:T(8,128)(2,1)} %get-tuple-element.30), channel_id=1, source_target_pairs={{0,96},{16,112},{32,0},{48,16},{64,32},{80,48},{96,64},{112,80},{1... | collective-permute-start | bytes 442376 | tf_op jit(solution)/shard_map/ppermute | solution.py:588
  83.7 43.4 %all-to-all-start = ((bf16[16,32,2688]{2,1,0:T(8,128)(2,1)}), bf16[16,32,2688]{2,1,0:T(8,128)(2,1)}, u32[]{:S(2)}, u32[]{:S(2)}) async-start(bf16[16,32,2688]{2,1,0:T(8,128)(2,1)} %bitcast.9), calls=%async_computation | async-start | bytes 5505024 | tf_op jit(solution)/shard_map/all_to_all | solution.py:592

commit v7 on v4

--- a/solution.py
+++ b/solution.py
@@ -30,7 +30,7 @@
 
 
 def params():
-    return pltpu.CompilerParams(vmem_limit_bytes=62 << 20)
+    return pltpu.CompilerParams(vmem_limit_bytes=67_043_328)
 
 
 def dot(a, b):
@@ -510,26 +510,32 @@
     )(*((x,) if first else (x, done, takes)))
 
 
-def finish_kernel(orders, *refs):
-    out_ref = refs[-1]
+def finish_kernel(order, x_ref, out_h, out_ref, sem):
     row, col = iota((TILE, 256), 0), iota((TILE, 256), 1)
     same = ((row >> 2) == (col >> 4)) & ((row & 3) == (col & 3))
     takes = [(same & (((col >> 2) & 3) == cq)).astype(F32).astype(BF16) for cq in range(4)]
-    for order, x_ref in zip(orders, refs):
-        for n, o in enumerate(order):
-            for cq in range(4):
-                at = o * 4 * QUARTER + cq * QUARTER
-                out_ref[0, :, at:at + QUARTER] = dot(takes[cq], x_ref[:, n * QUARTER:(n + 1) * QUARTER])
-
-
-def finish(orders, *parts):
-    return pl.pallas_call(
-        functools.partial(finish_kernel, orders),
-        out_shape=jax.ShapeDtypeStruct((1, TILE, DENSE), F32),
-        in_specs=[VMEM] * len(parts),
-        out_specs=VMEM,
-        compiler_params=params(),
-    )(*parts)
+    copies = []
+    for n, o in enumerate(order):
+        for cq in range(4):
+            at = o * 4 * QUARTER + cq * QUARTER
+            out_ref[0, :, at:at + QUARTER] = dot(takes[cq], x_ref[:, n * QUARTER:(n + 1) * QUARTER])
+        cols = slice(o * 4 * QUARTER, (o + 1) * 4 * QUARTER)
+        copies.append(pltpu.make_async_copy(out_ref.at[:, :, cols], out_h.at[:, :, cols], sem.at[n]))
+        copies[n].start()
+    for copy in copies:
+        copy.wait()
+
+
+def finish(order, x):
+    shape = (1, TILE, DENSE)
+    return pl.pallas_call(
+        functools.partial(finish_kernel, order),
+        out_shape=jax.ShapeDtypeStruct(shape, F32),
+        in_specs=[VMEM],
+        out_specs=ANY,
+        scratch_shapes=[pltpu.VMEM(shape, F32), pltpu.SemaphoreType.DMA((len(order),))],
+        compiler_params=params(),
+    )(x)
 
 
 def along(block, step):
@@ -562,7 +568,7 @@
     c, term = third(slab, p2, p1, m3, m2, p3, own, sm, smm, smo, ra, tpt, c)
     last = exchange(term)
     done, takes = merge(got)
-    level_two = finish(((3, 2, 4, 1, 5, 0, 6),), hand_over(merge(last, done, takes)))
+    level_two = finish((3, 2, 4, 1, 5, 0, 6), hand_over(merge(last, done, takes)))
     return c.reshape(N, TILE, 7 * W), level_two
 
 

time: 169 us -> 166 us (0.982)
  local copies, waits for them, and re-layouts: 2.65 us -> 0 us
    unnamed x14 -> x0, local copies, waits for them, and re-layouts: 2.65 us -> none
  transfers between devices with their start and end apart: 8 -> 8, of which waited for: 4 -> 4; matrix products, arithmetic and copies ran while one was open for 0% -> 0% of each run, Pallas kernels for 26% -> 27%
where the time goes in v7:
time: 166 us; the launch traced here: 164 us
  waiting for transfers between devices  59 us (36%)
  Pallas kernels  57.7 us (35%)
  starting transfers between devices  25.5 us (15%)
  blocking collectives  20.9 us (13%)
    all_to_all x2, waiting for transfers between devices, exchange(): lax.all_to_all(term.reshape(GROUPS, CHUNK, term.shape[1]), 'piece', 0, 0)  30.4 us
    ppermute x6, waiting for transfers between devices, along(): return lax.ppermute(block, 'slab', route)  28.6 us
    all_to_all x1, blocking collectives, hand_over(): lax.all_to_all(dense.reshape(GROUPS, 16, dense.shape[1]), 'piece', 0, 0)  20.9 us
    pallas_call x2, Pallas kernels, merge(): pl.pallas_call(functools.partial(merge_first_kernel if first else merge_l...  15.1 us
    pallas_call x1, Pallas kernels, third(): pl.pallas_call(functools.partial(third_kernel, lax.axis_size('slab')), ou...  14 us
    ppermute x6, starting transfers between devices, along(): return lax.ppermute(block, 'slab', route)  12.8 us
    all_to_all x2, starting transfers between devices, exchange(): lax.all_to_all(term.reshape(GROUPS, CHUNK, term.shape[1]), 'piece', 0, 0)  12.7 us
    pallas_call x1, Pallas kernels, near(): pl.pallas_call(functools.partial(near_kernel, lax.axis_size('slab')), gri...  10 us
  transfers between devices with their start and end apart: 8, of which 4 were waited for; matrix products, arithmetic and copies ran while one was open for 0% of the time, Pallas kernels for 27%

profile of v7, /device:TPU:2, one launch (start us, length us, event | category | flops | bytes accessed | tf_op | source)
XLA Modules:
  0.0 163.9 jit_solution(7890928673657689493)
XLA Ops:
  0.6 2.2 %shard_map.95.own = bf16[720,512]{1,0:T(8,128)(2,1)} custom-call(bf16[8,64,512]{2,1,0:T(8,128)(2,1)} %a_ref.1, bf16[8,64,64]{2,1,0:T(8,128)(2,1)} %d_ref.1, bf16[8,64,64]{2,1,0:T(8,128)(2,1)} %q_ref.1, bf16[8,64,64]{2,1,0:T(8,128)(2,1)} %t_ref.1, s32[8,8]{1,0:T(8,128)} %cols_ref.1, s32[8,8]{1,0:T(8,128)} %mask_ref.1, s32[1,8]{1,0:T(1,128)} %bitcast.13, ...), custom_call_target="tpu_custom_call" | custom-call | tf_op jit(solution)/shard_map/pallas_call | solution.py:59
  2.8 1.9 %collective-permute-start.2 = (bf16[720,512]{1,0:T(8,128)(2,1)}, bf16[720,512]{1,0:T(8,128)(2,1)}, u32[]{:S(2)}, u32[]{:S(2)}) collective-permute-start(bf16[720,512]{1,0:T(8,128)(2,1)} %shard_map.95.own), channel_id=1, source_target_pairs={{0,16},{16,32},{32,48},{48,64},{64,80},{80,96},{96,112},{112,0},{1... | collective-permute-start | bytes 2211848 | tf_op jit(solution)/shard_map/ppermute | solution.py:544
  4.8 2.2 %collective-permute-start = (bf16[720,512]{1,0:T(8,128)(2,1)}, bf16[720,512]{1,0:T(8,128)(2,1)}, u32[]{:S(2)}, u32[]{:S(2)}) collective-permute-start(bf16[720,512]{1,0:T(8,128)(2,1)} %shard_map.95.own), channel_id=1, source_target_pairs={{0,112},{16,0},{32,16},{48,32},{64,48},{80,64},{96,80},{112,96},{1... | collective-permute-start | bytes 2211848 | tf_op jit(solution)/shard_map/ppermute | solution.py:544
  7.0 7.1 %shard_map.96 = (f32[512,1536]{1,0:T(8,128)}, bf16[512,1536]{1,0:T(8,128)(2,1)}, bf16[512,512]{1,0:T(8,128)(2,1)}, bf16[512,512]{1,0:T(8,128)(2,1)}, bf16[512,512]{1,0:T(8,128)(2,1)}) custom-call(bf16[720,512]{1,0:T(8,128)(2,1)} %shard_map.95.own), custom_call_target="tpu_custom_call" | custom-call | flops 3000000000 | bytes 6291456 | tf_op jit(solution)/shard_map/pallas_call | solution.py:196
  14.1 9.6 %collective-permute-done.2.m1 = bf16[720,512]{1,0:T(8,128)(2,1)} collective-permute-done((bf16[720,512]{1,0:T(8,128)(2,1)}, bf16[720,512]{1,0:T(8,128)(2,1)}, u32[]{:S(2)}, u32[]{:S(2)}) %collective-permute-start.2) | collective-permute-done | bytes 737312 | tf_op jit(solution)/shard_map/ppermute | solution.py:544
  23.7 0.0 collective-permute-start.4
  23.7 0.0 collective-permute-done.p1
  23.7 4.1 %collective-permute-start.1 = (bf16[720,512]{1,0:T(8,128)(2,1)}, bf16[720,512]{1,0:T(8,128)(2,1)}, u32[]{:S(2)}, u32[]{:S(2)}) collective-permute-start(bf16[720,512]{1,0:T(8,128)(2,1)} %collective-permute-done.p1), channel_id=1, source_target_pairs={{0,112},{16,0},{32,16},{48,32},{64,48},{80,64},{96,80},{112,96},{1... | collective-permute-start | bytes 2211848 | tf_op jit(solution)/shard_map/ppermute | solution.py:544
  27.8 10.0 %shard_map.97 = (f32[512,3584]{1,0:T(8,128)}, bf16[512,1152]{1,0:T(8,128)(2,1)}, f32[512,512]{1,0:T(8,128)}, bf16[512,2560]{1,0:T(8,128)(2,1)}, bf16[512,1536]{1...) custom-call(s32[1]{0:T(128)} %bitcast.slab, bf16[720,512]{1,0:T(8,128)(2,1)} %collective-permute-done.2.m1, ...), custom_call_target="tpu_custom_call" | custom-call | flops 8999999488 | bytes 14680064 | tf_op jit(solution)/shard_map/pallas_call | solution.py:266
  37.8 5.8 %collective-permute-done.4.m2 = bf16[720,512]{1,0:T(8,128)(2,1)} collective-permute-done((bf16[720,512]{1,0:T(8,128)(2,1)}, bf16[720,512]{1,0:T(8,128)(2,1)}, u32[]{:S(2)}, u32[]{:S(2)}) %collective-permute-start.4) | collective-permute-done | bytes 737312 | tf_op jit(solution)/shard_map/ppermute | solution.py:544
  43.6 6.5 %shard_map.98 = (f32[512,3584]{1,0:T(8,128)}, bf16[512,1152]{1,0:T(8,128)(2,1)}, bf16[512,1024]{1,0:T(8,128)(2,1)}) custom-call(s32[1]{0:T(128)} %bitcast.slab, bf16[720,512]{1,0:T(8,128)(2,1)} %collective-permute-done.4.m2, bf16[720,512]{1,0:T(8,128)(2,1)} %collective-permute-done.2.m1, ...), custom_call_target="tpu_custom_call", output_to_operand_aliasing={{0}: (7, {}), {1}: (8, {})} | custom-call | flops 4000000000 | bytes 8388608 | tf_op jit(solution)/shard_map/pallas_call | solution.py:341
  50.1 6.6 %all-to-all-start.1 = ((bf16[16,32,1152]{2,1,0:T(8,128)(2,1)}), bf16[16,32,1152]{2,1,0:T(8,128)(2,1)}, u32[]{:S(2)}, u32[]{:S(2)}) async-start(bf16[16,32,1152]{2,1,0:T(8,128)(2,1)} %bitcast.9), calls=%async_computation.1 | async-start | bytes 2359296 | tf_op jit(solution)/shard_map/all_to_all | solution.py:548
  56.7 0.1 collective-permute-start.3
  56.8 4.4 %collective-permute-start.5 = (bf16[144,512]{1,0:T(8,128)(2,1)}, bf16[144,512]{1,0:T(8,128)(2,1)}, u32[]{:S(2)}, u32[]{:S(2)}) collective-permute-start(bf16[144,512]{1,0:T(8,128)(2,1)} %get-tuple-element.27), channel_id=1, source_target_pairs={{0,96},{16,112},{32,0},{48,16},{64,32},{80,48},{96,64},{112,80},{1... | collective-permute-start | bytes 442376 | tf_op jit(solution)/shard_map/ppermute | solution.py:544
  61.2 13.2 %collective-permute-done.3.m3 = bf16[144,512]{1,0:T(8,128)(2,1)} collective-permute-done((bf16[144,512]{1,0:T(8,128)(2,1)}, bf16[144,512]{1,0:T(8,128)(2,1)}, u32[]{:S(2)}, u32[]{:S(2)}) %collective-permute-start.3) | collective-permute-done | bytes 147488 | tf_op jit(solution)/shard_map/ppermute | solution.py:544
  74.5 0.0 collective-permute-done.5.p3
  74.5 0.0 collective-permute-done.1.p2
  74.5 14.0 %shard_map.99 = (f32[512,3584]{1,0:T(8,128)}, bf16[512,2688]{1,0:T(8,128)(2,1)}) custom-call(s32[1]{0:T(128)} %bitcast.slab, bf16[720,512]{1,0:T(8,128)(2,1)} %collective-permute-done.1.p2, bf16[720,512]{1,0:T(8,128)(2,1)} %collective-permute-done.p1, bf16[144,512]{1,0:T(8,128)(2,1)} %collective-permute-done.3.m3, ...), custom_call_target="tpu_custom_call", output_to_operand_aliasing={{0}: (12, {})} | custom-call | flops 7000000000 | bytes 18874368 | tf_op jit(solution)/shard_map/pallas_call | solution.py:405
  88.5 6.1 %all-to-all-start = ((bf16[16,32,2688]{2,1,0:T(8,128)(2,1)}), bf16[16,32,2688]{2,1,0:T(8,128)(2,1)}, u32[]{:S(2)}, u32[]{:S(2)}) async-start(bf16[16,32,2688]{2,1,0:T(8,128)(2,1)} %bitcast.11), calls=%async_computation | async-start | bytes 5505024 | tf_op jit(solution)/shard_map/all_to_all | solution.py:548
  94.7 6.0 %shard_map.100 = (bf16[256,512]{1,0:T(8,128)(2,1)}, bf16[4,256,512]{2,1,0:T(8,128)(2,1)}) custom-call(bf16[16,32,1152]{2,1,0:T(8,128)(2,1)} %all-to-all-done.1.x_ref), custom_call_target="tpu_custom_call" | custom-call | flops 2000000000 | bytes 2097152 | tf_op jit(solution)/shard_map/pallas_call | solution.py:497
  100.7 30.4 %all-to-all-done.x_ref = bf16[16,32,2688]{2,1,0:T(8,128)(2,1)} async-done(((bf16[16,32,2688]{2,1,0:T(8,128)(2,1)}), bf16[16,32,2688]{2,1,0:T(8,128)(2,1)}, u32[]{:S(2)}, u32[]{:S(2)}) %all-to-all-start) | async-done | bytes 2752544 | tf_op jit(solution)/shard_map/all_to_all | solution.py:548
  131.0 9.1 %shard_map.101 = bf16[256,1792]{1,0:T(8,128)(2,1)} custom-call(bf16[16,32,2688]{2,1,0:T(8,128)(2,1)} %all-to-all-done.x_ref, bf16[256,512]{1,0:T(8,128)(2,1)} %get-tuple-element.38.done, bf16[4,256,512]{2,1,0:T(8,128)(2,1)} %get-tuple-element.39.takes), custom_call_target="tpu_custom_call" | custom-call | flops 5000000000 | bytes 5242880 | tf_op jit(solution)/shard_map/pallas_call | solution.py:497
  140.2 20.9 %all_to_all.15 = bf16[16,16,1792]{2,1,0:T(8,128)(2,1)} all-to-all(bf16[16,16,1792]{2,1,0:T(8,128)(2,1)} %bitcast.12), channel_id=1, replica_groups=mesh['slab'=8,'piece'=16] {'piece'}, dimensions={0} | all-to-all | bytes 1835008 | tf_op jit(solution)/shard_map/all_to_all | solution.py:552
  161.1 2.7 %shard_map.102 = f32[1,64,7168]{2,1,0:T(8,128)} custom-call(bf16[256,1792]{1,0:T(8,128)(2,1)} %bitcast.10), custom_call_target="tpu_custom_call" | custom-call | tf_op jit(solution)/shard_map/pallas_call | solution.py:531
  (1 shorter events, 0.0 us)
Async XLA Ops:
  2.8 20.8 %collective-permute-start.2 = (bf16[720,512]{1,0:T(8,128)(2,1)}, bf16[720,512]{1,0:T(8,128)(2,1)}, u32[]{:S(2)}, u32[]{:S(2)}) collective-permute-start(bf16[720,512]{1,0:T(8,128)(2,1)} %shard_map.95.own), channel_id=1, source_target_pairs={{0,16},{16,32},{32,48},{48,64},{64,80},{80,96},{96,112},{112,0},{1... | collective-permute-start | bytes 2211848 | tf_op jit(solution)/shard_map/ppermute | solution.py:544
  4.8 18.9 %collective-permute-start = (bf16[720,512]{1,0:T(8,128)(2,1)}, bf16[720,512]{1,0:T(8,128)(2,1)}, u32[]{:S(2)}, u32[]{:S(2)}) collective-permute-start(bf16[720,512]{1,0:T(8,128)(2,1)} %shard_map.95.own), channel_id=1, source_target_pairs={{0,112},{16,0},{32,16},{48,32},{64,48},{80,64},{96,80},{112,96},{1... | collective-permute-start | bytes 2211848 | tf_op jit(solution)/shard_map/ppermute | solution.py:544
  23.7 20.0 %collective-permute-start.4 = (bf16[720,512]{1,0:T(8,128)(2,1)}, bf16[720,512]{1,0:T(8,128)(2,1)}, u32[]{:S(2)}, u32[]{:S(2)}) collective-permute-start(bf16[720,512]{1,0:T(8,128)(2,1)} %collective-permute-done.2.m1), channel_id=1, source_target_pairs={{0,16},{16,32},{32,48},{48,64},{64,80},{80,96},{96,112},{112,0},{1... | collective-permute-start | bytes 2211848 | tf_op jit(solution)/shard_map/ppermute | solution.py:544
  23.7 50.8 %collective-permute-start.1 = (bf16[720,512]{1,0:T(8,128)(2,1)}, bf16[720,512]{1,0:T(8,128)(2,1)}, u32[]{:S(2)}, u32[]{:S(2)}) collective-permute-start(bf16[720,512]{1,0:T(8,128)(2,1)} %collective-permute-done.p1), channel_id=1, source_target_pairs={{0,112},{16,0},{32,16},{48,32},{64,48},{80,64},{96,80},{112,96},{1... | collective-permute-start | bytes 2211848 | tf_op jit(solution)/shard_map/ppermute | solution.py:544
  50.1 38.4 %all-to-all-start.1 = ((bf16[16,32,1152]{2,1,0:T(8,128)(2,1)}), bf16[16,32,1152]{2,1,0:T(8,128)(2,1)}, u32[]{:S(2)}, u32[]{:S(2)}) async-start(bf16[16,32,1152]{2,1,0:T(8,128)(2,1)} %bitcast.9), calls=%async_computation.1 | async-start | bytes 2359296 | tf_op jit(solution)/shard_map/all_to_all | solution.py:548
  56.7 17.7 %collective-permute-start.3 = (bf16[144,512]{1,0:T(8,128)(2,1)}, bf16[144,512]{1,0:T(8,128)(2,1)}, u32[]{:S(2)}, u32[]{:S(2)}) collective-permute-start(bf16[144,512]{1,0:T(8,128)(2,1)} %get-tuple-element.26), channel_id=1, source_target_pairs={{0,32},{16,48},{32,64},{48,80},{64,96},{80,112},{96,0},{112,16},{1... | collective-permute-start | bytes 442376 | tf_op jit(solution)/shard_map/ppermute | solution.py:544
  56.8 17.7 %collective-permute-start.5 = (bf16[144,512]{1,0:T(8,128)(2,1)}, bf16[144,512]{1,0:T(8,128)(2,1)}, u32[]{:S(2)}, u32[]{:S(2)}) collective-permute-start(bf16[144,512]{1,0:T(8,128)(2,1)} %get-tuple-element.27), channel_id=1, source_target_pairs={{0,96},{16,112},{32,0},{48,16},{64,32},{80,48},{96,64},{112,80},{1... | collective-permute-start | bytes 442376 | tf_op jit(solution)/shard_map/ppermute | solution.py:544
  88.5 42.5 %all-to-all-start = ((bf16[16,32,2688]{2,1,0:T(8,128)(2,1)}), bf16[16,32,2688]{2,1,0:T(8,128)(2,1)}, u32[]{:S(2)}, u32[]{:S(2)}) async-start(bf16[16,32,2688]{2,1,0:T(8,128)(2,1)} %bitcast.11), calls=%async_computation | async-start | bytes 5505024 | tf_op jit(solution)/shard_map/all_to_all | solution.py:548
